TPU v7x, 32 devices: a whole 2x2x4 slice. The times are simulated.
32 devices in a mesh: img: 8 (over z, x), seq: 4 (over y, core).
Axes of the slice: x: 2, y: 2, z: 4, core: 2. Of those that a mesh axis runs over, the one named last changes fastest.
Arguments:
- tokens: bfloat16 [16, 680, 1024], P('img', 'seq'), may hold values from -6 to 6
- cotangent: bfloat16 [16, 680, 1024], P('img', 'seq'), may hold values from -6 to 6
- condition: float32 [16, 1024], P('img'), may hold values from -6 to 6
- scale_sizes: int32 [16, 10], P('img'), may hold values from 1 to 256, 680 in all within a row
- mod_weight: float32 [1024, 6144], P(('img', 'seq')), may hold values from -0.1875 to 0.1875
- mod_bias: float32 [6144], P(('img', 'seq')), may hold values from -1.8 to 1.8
- attn_weight: float32 [1024, 3072], P(('img', 'seq')), may hold values from -0.1875 to 0.1875
- query_bias: float32 [1024], P(('img', 'seq')), may hold values from -3 to 3
- value_bias: float32 [1024], P(('img', 'seq')), may hold values from -3 to 3
- out_weight: float32 [1024, 1024], P(('img', 'seq')), may hold values from -0.75 to 0.75
- out_bias: float32 [1024], P(('img', 'seq')), may hold values from -1.8 to 1.8
- expand_weight: float32 [1024, 4096], P(('img', 'seq')), may hold values from -0.1875 to 0.1875
- expand_bias: float32 [4096], P(('img', 'seq')), may hold values from -3 to 3
- shrink_weight: float32 [4096, 1024], P(('img', 'seq')), may hold values from -0.09375 to 0.09375
- shrink_bias: float32 [1024], P(('img', 'seq')), may hold values from -1.8 to 1.8
- log_scale: float32 [16], replicated, may hold values from 2.1 to 3.1
Outputs:
- layer_out: bfloat16 [16, 680, 1024], P('img', 'seq')
- token_grad: bfloat16 [16, 680, 1024], P('img', 'seq')
- condition_grad: float32 [16, 1024], P('img')
- modweight_grad: float32 [1024, 6144], P(('img', 'seq'))
- modbias_grad: float32 [6144], P(('img', 'seq'))
- attnweight_grad: float32 [1024, 3072], P(('img', 'seq'))
- querybias_grad: float32 [1024], P(('img', 'seq'))
- valuebias_grad: float32 [1024], P(('img', 'seq'))
- outweight_grad: float32 [1024, 1024], P(('img', 'seq'))
- outbias_grad: float32 [1024], P(('img', 'seq'))
- expandw_grad: float32 [1024, 4096], P(('img', 'seq'))
- expandb_grad: float32 [4096], P(('img', 'seq'))
- shrinkw_grad: float32 [4096, 1024], P(('img', 'seq'))
- shrinkb_grad: float32 [1024], P(('img', 'seq'))
- logscale_grad: float32 [16], replicated
Inputs may be any that keep to these rules, and one draw needn't show every extreme that they name: `scale_sizes`: each row holds 10 scale sizes that sum to 680; the largest is 256.
All inputs are finite; a program needn't handle non-finite values.
Results may differ from a plain program's by a relative error of at most 0.025.
Values may be sent and summed in bfloat16 or wider, within the bound.
A program may use at most 256 MiB of HBM per device.

v0:
```python
import jax
import jax.numpy as jnp
from jax import lax
from jax.sharding import PartitionSpec as P

HIGH = lax.Precision.HIGHEST


def normalize(values):
    centered = values - jnp.mean(values, axis=-1, keepdims=True)
    return centered * lax.rsqrt(jnp.mean(centered * centered, axis=-1, keepdims=True) + 1e-06)


def unit_rows(values):
    return values * lax.rsqrt(jnp.sum(values * values, axis=-1, keepdims=True) + 1e-06)


def scaled_query(raw_rows, log_scale):
    return unit_rows(raw_rows) * jnp.exp(log_scale)[:, None]


def gelu_tanh(values):
    return jax.nn.gelu(values, approximate=True)


def scale_ids(sizes, length):
    ends = jnp.cumsum(sizes, axis=-1)
    positions = jnp.arange(length, dtype=jnp.int32)
    return jnp.sum((positions[None, :, None] >= ends[:, None, :]).astype(jnp.int32), axis=-1)


def norm_back(values, grad_rows):
    return jax.vjp(normalize, values)[1](grad_rows)[0]


def masked_scores(query_low, keys_all, visible, heads):
    images, full_len, width = keys_all.shape
    keys_heads = keys_all.reshape(images, full_len, heads, width // heads)
    scores = jnp.einsum(
        "gqhd,gkhd->ghqk", query_low, keys_heads, preferred_element_type=jnp.float32
    )
    return jnp.where(visible, scores, -1e30)


def by_owner(part, img_count, seq_count):
    return part.reshape(
        (img_count, seq_count, part.shape[0] // (img_count * seq_count)) + part.shape[1:]
    )


def owner_rows(part):
    return part.reshape(part.shape[2:])


def body(
    tokens,
    cotangent,
    condition,
    scale_sizes,
    mod_weight,
    mod_bias,
    attn_weight,
    query_bias,
    value_bias,
    out_weight,
    out_bias,
    expand_weight,
    expand_bias,
    shrink_weight,
    shrink_bias,
    log_scale,
):
    images, rows_here, width = tokens.shape
    heads = log_scale.shape[0]
    headdim = width // heads
    seq_count = lax.axis_size("seq")
    img_count = lax.axis_size("img")
    full_len = rows_here * seq_count
    bf16 = jnp.bfloat16
    f32 = jnp.float32
    modw_low = mod_weight.astype(bf16)
    modb_low = mod_bias.astype(bf16)
    attnw_low = attn_weight.astype(bf16)
    qbias_low = query_bias.astype(bf16)
    vbias_low = value_bias.astype(bf16)
    outw_low = out_weight.astype(bf16)
    outb_low = out_bias.astype(bf16)
    expw_low = expand_weight.astype(bf16)
    expb_low = expand_bias.astype(bf16)
    shrw_low = shrink_weight.astype(bf16)
    shrb_low = shrink_bias.astype(bf16)
    (
        modw_full,
        modb_full,
        attnw_full,
        qbias_full,
        vbias_full,
        outw_full,
        outb_full,
        expw_full,
        expb_full,
        shrw_full,
        shrb_full,
    ) = (
        lax.all_gather(modw_low, ("img", "seq"), axis=0, tiled=True),
        lax.all_gather(modb_low, ("img", "seq"), axis=0, tiled=True),
        lax.all_gather(attnw_low, ("img", "seq"), axis=0, tiled=True),
        lax.all_gather(qbias_low, ("img", "seq"), axis=0, tiled=True),
        lax.all_gather(vbias_low, ("img", "seq"), axis=0, tiled=True),
        lax.all_gather(outw_low, ("img", "seq"), axis=0, tiled=True),
        lax.all_gather(outb_low, ("img", "seq"), axis=0, tiled=True),
        lax.all_gather(expw_low, ("img", "seq"), axis=0, tiled=True),
        lax.all_gather(expb_low, ("img", "seq"), axis=0, tiled=True),
        lax.all_gather(shrw_low, ("img", "seq"), axis=0, tiled=True),
        lax.all_gather(shrb_low, ("img", "seq"), axis=0, tiled=True),
    )
    silu_cond = jax.nn.silu(condition).astype(bf16)
    modulation = jnp.dot(silu_cond, modw_full, preferred_element_type=f32) + modb_full.astype(f32)
    gain_attn, gain_mlp, scale_attn, scale_mlp, shift_attn, shift_mlp = jnp.split(
        modulation[:, None, :], 6, axis=-1
    )
    resid_in = tokens.astype(f32)
    normed_in = normalize(resid_in)
    attn_input = (normed_in * (1.0 + scale_attn) + shift_attn).astype(bf16)
    packed = jnp.einsum("gtd,de->gte", attn_input, attnw_full, preferred_element_type=f32)
    query_raw = (packed[..., :width] + qbias_full.astype(f32)).reshape(
        images, rows_here, heads, headdim
    )
    key_raw = packed[..., width : 2 * width].reshape(images, rows_here, heads, headdim)
    value_raw = packed[..., 2 * width :] + vbias_full.astype(f32)
    query_low = scaled_query(query_raw, log_scale).astype(bf16)
    key_low = unit_rows(key_raw).astype(bf16).reshape(images, rows_here, width)
    value_low = value_raw.astype(bf16)
    keys_all, values_all = (
        lax.all_gather(key_low, "seq", axis=1, tiled=True),
        lax.all_gather(value_low, "seq", axis=1, tiled=True),
    )
    ids_all = scale_ids(scale_sizes, full_len)
    first_row = lax.axis_index("seq") * rows_here
    ids_query = lax.dynamic_slice_in_dim(ids_all, first_row, rows_here, 1)
    visible = (ids_all[:, None, :] <= ids_query[:, :, None])[:, None]
    masked = masked_scores(query_low, keys_all, visible, heads)
    top = jnp.max(masked, axis=-1, keepdims=True)
    expo = jnp.exp(masked - top)
    total = jnp.sum(expo, axis=-1, keepdims=True)
    log_total = top + jnp.log(total)
    probs_low = (expo / total).astype(bf16)
    context = jnp.einsum(
        "ghqk,gkhd->gqhd",
        probs_low,
        values_all.reshape(images, full_len, heads, headdim),
        preferred_element_type=f32,
    )
    context_low = context.reshape(images, rows_here, width).astype(bf16)
    attn_out = jnp.einsum(
        "gtd,de->gte", context_low, outw_full, preferred_element_type=f32
    ) + outb_full.astype(f32)
    resid_mid = resid_in + gain_attn * attn_out
    normed_mid = normalize(resid_mid)
    mlp_input = (normed_mid * (1.0 + scale_mlp) + shift_mlp).astype(bf16)
    expanded = jnp.einsum(
        "gtd,df->gtf", mlp_input, expw_full, preferred_element_type=f32
    ) + expb_full.astype(f32)
    activated_low = gelu_tanh(expanded).astype(bf16)
    shrunk = jnp.einsum(
        "gtf,fd->gtd", activated_low, shrw_full, preferred_element_type=f32
    ) + shrb_full.astype(f32)
    layer_out = (resid_mid + gain_mlp * shrunk).astype(bf16)
    modw_back, attnw_back, outw_back, expw_back, shrw_back = (
        lax.all_gather(modw_low, ("img", "seq"), axis=0, tiled=True),
        lax.all_gather(attnw_low, ("img", "seq"), axis=0, tiled=True),
        lax.all_gather(outw_low, ("img", "seq"), axis=0, tiled=True),
        lax.all_gather(expw_low, ("img", "seq"), axis=0, tiled=True),
        lax.all_gather(shrw_low, ("img", "seq"), axis=0, tiled=True),
    )
    keys_back, values_back = (
        lax.all_gather(key_low, "seq", axis=1, tiled=True),
        lax.all_gather(value_low, "seq", axis=1, tiled=True),
    )
    grad_out = cotangent.astype(f32)
    grad_gain_mlp = jnp.sum(grad_out * shrunk, axis=1)
    grad_shrunk = (grad_out * gain_mlp).astype(bf16)
    shrw_part = jnp.einsum("gtf,gtd->fd", activated_low, grad_shrunk, preferred_element_type=f32)
    shrb_part = jnp.sum(grad_shrunk.astype(f32), axis=(0, 1))
    grad_activated = jnp.einsum("gtd,fd->gtf", grad_shrunk, shrw_back, preferred_element_type=f32)
    grad_expanded = jax.vjp(gelu_tanh, expanded)[1](grad_activated)[0].astype(bf16)
    expw_part = jnp.einsum("gtd,gtf->df", mlp_input, grad_expanded, preferred_element_type=f32)
    expb_part = jnp.sum(grad_expanded.astype(f32), axis=(0, 1))
    grad_mlp_input = jnp.einsum("gtf,df->gtd", grad_expanded, expw_back, preferred_element_type=f32)
    grad_scale_mlp = jnp.sum(grad_mlp_input * normed_mid, axis=1)
    grad_shift_mlp = jnp.sum(grad_mlp_input, axis=1)
    grad_mid = grad_out + norm_back(resid_mid, grad_mlp_input * (1.0 + scale_mlp))
    grad_gain_attn = jnp.sum(grad_mid * attn_out, axis=1)
    grad_attn_out = (grad_mid * gain_attn).astype(bf16)
    outw_part = jnp.einsum("gtd,gte->de", context_low, grad_attn_out, preferred_element_type=f32)
    outb_part = jnp.sum(grad_attn_out.astype(f32), axis=(0, 1))
    grad_context = jnp.einsum("gte,de->gtd", grad_attn_out, outw_back, preferred_element_type=f32)
    grad_context_low = grad_context.astype(bf16).reshape(images, rows_here, heads, headdim)
    masked_again = masked_scores(query_low, keys_back, visible, heads)
    probs = jnp.exp(masked_again - log_total)
    probs_again = probs.astype(bf16)
    values_heads = values_back.reshape(images, full_len, heads, headdim)
    keys_heads = keys_back.reshape(images, full_len, heads, headdim)
    grad_probs = jnp.einsum(
        "gqhd,gkhd->ghqk", grad_context_low, values_heads, preferred_element_type=f32
    )
    delta = jnp.sum(probs * grad_probs, axis=-1, keepdims=True)
    grad_scores = (probs * (grad_probs - delta)).astype(bf16)
    grad_query = jnp.einsum(
        "ghqk,gkhd->gqhd", grad_scores, keys_heads, preferred_element_type=f32
    ).astype(bf16)
    grad_keys_part = jnp.einsum(
        "ghqk,gqhd->gkhd", grad_scores, query_low, preferred_element_type=f32
    )
    grad_values_part = jnp.einsum(
        "ghqk,gqhd->gkhd", probs_again, grad_context_low, preferred_element_type=f32
    )
    grad_keys, grad_values = (
        lax.psum_scatter(
            grad_keys_part.reshape(images, full_len, width).astype(jnp.bfloat16),
            "seq",
            scatter_dimension=1,
            tiled=True,
        ).astype(jnp.float32),
        lax.psum_scatter(
            grad_values_part.reshape(images, full_len, width).astype(jnp.bfloat16),
            "seq",
            scatter_dimension=1,
            tiled=True,
        ).astype(jnp.float32),
    )
    grad_keys_low = grad_keys.astype(bf16).astype(f32).reshape(images, rows_here, heads, headdim)
    grad_values_f = grad_values.astype(bf16).astype(f32)
    grad_query_raw, grad_logs = jax.vjp(scaled_query, query_raw, log_scale)[1](
        grad_query.astype(f32)
    )
    grad_key_raw = jax.vjp(unit_rows, key_raw)[1](grad_keys_low)[0]
    grad_query_flat = grad_query_raw.reshape(images, rows_here, width)
    qbias_part = jnp.sum(grad_query_flat, axis=(0, 1))
    vbias_part = jnp.sum(grad_values_f, axis=(0, 1))
    grad_packed = jnp.concatenate(
        [grad_query_flat, grad_key_raw.reshape(images, rows_here, width), grad_values_f], axis=-1
    ).astype(bf16)
    attnw_part = jnp.einsum("gtd,gte->de", attn_input, grad_packed, preferred_element_type=f32)
    grad_attn_input = jnp.einsum("gte,de->gtd", grad_packed, attnw_back, preferred_element_type=f32)
    grad_scale_attn = jnp.sum(grad_attn_input * normed_in, axis=1)
    grad_shift_attn = jnp.sum(grad_attn_input, axis=1)
    token_grad = (grad_mid + norm_back(resid_in, grad_attn_input * (1.0 + scale_attn))).astype(bf16)
    grad_mod = jnp.concatenate(
        [
            grad_gain_attn,
            grad_gain_mlp,
            grad_scale_attn,
            grad_scale_mlp,
            grad_shift_attn,
            grad_shift_mlp,
        ],
        axis=-1,
    )
    logs_total = lax.psum(grad_logs, ("img", "seq"))
    group_sums = (
        lax.psum_scatter(
            by_owner(attnw_part, img_count, seq_count).astype(jnp.bfloat16),
            "seq",
            scatter_dimension=1,
            tiled=True,
        ).astype(jnp.float32),
        lax.psum_scatter(
            by_owner(qbias_part, img_count, seq_count).astype(jnp.bfloat16),
            "seq",
            scatter_dimension=1,
            tiled=True,
        ).astype(jnp.float32),
        lax.psum_scatter(
            by_owner(vbias_part, img_count, seq_count).astype(jnp.bfloat16),
            "seq",
            scatter_dimension=1,
            tiled=True,
        ).astype(jnp.float32),
        lax.psum_scatter(
            by_owner(outw_part, img_count, seq_count).astype(jnp.bfloat16),
            "seq",
            scatter_dimension=1,
            tiled=True,
        ).astype(jnp.float32),
        lax.psum_scatter(
            by_owner(outb_part, img_count, seq_count).astype(jnp.bfloat16),
            "seq",
            scatter_dimension=1,
            tiled=True,
        ).astype(jnp.float32),
        lax.psum_scatter(
            by_owner(expw_part, img_count, seq_count).astype(jnp.bfloat16),
            "seq",
            scatter_dimension=1,
            tiled=True,
        ).astype(jnp.float32),
        lax.psum_scatter(
            by_owner(expb_part, img_count, seq_count).astype(jnp.bfloat16),
            "seq",
            scatter_dimension=1,
            tiled=True,
        ).astype(jnp.float32),
        lax.psum_scatter(
            by_owner(shrw_part, img_count, seq_count).astype(jnp.bfloat16),
            "seq",
            scatter_dimension=1,
            tiled=True,
        ).astype(jnp.float32),
        lax.psum_scatter(
            by_owner(shrb_part, img_count, seq_count).astype(jnp.bfloat16),
            "seq",
            scatter_dimension=1,
            tiled=True,
        ).astype(jnp.float32),
    )
    owned_blocks = (
        lax.psum_scatter(
            group_sums[0].astype(jnp.bfloat16), "img", scatter_dimension=0, tiled=True
        ).astype(jnp.float32),
        lax.psum_scatter(
            group_sums[1].astype(jnp.bfloat16), "img", scatter_dimension=0, tiled=True
        ).astype(jnp.float32),
        lax.psum_scatter(
            group_sums[2].astype(jnp.bfloat16), "img", scatter_dimension=0, tiled=True
        ).astype(jnp.float32),
        lax.psum_scatter(
            group_sums[3].astype(jnp.bfloat16), "img", scatter_dimension=0, tiled=True
        ).astype(jnp.float32),
        lax.psum_scatter(
            group_sums[4].astype(jnp.bfloat16), "img", scatter_dimension=0, tiled=True
        ).astype(jnp.float32),
        lax.psum_scatter(
            group_sums[5].astype(jnp.bfloat16), "img", scatter_dimension=0, tiled=True
        ).astype(jnp.float32),
        lax.psum_scatter(
            group_sums[6].astype(jnp.bfloat16), "img", scatter_dimension=0, tiled=True
        ).astype(jnp.float32),
        lax.psum_scatter(
            group_sums[7].astype(jnp.bfloat16), "img", scatter_dimension=0, tiled=True
        ).astype(jnp.float32),
        lax.psum_scatter(
            group_sums[8].astype(jnp.bfloat16), "img", scatter_dimension=0, tiled=True
        ).astype(jnp.float32),
    )
    owned = [owner_rows(block) for block in owned_blocks]
    modw_part = jnp.dot(silu_cond.astype(f32).T, grad_mod, precision=HIGH)
    modb_part = jnp.sum(grad_mod, axis=0)
    modw_group, modb_group = (
        lax.psum_scatter(
            by_owner(modw_part, img_count, seq_count).astype(jnp.bfloat16),
            "seq",
            scatter_dimension=1,
            tiled=True,
        ).astype(jnp.float32),
        lax.psum_scatter(
            by_owner(modb_part, img_count, seq_count).astype(jnp.bfloat16),
            "seq",
            scatter_dimension=1,
            tiled=True,
        ).astype(jnp.float32),
    )
    modw_block, modb_block = (
        lax.psum_scatter(
            modw_group.astype(jnp.bfloat16), "img", scatter_dimension=0, tiled=True
        ).astype(jnp.float32),
        lax.psum_scatter(
            modb_group.astype(jnp.bfloat16), "img", scatter_dimension=0, tiled=True
        ).astype(jnp.float32),
    )
    modw_own = owner_rows(modw_block)
    modb_own = owner_rows(modb_block)
    grad_silu = jnp.dot(grad_mod, modw_back.astype(f32).T, precision=HIGH)
    cond_part = jax.vjp(jax.nn.silu, condition)[1](grad_silu)[0]
    cond_total = lax.psum(cond_part, "seq")
    return (
        layer_out,
        token_grad,
        cond_total,
        modw_own,
        modb_own,
        owned[0],
        owned[1],
        owned[2],
        owned[3],
        owned[4],
        owned[5],
        owned[6],
        owned[7],
        owned[8],
        logs_total,
    )


def solution(mesh):
    return jax.shard_map(
        body,
        mesh=mesh,
        in_specs=(
            P("img", "seq", None),
            P("img", "seq", None),
            P("img", None),
            P("img", None),
            P(("img", "seq"), None),
            P(("img", "seq")),
            P(("img", "seq"), None),
            P(("img", "seq")),
            P(("img", "seq")),
            P(("img", "seq"), None),
            P(("img", "seq")),
            P(("img", "seq"), None),
            P(("img", "seq")),
            P(("img", "seq"), None),
            P(("img", "seq")),
            P(),
        ),
        out_specs=(
            P("img", "seq", None),
            P("img", "seq", None),
            P("img", None),
            P(("img", "seq"), None),
            P(("img", "seq")),
            P(("img", "seq"), None),
            P(("img", "seq")),
            P(("img", "seq")),
            P(("img", "seq"), None),
            P(("img", "seq")),
            P(("img", "seq"), None),
            P(("img", "seq")),
            P(("img", "seq"), None),
            P(("img", "seq")),
            P(),
        ),
        check_vma=False,
    )
```

profile of v0, /device:TPU:1, one launch (start us, length us, event | category | flops | bytes accessed | tf_op | source)
XLA Modules:
  0.0 1716.7 jit_solution(11322168727319704416)
XLA Ops:
  12.3 43.6 %all-reduce.23 = (bf16[6144]{0:T(1024)(128)(2,1)S(1)}, bf16[1024]{0:T(1024)(128)(2,1)S(1)}, bf16[1024]{0:T(1024)(128)(2,1)S(1)}, bf16[1024]{0:T(1024)(128)(2,1)}, bf16[1024]{0:T(1024)(128)(2,1)}) all-reduce(bf16[6144]{0:T(1024)(128)(2,1)S(1)} %dynamic-update-slice, ...), channel_id=1, replica_groups=mesh['img'=8,'seq'=4] {'img','seq'}, use_global_device_ids=true, to_apply=%add | all-reduce | flops 10240 | bytes 40960
  57.2 53.0 %all-gather.9.cloned.1.call-done = bf16[1024,6144]{1,0:T(8,128)(2,1)} async-done(((bf16[32,6144]{1,0:T(8,128)(2,1)}), bf16[1024,6144]{1,0:T(8,128)(2,1)}) %all-gather.9.cloned.1.call-update) | async-done | bytes 12582928 | tf_op jit(solution)/shard_map/all_gather | solution.py:105
  117.2 64.4 %all-gather.11.cloned.1.call-done = bf16[1024,3072]{1,0:T(8,128)(2,1)} async-done(((bf16[32,3072]{1,0:T(8,128)(2,1)}), bf16[1024,3072]{1,0:T(8,128)(2,1)}) %all-gather.11.cloned.1.call-update) | async-done | bytes 6291472 | tf_op jit(solution)/shard_map/all_gather | solution.py:107
  202.3 39.4 %all-gather = bf16[32,1,128]{2,1,0:T(2,128)(2,1)S(1)} all-gather(bf16[1,1,128]{2,1,0:T(2,128)(2,1)S(1)} %convert_bitcast_fusion), channel_id=1, replica_groups=mesh['img'=8,'seq'=4] {'img','seq'}, dimensions={0}, use_global_device_ids=true | all-gather | bytes 8448 | tf_op jit(solution)/shard_map/all_gather | solution.py:113
  246.8 8.8 copy.138
  255.6 8.6 copy.132
  276.7 7.2 fusion.50
  284.0 27.0 %all-gather.17.cloned.1.call-done = bf16[1024,1024]{1,0:T(8,128)(2,1)} async-done(((bf16[32,1024]{1,0:T(8,128)(2,1)}), bf16[1024,1024]{1,0:T(8,128)(2,1)}) %all-gather.17.cloned.1.call-update) | async-done | bytes 2097168 | tf_op jit(solution)/shard_map/all_gather | solution.py:110
  315.7 74.6 %all-gather.19.cloned.1.call-done = bf16[1024,4096]{1,0:T(8,128)(2,1)} async-done(((bf16[32,4096]{1,0:T(8,128)(2,1)}), bf16[1024,4096]{1,0:T(8,128)(2,1)}) %all-gather.19.cloned.1.call-update) | async-done | bytes 8388624 | tf_op jit(solution)/shard_map/all_gather | solution.py:112
  390.3 8.6 fusion.28
  398.9 70.6 %all-gather.21.cloned.1.call-done = bf16[4096,1024]{1,0:T(8,128)(2,1)} async-done(((bf16[128,1024]{1,0:T(8,128)(2,1)}), bf16[4096,1024]{1,0:T(8,128)(2,1)}) %all-gather.21.cloned.1.call-update) | async-done | bytes 8388624 | tf_op jit(solution)/shard_map/all_gather | solution.py:114
  469.5 10.6 fusion.109
  488.6 13.6 multiply_reduce_fusion
  502.3 12.9 multiply_convert_fusion
  525.1 9.3 fusion.33
  534.4 8.7 copy.142
  543.1 8.7 copy.147
  564.7 7.1 bitcast_convert_fusion.1
  571.8 7.9 bitcast_convert_fusion
  579.7 78.0 %all-reduce.33.cloned.1.call-done = (bf16[2,680,1024]{2,0,1:T(2,128)(2,1)}, bf16[2,680,1024]{2,0,1:T(2,128)(2,1)}) async-done(((bf16[2,680,1024]{2,0,1:T(2,128)(2,1)}, bf16[2,680,1024]{2,0,1:T(2,128)(2,1)}), (bf16[2,680,1024]{2,0,1:T(2,128)(2,1)}, bf16[2,680,1024]{2,0,1:T(2,128)(2,1)})) %all-reduce.33.cloned.1.call-update) | async-done | bytes 5570576
  675.7 6.4 bitcast_convert_fusion.2
  686.4 6.8 fusion.60
  693.3 12.7 convolution_convert_fusion
  706.9 626.3 %all-reduce.31.cloned.1.call-done = (bf16[8,4,32,6144]{3,2,1,0:T(8,128)(2,1)}, bf16[8,4,32,3072]{3,2,1,0:T(8,128)(2,1)}, bf16[8,4,32,1024]{3,2,1,0:T(8,128)(2,1)...) async-done(((bf16[8,4,32,6144]{3,2,1,0:T(8,128)(2,1)}, bf16[8,4,32,3072]{3,2,1,0:T(8,128)(2,1)}, bf16[8,4,32,1024]{3,2,1,0:T(8,128)(2,1)}, ...) | async-done | bytes 37748752
  1352.9 39.5 %psum.15 = f32[16]{0:T(128)} all-reduce(f32[16]{0:T(128)S(1)} %exponential_multiply_fusion), channel_id=1, replica_groups=mesh['img'=8,'seq'=4] {'img','seq'}, use_global_device_ids=true, to_apply=%region_55.56 | all-reduce | flops 16 | bytes 128 | tf_op jit(solution)/shard_map/psum | solution.py:260
  1392.8 11.6 all-reduce.25
  1410.9 12.7 fusion.83
  1430.5 28.9 %all-reduce.24 = (bf16[8,1,192]{2,1,0:T(2,128)(2,1)S(1)}, bf16[8,1,32]{2,1,0:T(2,128)(2,1)S(1)}, bf16[8,1,32]{2,1,0:T(2,128)(2,1)S(1)}, bf16[8,1,32]{2,1,0:T(2,1...) all-reduce(bf16[8,1,192]{2,1,0:T(2,128)(2,1)S(1)} %copy.151, ...), channel_id=7, replica_groups=mesh['img'=8,'seq'=4] {'img'}, use_global_device_ids=true, to_apply=%region_30.31.clone | all-reduce | flops 3584 | bytes 14336
  1467.9 20.0 %reduce-scatter.26.cloned.1.call-done = bf16[1,1,32,3072]{3,2,1,0:T(8,128)(2,1)} async-done(((bf16[8,1,32,3072]{3,2,1,0:T(8,128)(2,1)}), bf16[1,1,32,3072]{3,2,1,0:T(8,128)(2,1)}) %reduce-scatter.26.cloned.1.call-update) | async-done | bytes 196624 | tf_op jit(solution)/shard_map/reduce_scatter | solution.py:318
  1489.7 69.7 %reduce-scatter.32.cloned.1.call-done = bf16[1,1,128,1024]{3,2,1,0:T(8,128)(2,1)} async-done(((bf16[8,1,128,1024]{3,2,1,0:T(8,128)(2,1)}), bf16[1,1,128,1024]{3,2,1,0:T(8,128)(2,1)}) %reduce-scatter.32.cloned.1.call-update) | async-done | bytes 262160 | tf_op jit(solution)/shard_map/reduce_scatter | solution.py:339
  1561.1 69.0 %reduce-scatter.30.cloned.1.call-done = bf16[1,1,32,4096]{3,2,1,0:T(8,128)(2,1)} async-done(((bf16[8,1,32,4096]{3,2,1,0:T(8,128)(2,1)}), bf16[1,1,32,4096]{3,2,1,0:T(8,128)(2,1)}) %reduce-scatter.30.cloned.1.call-update) | async-done | bytes 262160 | tf_op jit(solution)/shard_map/reduce_scatter | solution.py:333
  1631.9 75.9 %reduce-scatter.22.cloned.1.call-done = bf16[1,1,32,6144]{3,2,1,0:T(8,128)(2,1)} async-done(((bf16[8,1,32,6144]{3,2,1,0:T(8,128)(2,1)}), bf16[1,1,32,6144]{3,2,1,0:T(8,128)(2,1)}) %reduce-scatter.22.cloned.1.call-update) | async-done | bytes 393232 | tf_op jit(solution)/shard_map/reduce_scatter | solution.py:364
  (363 shorter events, 158.1 us)
Async XLA Ops:
  7.2 48.7 %copy-start.6 = (bf16[2,170,1024]{2,0,1:T(2,128)(2,1)S(1)}, bf16[2,170,1024]{2,0,1:T(2,128)(2,1)}, u32[]{:S(2)}) copy-start(bf16[2,170,1024]{2,0,1:T(2,128)(2,1)} %param.16) | copy-start | bytes 2088964
  7.2 103.0 %copy-start.37 = (f32[2,1024]{1,0:T(2,128)S(1)}, f32[2,1024]{1,0:T(2,128)}, u32[]{:S(2)}) copy-start(f32[2,1024]{1,0:T(2,128)} %param.18) | copy-start | bytes 24580
  7.3 103.0 %all-gather.9.cloned.1.call-start = ((), (), s32[]{:S(2)}) async-start(), calls=%async_computation.6 | async-start | bytes 12976128 | tf_op jit(solution)/shard_map/all_gather | solution.py:105
  9.3 172.3 %all-gather.11.cloned.1.call-start = ((), (), s32[]{:S(2)}) async-start(), calls=%async_computation.7 | async-start | bytes 6488064 | tf_op jit(solution)/shard_map/all_gather | solution.py:107
  11.1 235.7 %all-gather.15.cloned.1.call-start = ((), (), s32[]{:S(2)}) async-start(), calls=%async_computation.9 | async-start | bytes 3481600 | tf_op jit(solution)/shard_map/all_gather | solution.py:135
  56.2 125.4 %copy-start.50 = (f32[2,170]{1,0:T(2,128)}, f32[2,170]{1,0:T(2,128)S(1)}, u32[]{:S(2)}) copy-start(f32[2,170]{1,0:T(2,128)S(1)} %broadcast_multiply_fusion.1) | copy-start | bytes 4084
  57.2 124.4 %copy-start.68 = (f32[2,170]{1,0:T(2,128)}, f32[2,170]{1,0:T(2,128)S(1)}, u32[]{:S(2)}) copy-start(f32[2,170]{1,0:T(2,128)S(1)} %fusion.86) | copy-start | bytes 4084
  117.2 69.8 %copy-start.40 = (f32[2,1024]{1,0:T(2,128)}, f32[2,1024]{1,0:T(2,128)S(1)}, u32[]{:S(2)}) copy-start(f32[2,1024]{1,0:T(2,128)S(1)} %get-tuple-element.143) | copy-start | bytes 24580
  117.2 69.8 %copy-start.60 = (f32[2,1024]{1,0:T(2,128)}, f32[2,1024]{1,0:T(2,128)S(1)}, u32[]{:S(2)}) copy-start(f32[2,1024]{1,0:T(2,128)S(1)} %get-tuple-element.142) | copy-start | bytes 24580
  197.8 57.8 %all-gather.13.cloned.1.call-start = ((), (), s32[]{:S(2)}) async-start(), calls=%async_computation.8 | async-start | bytes 3481600 | tf_op jit(solution)/shard_map/all_gather | solution.py:136
  197.9 44.4 %copy-start.71 = (bf16[1024]{0:T(1024)(128)(2,1)S(1)}, bf16[1024]{0:T(1024)(128)(2,1)}, u32[]{:S(2)}) copy-start(bf16[1024]{0:T(1024)(128)(2,1)} %get-tuple-element.105) | copy-start | bytes 6148
  197.9 44.9 %copy-start.85 = (u32[32]{0:T(128)S(1)}, u32[32]{0:T(128)}, u32[]{:S(2)}) copy-start(u32[32]{0:T(128)} %constant.83) | copy-start | bytes 388
  199.5 111.5 %all-gather.17.cloned.1.call-start = ((), (), s32[]{:S(2)}) async-start(), calls=%async_computation.10 | async-start | bytes 2162688 | tf_op jit(solution)/shard_map/all_gather | solution.py:110
  200.2 190.1 %all-gather.19.cloned.1.call-start = ((), (), s32[]{:S(2)}) async-start(), calls=%async_computation.11 | async-start | bytes 8650752 | tf_op jit(solution)/shard_map/all_gather | solution.py:112
  201.0 268.4 %all-gather.21.cloned.1.call-start = ((), (), s32[]{:S(2)}) async-start(), calls=%async_computation.12 | async-start | bytes 8650752 | tf_op jit(solution)/shard_map/all_gather | solution.py:114
  201.8 455.9 %all-reduce.33.cloned.1.call-start = ((), (), s32[]{:S(2)}) async-start(), calls=%async_computation.20 | async-start | bytes 11141120
  202.2 62.0 %copy-start.44 = (f32[16]{0:T(128)}, f32[16]{0:T(128)S(1)}, u32[]{:S(2)}) copy-start(f32[16]{0:T(128)S(1)} %exp.17) | copy-start | bytes 196
  311.0 79.3 %copy-start.42 = (f32[2,1024]{1,0:T(2,128)S(1)}, f32[2,1024]{1,0:T(2,128)}, u32[]{:S(2)}) copy-start(f32[2,1024]{1,0:T(2,128)} %get-tuple-element.141) | copy-start | bytes 24580
  311.0 79.3 %copy-start.53 = (f32[32,1,128]{2,1,0:T(1,128)S(1)}, f32[32,1,128]{2,1,0:T(1,128)}, u32[]{:S(2)}) copy-start(f32[32,1,128]{2,1,0:T(1,128)} %convert_element_type.315) | copy-start | bytes 49156
  311.0 79.3 %copy-start.62 = (f32[2,1024]{1,0:T(2,128)S(1)}, f32[2,1024]{1,0:T(2,128)}, u32[]{:S(2)}) copy-start(f32[2,1024]{1,0:T(2,128)} %get-tuple-element.140) | copy-start | bytes 24580
  315.3 168.9 %copy-start.46 = (f32[2,170]{1,0:T(2,128)}, f32[2,170]{1,0:T(2,128)S(1)}, u32[]{:S(2)}) copy-start(f32[2,170]{1,0:T(2,128)S(1)} %broadcast_multiply_fusion) | copy-start | bytes 4084
  315.7 168.6 %copy-start.58 = (f32[2,170]{1,0:T(2,128)}, f32[2,170]{1,0:T(2,128)S(1)}, u32[]{:S(2)}) copy-start(f32[2,170]{1,0:T(2,128)S(1)} %fusion.87) | copy-start | bytes 4084
  315.7 172.9 %copy-start.28 = (f32[2,16,170]{2,1,0:T(8,128)}, f32[2,16,170]{2,1,0:T(8,128)S(1)}, u32[]{:S(2)}) copy-start(f32[2,16,170]{2,1,0:T(8,128)S(1)} %log_add_fusion) | copy-start | bytes 65284
  390.3 79.1 %copy-start.21 = (bf16[2,170,1024]{2,0,1:T(2,128)(2,1)S(1)}, bf16[2,170,1024]{2,0,1:T(2,128)(2,1)}, u32[]{:S(2)}) copy-start(bf16[2,170,1024]{2,0,1:T(2,128)(2,1)} %param.17) | copy-start | bytes 2088964
  390.3 79.1 %copy-start.39 = (f32[2,1024]{1,0:T(2,128)S(1)}, f32[2,1024]{1,0:T(2,128)}, u32[]{:S(2)}) copy-start(f32[2,1024]{1,0:T(2,128)} %get-tuple-element.139) | copy-start | bytes 24580
  551.8 781.4 %all-reduce.31.cloned.1.call-start = ((), (), s32[]{:S(2)}) async-start(), calls=%async_computation.19 | async-start | bytes 75497472
  706.0 723.9 %reduce-scatter.24.cloned.1.call-start = ((), (), s32[]{:S(2)}) async-start(), calls=%async_computation.14 | async-start | bytes 20480 | tf_op jit(solution)/shard_map/reduce_scatter | solution.py:356
  706.8 759.6 %reduce-scatter.28.cloned.1.call-start = ((), (), s32[]{:S(2)}) async-start(), calls=%async_computation.16 | async-start | bytes 589824 | tf_op jit(solution)/shard_map/reduce_scatter | solution.py:327
  1335.8 152.2 %reduce-scatter.26.cloned.1.call-start = ((), (), s32[]{:S(2)}) async-start(), calls=%async_computation.15 | async-start | bytes 1769472 | tf_op jit(solution)/shard_map/reduce_scatter | solution.py:318
  1339.2 220.2 %reduce-scatter.32.cloned.1.call-start = ((), (), s32[]{:S(2)}) async-start(), calls=%async_computation.18 | async-start | bytes 2359296 | tf_op jit(solution)/shard_map/reduce_scatter | solution.py:339
  1342.9 287.2 %reduce-scatter.30.cloned.1.call-start = ((), (), s32[]{:S(2)}) async-start(), calls=%async_computation.17 | async-start | bytes 2359296 | tf_op jit(solution)/shard_map/reduce_scatter | solution.py:333
  1346.8 361.0 %reduce-scatter.22.cloned.1.call-start = ((), (), s32[]{:S(2)}) async-start(), calls=%async_computation.13 | async-start | bytes 3538944 | tf_op jit(solution)/shard_map/reduce_scatter | solution.py:364
  (77 other events, 577.0 us)
Sparse Core Ops, SparseCore 0:
  11.5 98.6 all-gather.8
  113.7 67.8 all-gather.10
  197.9 25.0 all-gather.14
  225.0 26.4 all-gather.12
  254.8 56.2 all-gather.16
  314.3 75.9 all-gather.18
  393.7 75.6 all-gather.20
  552.0 105.7 all-reduce.32
  706.1 627.0 all-reduce.30
  1336.1 18.8 reduce-scatter.23
  1358.9 61.2 reduce-scatter.27
  1423.4 64.4 reduce-scatter.25
  1491.5 67.7 reduce-scatter.31
  1562.7 67.3 reduce-scatter.29
  1633.6 74.1 reduce-scatter.21
where the time goes:
time: 1730 us; the launch traced here: 1720 us
  waiting for transfers between devices  1230 us (71%)
  blocking collectives  169 us (10%)
  matrix products  145 us (8%)
  local copies, waits for them, and re-layouts  90.9 us (5%)
  other arithmetic  65 us (4%)
    unnamed x17, waiting for transfers between devices  705 us
    unnamed x3, blocking collectives  84.1 us
    reduce_scatter x1, waiting for transfers between devices, body(): lax.psum_scatter(modw_group.astype(jnp.bfloat16), 'img', scatter_dimensio...  75.9 us
    all_gather x1, waiting for transfers between devices, body(): lax.all_gather(expw_low, ('img', 'seq'), axis=0, tiled=True)  74.6 us
    all_gather x1, waiting for transfers between devices, body(): lax.all_gather(shrw_low, ('img', 'seq'), axis=0, tiled=True)  70.6 us
    reduce_scatter x1, waiting for transfers between devices, body(): lax.psum_scatter(group_sums[7].astype(jnp.bfloat16), 'img', scatter_dimen...  69.7 us
    reduce_scatter x1, waiting for transfers between devices, body(): lax.psum_scatter(group_sums[5].astype(jnp.bfloat16), 'img', scatter_dimen...  69 us
    all_gather x1, waiting for transfers between devices, body(): lax.all_gather(attnw_low, ('img', 'seq'), axis=0, tiled=True)  64.4 us
  transfers between devices with their start and end apart: 15, of which 11 were waited for; matrix products, arithmetic and copies ran while one was open for 9% of the time, Pallas kernels for 0%

commit v1 on v0

v1 whole, which is shorter than its diff:
```python
import functools

import jax
import jax.numpy as jnp
from jax import lax
from jax.experimental import pallas as pl
from jax.experimental.pallas import tpu as pltpu
from jax.sharding import PartitionSpec as P

HIGH = lax.Precision.HIGHEST
MESH = pl.DeviceIdType.MESH
bf16 = jnp.bfloat16
f32 = jnp.float32
VM = pltpu.VMEM
LIMIT = 56 << 20


def greet(axis, peers):
    barrier = pltpu.get_barrier_semaphore()
    for peer in peers:
        pl.semaphore_signal(barrier, inc=1, device_id={axis: peer}, device_id_type=MESH)
    pl.semaphore_wait(barrier, len(peers))


def direct_kernel(axis, n, everyone, src_rel, dst_rel, x_ref, out_ref, send_sem, recv_sem):
    me = lax.axis_index(axis)
    greet(axis, [me ^ j for j in range(1, n)])
    copies = []
    for j in range(1, n):
        peer = me ^ j
        copy = pltpu.make_async_remote_copy(
            src_ref=x_ref if everyone else x_ref.at[j if src_rel else peer],
            dst_ref=out_ref.at[j if dst_rel else me],
            send_sem=send_sem.at[j],
            recv_sem=recv_sem.at[j],
            device_id={axis: peer},
            device_id_type=MESH,
        )
        copy.start()
        copies.append(copy)
    own = x_ref[...] if everyone else x_ref[0 if src_rel else me]
    out_ref[0 if dst_rel else me] = own
    for copy in copies:
        copy.wait()


def direct(x, axis, cid, everyone=False, src_rel=False, dst_rel=False):
    n = lax.axis_size(axis)
    shape = ((n,) + x.shape) if everyone else x.shape
    return pl.pallas_call(
        functools.partial(direct_kernel, axis, n, everyone, src_rel, dst_rel),
        out_shape=jax.ShapeDtypeStruct(shape, x.dtype),
        in_specs=[pl.BlockSpec(memory_space=VM)],
        out_specs=pl.BlockSpec(memory_space=VM),
        scratch_shapes=[pltpu.SemaphoreType.DMA((n,)), pltpu.SemaphoreType.DMA((n,))],
        compiler_params=pltpu.CompilerParams(collective_id=cid, has_side_effects=True),
        name=f"direct_{cid}",
    )(x)


def gather_kernel(axis, n, x_ref, out_ref, own_sem, send_sem, recv_sem):
    me = lax.axis_index(axis)
    chunks = x_ref.shape[0]
    outer = n // 2
    greet(axis, [me ^ 1] + [me ^ (2 * o) for o in range(1, outer)])

    def remote(src, block, c, j, peer):
        return pltpu.make_async_remote_copy(
            src_ref=src,
            dst_ref=out_ref.at[block, c],
            send_sem=send_sem.at[j, c],
            recv_sem=recv_sem.at[j, c],
            device_id={axis: peer},
            device_id_type=MESH,
        )

    keep = pltpu.make_async_copy(x_ref, out_ref.at[0], own_sem)
    keep.start()
    sends = []
    for c in range(chunks):
        for o in range(1, outer):
            copy = remote(x_ref.at[c], 2 * o, c, 2 * o, me ^ (2 * o))
            copy.start()
            sends.append(copy)
    near = []
    for c in range(chunks):
        copy = remote(x_ref.at[c], 1, c, 1, me ^ 1)
        copy.start()
        near.append(copy)
    for i, copy in enumerate(sends):
        c, o = divmod(i, outer - 1)
        o += 1
        copy.wait_recv()
        hand = remote(out_ref.at[2 * o, c], 2 * o + 1, c, 2 * o + 1, me ^ 1)
        hand.start()
        near.append(hand)
    for copy in sends:
        copy.wait_send()
    for copy in near:
        copy.wait()
    keep.wait()


def gather_rel(x, axis, cid):
    n = lax.axis_size(axis)
    return pl.pallas_call(
        functools.partial(gather_kernel, axis, n),
        out_shape=jax.ShapeDtypeStruct((n,) + x.shape, x.dtype),
        in_specs=[pl.BlockSpec(memory_space=VM)],
        out_specs=pl.BlockSpec(memory_space=pl.ANY),
        scratch_shapes=[
            pltpu.SemaphoreType.DMA,
            pltpu.SemaphoreType.DMA((n, x.shape[0])),
            pltpu.SemaphoreType.DMA((n, x.shape[0])),
        ],
        compiler_params=pltpu.CompilerParams(
            collective_id=cid, has_side_effects=True, vmem_limit_bytes=LIMIT
        ),
        name=f"gather_{cid}",
    )(x)


def scatter_kernel(axis, n, rel, x_ref, out_ref, near_buf, send_buf, far_buf, s1, r1, s2, r2):
    me = lax.axis_index(axis)
    chunks = x_ref.shape[1]
    outer = n // 2
    greet(axis, [me ^ 1] + [me ^ (2 * o) for o in range(1, outer)])

    def block(j):
        return j if rel else me ^ j

    near = {}
    order = list(range(1, outer)) + [0]
    for o in order:
        for c in range(chunks):
            copy = pltpu.make_async_remote_copy(
                src_ref=x_ref.at[block(2 * o + 1), c],
                dst_ref=near_buf.at[o, c],
                send_sem=s1.at[o, c],
                recv_sem=r1.at[o, c],
                device_id={axis: me ^ 1},
                device_id_type=MESH,
            )
            copy.start()
            near[o, c] = copy
    far = []
    for o in order[:-1]:
        for c in range(chunks):
            near[o, c].wait_recv()
            total = x_ref[block(2 * o), c].astype(f32) + near_buf[o, c].astype(f32)
            send_buf[o, c] = total.astype(send_buf.dtype)
            copy = pltpu.make_async_remote_copy(
                src_ref=send_buf.at[o, c],
                dst_ref=far_buf.at[o, c],
                send_sem=s2.at[o, c],
                recv_sem=r2.at[o, c],
                device_id={axis: me ^ (2 * o)},
                device_id_type=MESH,
            )
            copy.start()
            far.append((o, c, copy))
    for c in range(chunks):
        near[0, c].wait_recv()
        out_ref[c] = x_ref[block(0), c].astype(f32) + near_buf[0, c].astype(f32)
    for o, c, copy in far:
        copy.wait_recv()
        out_ref[c] = out_ref[c] + far_buf[o, c].astype(f32)
    for copy in near.values():
        copy.wait_send()
    for _, _, copy in far:
        copy.wait_send()


def scatter_sum(x, axis, cid, rel):
    n = lax.axis_size(axis)
    inner = x.shape[1:]
    half = (n // 2,) + inner
    sems = pltpu.SemaphoreType.DMA((n // 2, inner[0]))
    return pl.pallas_call(
        functools.partial(scatter_kernel, axis, n, rel),
        out_shape=jax.ShapeDtypeStruct(inner, f32),
        in_specs=[pl.BlockSpec(memory_space=VM)],
        out_specs=pl.BlockSpec(memory_space=VM),
        scratch_shapes=[VM(half, x.dtype), VM(half, x.dtype), VM(half, x.dtype), sems, sems, sems, sems],
        compiler_params=pltpu.CompilerParams(
            collective_id=cid, has_side_effects=True, vmem_limit_bytes=LIMIT
        ),
        name=f"scatter_{cid}",
    )(x)


def half_sums(values, low_half):
    first = jnp.sum(jnp.where(low_half, values, 0.0), axis=-1, keepdims=True)
    second = jnp.sum(jnp.where(low_half, 0.0, values), axis=-1, keepdims=True)
    return jnp.where(low_half, first, second)


def dot(a, b, dims):
    return lax.dot_general(a, b, (dims, ((), ())), preferred_element_type=f32)


def load_heads(p_ref, b_ref, rows):
    both = p_ref[...].reshape(rows, 384)
    query = both[:, :128] + b_ref[0, :, :128]
    key = both[:, 128:256]
    value = both[:, 256:] + b_ref[0, :, 256:]
    low_half = lax.broadcasted_iota(jnp.int32, (rows, 128), 1) < 64
    r_query = lax.rsqrt(half_sums(query * query, low_half) + 1e-06)
    r_key = lax.rsqrt(half_sums(key * key, low_half) + 1e-06)
    return query, key, value, low_half, r_query, r_key


def attend_kernel(p_ref, b_ref, es_ref, sk_ref, sq_ref, o_ref, k_buf, v_buf):
    blocks, _, rows_b, _ = p_ref.shape
    rows = blocks * rows_b
    query, key, value, low_half, r_query, r_key = load_heads(p_ref, b_ref, rows)
    query_low = query * r_query * es_ref[0]
    k_buf[...] = (key * r_key).astype(bf16).reshape(blocks, rows_b, 128)
    v_buf[...] = value.astype(bf16).reshape(blocks, rows_b, 128)
    sid_q = sq_ref[0]
    parts = []
    for h in range(2):
        mine = low_half if h == 0 else jnp.logical_not(low_half)
        q_t = jnp.transpose(jnp.where(mine, query_low, 0.0)).astype(bf16)

        def step(b, carry, q_t=q_t):
            total, acc = carry
            scores = dot(k_buf[b], q_t, ((1,), (0,)))
            expo = jnp.where(sk_ref[0, b] <= sid_q, jnp.exp(scores), 0.0)
            total = total + jnp.sum(expo, axis=0, keepdims=True)
            acc = acc + dot(v_buf[b], expo.astype(bf16), ((0,), (0,)))
            return total, acc

        total, acc = lax.fori_loop(
            0, blocks, step, (jnp.zeros((1, rows), f32), jnp.zeros((128, rows), f32))
        )
        parts.append((acc / total)[64 * h : 64 * h + 64])
    out = jnp.transpose(jnp.concatenate(parts, axis=0))
    o_ref[...] = out.astype(bf16).reshape(o_ref.shape)


def attend_back_kernel(
    p_ref, do_ref, b_ref, es_ref, sk_ref, sq_ref, dp_ref, st_ref, k_buf, v_buf, e_buf, g_buf, dk_buf, dv_buf
):
    blocks, _, rows_b, _ = p_ref.shape
    rows = blocks * rows_b
    query, key, value, low_half, r_query, r_key = load_heads(p_ref, b_ref, rows)
    scale = es_ref[0]
    q_unit = query * r_query
    k_unit = key * r_key
    q_full = q_unit * scale
    k_buf[...] = k_unit.astype(bf16).reshape(blocks, rows_b, 128)
    v_buf[...] = value.astype(bf16).reshape(blocks, rows_b, 128)
    d_out = do_ref[...].reshape(rows, 128).astype(f32)
    sid_q = sq_ref[0]
    parts = []
    for h in range(2):
        mine = low_half if h == 0 else jnp.logical_not(low_half)
        q_f = jnp.where(mine, q_full, 0.0)
        do_f = jnp.where(mine, d_out, 0.0)
        q_h = q_f.astype(bf16)
        do_h = do_f.astype(bf16)
        q_t = jnp.transpose(q_f).astype(bf16)
        do_t = jnp.transpose(do_f).astype(bf16)

        def first(b, carry, q_t=q_t, do_t=do_t):
            total, mixed = carry
            scores = dot(k_buf[b], q_t, ((1,), (0,)))
            expo = jnp.where(sk_ref[0, b] <= sid_q, jnp.exp(scores), 0.0)
            grad = dot(v_buf[b], do_t, ((1,), (0,)))
            e_buf[b] = expo
            g_buf[b] = grad
            total = total + jnp.sum(expo, axis=0, keepdims=True)
            mixed = mixed + jnp.sum(expo * grad, axis=0, keepdims=True)
            return total, mixed

        zero = jnp.zeros((1, rows), f32)
        total, mixed = lax.fori_loop(0, blocks, first, (zero, zero))
        inverse = 1.0 / total
        delta = mixed * inverse

        def second(b, acc, inverse=inverse, delta=delta, q_h=q_h, do_h=do_h, h=h):
            probs = e_buf[b] * inverse
            scores_grad = (probs * (g_buf[b] - delta)).astype(bf16)
            dv = dot(probs.astype(bf16), do_h, ((1,), (0,)))
            dk = dot(scores_grad, q_h, ((1,), (0,)))
            if h == 0:
                dv_buf[b] = dv
                dk_buf[b] = dk
            else:
                dv_buf[b] = dv_buf[b] + dv
                dk_buf[b] = dk_buf[b] + dk
            return acc + dot(k_buf[b], scores_grad, ((0,), (0,)))

        acc = lax.fori_loop(0, blocks, second, jnp.zeros((128, rows), f32))
        parts.append(acc[64 * h : 64 * h + 64])
    dq = jnp.transpose(jnp.concatenate(parts, axis=0)).astype(bf16).astype(f32)
    dk = dk_buf[...].reshape(rows, 128).astype(bf16).astype(f32)
    dv = dv_buf[...].reshape(rows, 128).astype(bf16).astype(f32)
    dq_raw = scale * r_query * (dq - q_unit * half_sums(q_unit * dq, low_half))
    dk_raw = r_key * (dk - k_unit * half_sums(k_unit * dk, low_half))
    together = jnp.concatenate([dq_raw, dk_raw, dv], axis=1).astype(bf16)
    dp_ref[...] = together.reshape(dp_ref.shape)
    sums = [
        jnp.sum(dq_raw, axis=0, keepdims=True),
        jnp.sum(dv, axis=0, keepdims=True),
        jnp.sum(dq * q_full, axis=0, keepdims=True),
        jnp.zeros((5, 128), f32),
    ]
    st_ref[0, 0] = jnp.concatenate(sums, axis=0)


def attention_specs(blocks, rows_b):
    rows = blocks * rows_b
    wide = pl.BlockSpec((blocks, 1, rows_b, 384), lambda g, p: (0, g, 0, p))
    slim = pl.BlockSpec((blocks, 1, rows_b, 128), lambda g, p: (0, g, 0, p))
    rest = [
        pl.BlockSpec((1, 1, 384), lambda g, p: (p, 0, 0)),
        pl.BlockSpec((1, 1, 128), lambda g, p: (p, 0, 0)),
        pl.BlockSpec((1, blocks, rows_b, 1), lambda g, p: (g, 0, 0, 0)),
        pl.BlockSpec((1, 1, rows), lambda g, p: (g, 0, 0)),
    ]
    return wide, slim, rest


def attend(packed, bias, scale, sid_k, sid_q):
    blocks, images, rows_b, width = packed.shape
    pairs = width // 384
    wide, slim, rest = attention_specs(blocks, rows_b)
    return pl.pallas_call(
        attend_kernel,
        grid=(images, pairs),
        out_shape=jax.ShapeDtypeStruct((blocks, images, rows_b, pairs * 128), bf16),
        in_specs=[wide] + rest,
        out_specs=slim,
        scratch_shapes=[VM((blocks, rows_b, 128), bf16), VM((blocks, rows_b, 128), bf16)],
        compiler_params=pltpu.CompilerParams(vmem_limit_bytes=LIMIT),
        name="attend",
    )(packed, bias, scale, sid_k, sid_q)


def attend_back(packed, d_out, bias, scale, sid_k, sid_q):
    blocks, images, rows_b, width = packed.shape
    pairs = width // 384
    rows = blocks * rows_b
    wide, slim, rest = attention_specs(blocks, rows_b)
    return pl.pallas_call(
        attend_back_kernel,
        grid=(images, pairs),
        out_shape=(
            jax.ShapeDtypeStruct(packed.shape, bf16),
            jax.ShapeDtypeStruct((images, pairs, 8, 128), f32),
        ),
        in_specs=[wide, slim] + rest,
        out_specs=(wide, pl.BlockSpec((1, 1, 8, 128), lambda g, p: (g, p, 0, 0))),
        scratch_shapes=[
            VM((blocks, rows_b, 128), bf16),
            VM((blocks, rows_b, 128), bf16),
            VM((blocks, rows_b, rows), f32),
            VM((blocks, rows_b, rows), f32),
            VM((blocks, rows_b, 128), f32),
            VM((blocks, rows_b, 128), f32),
        ],
        compiler_params=pltpu.CompilerParams(vmem_limit_bytes=LIMIT),
        name="attend_back",
    )(packed, d_out, bias, scale, sid_k, sid_q)


def normalize(values):
    centered = values - jnp.mean(values, axis=-1, keepdims=True)
    return centered * lax.rsqrt(jnp.mean(centered * centered, axis=-1, keepdims=True) + 1e-06)


def norm_back(values, grad_rows):
    return jax.vjp(normalize, values)[1](grad_rows)[0]


def gelu_tanh(values):
    return jax.nn.gelu(values, approximate=True)


def pad_to(x, size, axis):
    widths = [(0, 0)] * x.ndim
    widths[axis] = (0, size - x.shape[axis])
    return jnp.pad(x, widths)


def flat_rows(vector):
    size = -(-vector.shape[-1] // 1024) * 1024
    vector = pad_to(vector, size, vector.ndim - 1)
    return vector.reshape(vector.shape[:-1] + (size // 128, 128))


def mm(a, b):
    return jnp.dot(a, b, preferred_element_type=f32)


def mm_nt(a, b):
    return lax.dot_general(a, b, (((1,), (1,)), ((), ())), preferred_element_type=f32)


def mm_tn(a, b):
    return lax.dot_general(a, b, (((0,), (0,)), ((), ())), preferred_element_type=f32)


def body(
    tokens,
    cotangent,
    condition,
    scale_sizes,
    mod_weight,
    mod_bias,
    attn_weight,
    query_bias,
    value_bias,
    out_weight,
    out_bias,
    expand_weight,
    expand_bias,
    shrink_weight,
    shrink_bias,
    log_scale,
):
    images, rows, width = tokens.shape
    heads = log_scale.shape[0]
    headdim = width // heads
    seq_n = lax.axis_size("seq")
    img_n = lax.axis_size("img")
    seq_i = lax.axis_index("seq")
    img_i = lax.axis_index("img")
    rank = img_i * seq_n + seq_i
    ranks = img_n * seq_n
    own = width // ranks
    rows_p = -(-rows // 16) * 16
    dim_l = width // seq_n
    pairs = dim_l // 128
    hidden = expand_bias.shape[0] * ranks
    hid_l = hidden // seq_n
    hid_o = hidden // ranks
    mods = mod_weight.shape[1]
    mod_o = mods // ranks

    attn_cut = (
        attn_weight.astype(bf16)
        .reshape(own, 3, seq_n, pairs, 128)
        .transpose(2, 0, 3, 1, 4)
        .reshape(seq_n, own, 3 * dim_l)
    )
    exp_cut = (
        expand_weight.astype(bf16)
        .reshape(own, img_n, seq_n, hid_o)
        .transpose(2, 0, 1, 3)
        .reshape(seq_n, own, hid_l)
    )
    out_cut = jnp.broadcast_to(out_weight.astype(bf16)[None], (seq_n, own, width))
    cut = direct(jnp.concatenate([attn_cut, exp_cut, out_cut], axis=2), "seq", 1)
    cut = cut.reshape(seq_n * own, 3 * dim_l + hid_l + width)
    attn_w = lax.all_gather(cut[:, : 3 * dim_l], "img", axis=0, tiled=True)
    out_w = lax.all_gather(cut[:, 3 * dim_l + hid_l :], "img", axis=0, tiled=True)
    exp_w = lax.all_gather(cut[:, 3 * dim_l : 3 * dim_l + hid_l], "img", axis=0, tiled=True)
    shr_w = lax.all_gather(shrink_weight.astype(bf16), "img", axis=0, tiled=True)

    silu_cond = jax.nn.silu(condition).astype(bf16)
    small_bias = jnp.concatenate([query_bias, value_bias, out_bias, shrink_bias, expand_bias])
    small = jnp.concatenate([silu_cond.astype(f32).reshape(-1), small_bias.astype(bf16).astype(f32)])
    small_n = small.shape[0]
    small_all = direct(flat_rows(small), "img", 2, everyone=True).reshape(img_n, -1)
    cond_all = small_all[:, : images * width].reshape(img_n * images, width)
    bias_col = small_all[:, images * width : small_n]
    cond_mine = lax.dynamic_slice_in_dim(cond_all, rank * own, own, 1).astype(bf16)
    modw_low = mod_weight.astype(bf16)
    mod_part = mm(cond_mine, modw_low)
    bias_here = lax.dynamic_update_slice_in_dim(
        jnp.zeros((mods,), f32), mod_bias.astype(bf16).astype(f32), rank * mod_o, 0
    )
    mod_part = mod_part + bias_here[None]
    mod_img = direct(mod_part.reshape(img_n, images * mods // 128, 128), "img", 3)
    mod_img = jnp.sum(mod_img, axis=0).reshape(-1)
    mod_send = flat_rows(jnp.concatenate([mod_img, bias_col.reshape(-1)]))
    mod_all = direct(mod_send, "seq", 4, everyone=True).reshape(seq_n, -1)
    modulation = jnp.sum(mod_all[:, : images * mods], axis=0).reshape(images, mods)
    bias_n = bias_col.shape[1]
    bias_all = mod_all[:, images * mods : images * mods + img_n * bias_n]
    bias_all = bias_all.reshape(seq_n, img_n, bias_n).transpose(1, 0, 2)
    q_bias = bias_all[:, :, :own].reshape(width)
    v_bias = bias_all[:, :, own : 2 * own].reshape(width)
    o_bias = bias_all[:, :, 2 * own : 3 * own].reshape(width)
    s_bias = bias_all[:, :, 3 * own : 4 * own].reshape(width)
    e_bias = lax.dynamic_slice_in_dim(bias_all[:, :, 4 * own :], seq_i, 1, 1).reshape(hid_l)
    qb_l = lax.dynamic_slice_in_dim(q_bias, seq_i * dim_l, dim_l, 0).reshape(pairs, 1, 128)
    vb_l = lax.dynamic_slice_in_dim(v_bias, seq_i * dim_l, dim_l, 0).reshape(pairs, 1, 128)
    pair_bias = jnp.concatenate([qb_l, jnp.zeros_like(qb_l), vb_l], axis=2)
    head_scale = jnp.exp(jnp.repeat(log_scale, headdim))
    pair_scale = lax.dynamic_slice_in_dim(head_scale, seq_i * dim_l, dim_l, 0).reshape(pairs, 1, 128)
    gain_attn, gain_mlp, scale_attn, scale_mlp, shift_attn, shift_mlp = jnp.split(
        modulation[:, None, :], 6, axis=-1
    )

    ends = jnp.cumsum(scale_sizes, axis=-1)
    offset = jnp.arange(rows_p, dtype=jnp.int32)
    place = (seq_i ^ jnp.arange(seq_n, dtype=jnp.int32))[:, None] * rows + offset[None]
    sid = jnp.sum((place[None, :, :, None] >= ends[:, None, None, :]).astype(jnp.int32), axis=-1)
    sid_q = sid.reshape(images, 1, seq_n * rows_p)
    sid_k = jnp.where(offset[None, None] < rows, sid, 1 << 20)[..., None]

    resid_in = pad_to(tokens, rows_p, 1).astype(f32)
    grad_out = pad_to(cotangent, rows_p, 1).astype(f32)
    all_rows = seq_n * images * rows_p

    normed_in = normalize(resid_in)
    attn_input = (normed_in * (1.0 + scale_attn) + shift_attn).astype(bf16)
    h1 = gather_rel(attn_input, "seq", 5).reshape(all_rows, width)
    packed = mm(h1, attn_w).reshape(seq_n, images, rows_p, 3 * dim_l)
    context = attend(packed, pair_bias, pair_scale, sid_k, sid_q)
    context = direct(context, "seq", 6, src_rel=True)
    context_low = context.transpose(1, 2, 0, 3).reshape(images * rows_p, width)
    attn_out = (mm(context_low, out_w) + o_bias).reshape(images, rows_p, width)
    resid_mid = resid_in + gain_attn * attn_out
    normed_mid = normalize(resid_mid)
    mlp_input = (normed_mid * (1.0 + scale_mlp) + shift_mlp).astype(bf16)
    h2 = gather_rel(mlp_input, "seq", 7).reshape(all_rows, width)
    expanded = mm(h2, exp_w) + e_bias
    activated = gelu_tanh(expanded).astype(bf16)
    shrunk_part = mm(activated, shr_w).astype(bf16).reshape(seq_n, images, rows_p, width)
    shrunk = scatter_sum(shrunk_part, "seq", 8, True) + s_bias
    layer_out = (resid_mid + gain_mlp * shrunk).astype(bf16)

    grad_gain_mlp = jnp.sum(grad_out * shrunk, axis=1)
    grad_shrunk = (grad_out * gain_mlp).astype(bf16)
    shrb_part = jnp.sum(grad_shrunk.astype(f32), axis=(0, 1))
    df = gather_rel(grad_shrunk, "seq", 9).reshape(all_rows, width)
    shrw_part = mm_tn(activated, df).astype(bf16)
    shrw_own = lax.psum_scatter(shrw_part, "img", scatter_dimension=0, tiled=True).astype(f32)
    grad_act = mm_nt(df, shr_w)
    grad_exp = jax.vjp(gelu_tanh, expanded)[1](grad_act)[0].astype(bf16)
    expb_part = jnp.sum(grad_exp.astype(f32), axis=0)
    expw_part = mm_tn(h2, grad_exp).astype(bf16)
    expw_blk = lax.psum_scatter(expw_part, "img", scatter_dimension=0, tiled=True)
    grad_mlp_part = mm_nt(grad_exp, exp_w).astype(bf16).reshape(seq_n, images, rows_p, width)
    grad_mlp_input = scatter_sum(grad_mlp_part, "seq", 10, True)
    grad_scale_mlp = jnp.sum(grad_mlp_input * normed_mid, axis=1)
    grad_shift_mlp = jnp.sum(grad_mlp_input, axis=1)
    grad_mid = grad_out + norm_back(resid_mid, grad_mlp_input * (1.0 + scale_mlp))
    grad_gain_attn = jnp.sum(grad_mid * attn_out, axis=1)
    grad_attn_out = (grad_mid * gain_attn).astype(bf16)
    outb_part = jnp.sum(grad_attn_out.astype(f32), axis=(0, 1))
    da = grad_attn_out.reshape(images * rows_p, width)
    outw_part = mm_tn(context_low, da).astype(bf16)
    outw_blk = lax.psum_scatter(outw_part, "img", scatter_dimension=0, tiled=True)
    grad_context = mm_nt(da, out_w).astype(bf16)
    grad_context = grad_context.reshape(images, rows_p, seq_n, dim_l).transpose(2, 0, 1, 3)
    grad_context = direct(grad_context, "seq", 11, dst_rel=True)
    grad_packed, sums = attend_back(packed, grad_context, pair_bias, pair_scale, sid_k, sid_q)
    sums = jnp.sum(sums, axis=0)
    qb_part = sums[:, 0].reshape(dim_l)
    vb_part = sums[:, 1].reshape(dim_l)
    logs_part = jnp.sum(sums[:, 2].reshape(dim_l // headdim, headdim), axis=1)
    grad_packed = grad_packed.reshape(all_rows, 3 * dim_l)
    grad_in_part = mm_nt(grad_packed, attn_w).astype(bf16).reshape(seq_n, images, rows_p, width)
    attnw_part = mm_tn(h1, grad_packed).astype(bf16)
    grad_attn_input = scatter_sum(grad_in_part, "seq", 12, True)
    grad_scale_attn = jnp.sum(grad_attn_input * normed_in, axis=1)
    grad_shift_attn = jnp.sum(grad_attn_input, axis=1)
    token_grad = grad_mid + norm_back(resid_in, grad_attn_input * (1.0 + scale_attn))
    token_grad = token_grad.astype(bf16)

    cut_rows = seq_n * own
    attnw_blk = scatter_sum(
        attnw_part.reshape(img_n, seq_n, own, 3 * dim_l), "img", 13, False
    ).astype(bf16)
    back_cut = jnp.concatenate(
        [
            attnw_blk.reshape(seq_n, own, 3 * dim_l),
            expw_blk.reshape(seq_n, own, hid_l),
            outw_blk.reshape(seq_n, own, width),
        ],
        axis=2,
    )
    back_cut = direct(back_cut, "seq", 14).astype(f32)
    attnw_own = (
        back_cut[:, :, : 3 * dim_l]
        .reshape(seq_n, own, pairs, 3, 128)
        .transpose(1, 3, 0, 2, 4)
        .reshape(own, 3 * width)
    )
    expw_own = (
        back_cut[:, :, 3 * dim_l : 3 * dim_l + hid_l]
        .reshape(seq_n, own, img_n, hid_o)
        .transpose(1, 2, 0, 3)
        .reshape(own, hidden)
    )
    outw_own = jnp.sum(back_cut[:, :, 3 * dim_l + hid_l :], axis=0)

    grad_mod = jnp.concatenate(
        [grad_gain_attn, grad_gain_mlp, grad_scale_attn, grad_scale_mlp, grad_shift_attn, grad_shift_mlp],
        axis=-1,
    )
    mine = jnp.concatenate(
        [grad_mod.reshape(-1), shrb_part, outb_part, qb_part, vb_part, logs_part, expb_part]
    )
    seen = direct(flat_rows(mine), "seq", 15, everyone=True).reshape(seq_n, -1)
    at = images * mods
    grad_mod = jnp.sum(seen[:, :at], axis=0)
    shrb_sum = jnp.sum(seen[:, at : at + width], axis=0).reshape(img_n, seq_n, own)
    at += width
    outb_sum = jnp.sum(seen[:, at : at + width], axis=0).reshape(img_n, seq_n, own)
    at += width
    qb_sum = seen[:, at : at + dim_l].reshape(img_n, seq_n, own)
    at += dim_l
    vb_sum = seen[:, at : at + dim_l].reshape(img_n, seq_n, own)
    at += dim_l
    logs_sum = seen[:, at : at + heads // seq_n].reshape(heads)
    bias_mine = jnp.stack([shrb_sum, outb_sum, qb_sum, vb_sum], axis=2)
    bias_mine = lax.dynamic_slice_in_dim(bias_mine, seq_i, 1, 1).reshape(img_n, 4 * own)
    block = jnp.concatenate(
        [
            jnp.broadcast_to(grad_mod[None], (img_n, images * mods)),
            bias_mine,
            expb_part.reshape(img_n, hid_o),
            jnp.broadcast_to(logs_sum[None], (img_n, heads)),
        ],
        axis=1,
    )
    got = direct(flat_rows(block), "img", 16).reshape(img_n, -1)
    at = images * mods
    grad_mod_all = got[:, :at].reshape(img_n * images, mods)
    tail = jnp.sum(got[:, at:], axis=0)
    shrb_own = tail[:own]
    outb_own = tail[own : 2 * own]
    qb_own = tail[2 * own : 3 * own]
    vb_own = tail[3 * own : 4 * own]
    expb_own = tail[4 * own : 4 * own + hid_o]
    logs_total = tail[4 * own + hid_o : 4 * own + hid_o + heads]
    modw_own = lax.dot_general(
        cond_mine.astype(f32), grad_mod_all, (((0,), (0,)), ((), ())), precision=HIGH
    )
    modb_own = lax.dynamic_slice_in_dim(jnp.sum(grad_mod_all, axis=0), rank * mod_o, mod_o, 0)
    grad_silu = lax.dot_general(
        grad_mod_all, modw_low.astype(f32), (((1,), (1,)), ((), ())), precision=HIGH
    )
    grad_silu = direct(flat_rows(grad_silu.reshape(img_n, images * own)), "img", 17)
    grad_silu = direct(grad_silu[:, 0], "seq", 18, everyone=True)
    grad_silu = grad_silu[:, :, : images * own].reshape(seq_n, img_n, images, own)
    grad_silu = grad_silu.transpose(2, 1, 0, 3).reshape(images, width)
    cond_grad = jax.vjp(jax.nn.silu, condition)[1](grad_silu)[0]
    return (
        layer_out[:, :rows],
        token_grad[:, :rows],
        cond_grad,
        modw_own,
        modb_own,
        attnw_own,
        qb_own,
        vb_own,
        outw_own,
        outb_own,
        expw_own,
        expb_own,
        shrw_own,
        shrb_own,
        logs_total,
    )


def solution(mesh):
    both = P(("img", "seq"))
    rows = P(("img", "seq"), None)
    return jax.shard_map(
        body,
        mesh=mesh,
        in_specs=(
            P("img", "seq", None),
            P("img", "seq", None),
            P("img", None),
            P("img", None),
            rows,
            both,
            rows,
            both,
            both,
            rows,
            both,
            rows,
            both,
            rows,
            both,
            P(),
        ),
        out_specs=(
            P("img", "seq", None),
            P("img", "seq", None),
            P("img", None),
            rows,
            both,
            rows,
            both,
            both,
            rows,
            both,
            rows,
            both,
            rows,
            both,
            P(),
        ),
        check_vma=False,
    )
```

time: 1730 us -> 533 us (0.31)
  waiting for transfers between devices: 1230 us -> 27.1 us
  Pallas kernels: 0 us -> 338 us
  blocking collectives: 169 us -> 0 us
  matrix products: 145 us -> 75.3 us
  local copies, waits for them, and re-layouts: 90.9 us -> 39.8 us
  other arithmetic: 65 us -> 29 us
    unnamed x17 -> x7, waiting for transfers between devices: 705 us -> 0.78 us
    pallas_call x0 -> x20, Pallas kernels: none -> 338 us  [the longest x11 127 us: direct(): pl.pallas_call(functools.partial(direct_kernel, axis, n, everyone, src_re...]
    all_gather x7 -> x4, waiting for transfers between devices: 290 us -> 26.4 us  [the longest x1 26.3 us: body(): lax.all_gather(shrink_weight.astype(bf16), 'img', axis=0, tiled=True)]
    reduce_scatter x6 -> x3, waiting for transfers between devices: 235 us -> 0.01 us  [the longest x1 0.01 us: body(): lax.psum_scatter(expw_part, 'img', scatter_dimension=0, tiled=True)]
    unnamed x3 -> x0, blocking collectives: 84.1 us -> none
    dot_general x21 -> x15, matrix products: 145 us -> 75.3 us  [the longest x5 26.6 us: mm(): return jnp.dot(a, b, preferred_element_type=f32)]
    psum x2 -> x0, blocking collectives: 45.7 us -> none  [the longest x1 39.5 us: body(): logs_total = lax.psum(grad_logs, ('img', 'seq'))]
    all_gather x1 -> x0, blocking collectives: 39.4 us -> none  [body(): lax.all_gather(expb_low, ('img', 'seq'), axis=0, tiled=True)]
  transfers between devices with their start and end apart: 15 -> 7, of which waited for: 11 -> 1; matrix products, arithmetic and copies ran while one was open for 9% -> 22% of each run, Pallas kernels for 0% -> 62%
where the time goes in v1:
time: 533 us; the launch traced here: 525 us
  Pallas kernels  338 us (63%)
  matrix products  75.3 us (14%)
  local copies, waits for them, and re-layouts  39.8 us (7%)
  other arithmetic  29 us (5%)
  waiting for transfers between devices  27.1 us (5%)
  between operations  15.4 us (3%)
    pallas_call x11, Pallas kernels, direct(): pl.pallas_call(functools.partial(direct_kernel, axis, n, everyone, src_re...  127 us
    pallas_call x4, Pallas kernels, scatter_sum(): pl.pallas_call(functools.partial(scatter_kernel, axis, n, rel), out_shape...  98.3 us
    pallas_call x3, Pallas kernels, gather_rel(): pl.pallas_call(functools.partial(gather_kernel, axis, n), out_shape=jax.S...  64.3 us
    pallas_call x1, Pallas kernels, attend_back(): pl.pallas_call(attend_back_kernel, grid=(images, pairs), out_shape=(jax.S...  29.6 us
    dot_general x5, matrix products, mm(): return jnp.dot(a, b, preferred_element_type=f32)  26.6 us
    dot_general x4, matrix products, mm_nt(): lax.dot_general(a, b, (((1,), (1,)), ((), ())), preferred_element_type=f32)  26.3 us
    all_gather x1, waiting for transfers between devices, body(): lax.all_gather(shrink_weight.astype(bf16), 'img', axis=0, tiled=True)  26.3 us
    dot_general x4, matrix products, mm_tn(): lax.dot_general(a, b, (((0,), (0,)), ((), ())), preferred_element_type=f32)  20.5 us
  transfers between devices with their start and end apart: 7, of which 1 were waited for; matrix products, arithmetic and copies ran while one was open for 22% of the time, Pallas kernels for 62%

profile of v1, /device:TPU:1, one launch (start us, length us, event | category | flops | bytes accessed | tf_op | source)
XLA Modules:
  0.0 525.4 jit_solution(10716068639767620650)
XLA Ops:
  11.0 13.6 %direct_1.1 = bf16[4,32,2816]{2,1,0:T(8,128)(2,1)} custom-call(bf16[4,32,2816]{2,1,0:T(8,128)(2,1)} %pad_maximum_fusion.x_ref), custom_call_target="tpu_custom_call" | custom-call | tf_op jit(solution)/shard_map/direct_1/pallas_call | solution.py:50
  30.8 9.1 %direct_2.1 = f32[8,24,128]{2,1,0:T(8,128)} custom-call(f32[24,128]{1,0:T(8,128)} %bitcast_convert_fusion.1.x_ref), custom_call_target="tpu_custom_call" | custom-call | tf_op jit(solution)/shard_map/direct_2/pallas_call | solution.py:50
  42.2 13.4 %direct_3.1 = f32[8,96,128]{2,1,0:T(8,128)} custom-call(f32[8,96,128]{2,1,0:T(8,128)} %reshape.296.x_ref), custom_call_target="tpu_custom_call" | custom-call | tf_op jit(solution)/shard_map/direct_3/pallas_call | solution.py:50
  57.3 9.7 %direct_4.1 = f32[4,112,128]{2,1,0:T(8,128)} custom-call(f32[112,128]{1,0:T(8,128)} %maximum_bitcast_fusion.x_ref), custom_call_target="tpu_custom_call" | custom-call | tf_op jit(solution)/shard_map/direct_4/pallas_call | solution.py:50
  75.1 21.4 %gather_5.1 = bf16[4,2,176,1024]{3,2,1,0:T(8,128)(2,1)} custom-call(bf16[2,176,1024]{2,1,0:T(8,128)(2,1)} %fusion.16.x_ref), custom_call_target="tpu_custom_call" | custom-call | tf_op jit(solution)/shard_map/gather_5/pallas_call | solution.py:106
  96.6 21.4 %gather_9.1 = bf16[4,2,176,1024]{3,2,1,0:T(8,128)(2,1)} custom-call(bf16[2,176,1024]{2,1,0:T(8,128)(2,1)} %get-tuple-element.107.x_ref), custom_call_target="tpu_custom_call" | custom-call | tf_op jit(solution)/shard_map/gather_9/pallas_call | solution.py:106
  119.7 6.7 %fusion.13.p_ref = f32[4,2,176,768]{3,2,1,0:T(8,128)} fusion(bf16[4,2,176,1024]{3,2,1,0:T(8,128)(2,1)} %gather_5.1, bf16[1024,768]{1,0:T(8,128)(2,1)} %all-gather.5.cloned.1.call-done), kind=kOutput, calls=%fused_computation.33 | convolution fusion | flops 2214592512 | bytes 8781824 | tf_op jit(solution)/shard_map/dot_general | solution.py:395
  126.4 19.0 %attend.1.x_ref = bf16[4,2,176,256]{3,2,1,0:T(8,128)(2,1)} custom-call(f32[4,2,176,768]{3,2,1,0:T(8,128)} %fusion.13.p_ref, f32[2,1,384]{2,1,0:T(1,128)} %pad_maximum_fusion.2.b_ref, f32[2,1,128]{2,1,0:T(1,128)} %bitcast.197, s32[2,4,176,1]{3,2,1,0:T(8,128)} %broadcast_select_fusion.sk_ref, s32[2,1,704]{2,1,0:T(1,128)} %reshape.312.sq_ref), custom_call_target="tpu_custom_call" | custom-call | tf_op jit(solution)/shard_map/attend/pallas_call | solution.py:330
  145.4 12.6 %direct_6.1 = bf16[4,2,176,256]{3,2,1,0:T(8,128)(2,1)} custom-call(bf16[4,2,176,256]{3,2,1,0:T(8,128)(2,1)} %attend.1.x_ref), custom_call_target="tpu_custom_call" | custom-call | tf_op jit(solution)/shard_map/direct_6/pallas_call | solution.py:50
  159.9 2.7 convolution_add_fusion.1
  165.3 21.4 %gather_7.1 = bf16[4,2,176,1024]{3,2,1,0:T(8,128)(2,1)} custom-call(bf16[2,176,1024]{2,1,0:T(8,128)(2,1)} %add_convert_fusion.x_ref), custom_call_target="tpu_custom_call" | custom-call | tf_op jit(solution)/shard_map/gather_7/pallas_call | solution.py:106
  186.8 8.1 %fusion.48 = f32[1408,1024]{1,0:T(8,128)} fusion(bf16[1408,1024]{1,0:T(8,128)(2,1)} %bitcast.147, bf16[1024,1024]{1,0:T(8,128)(2,1)} %all-gather.9.cloned.1.call-done), kind=kOutput, calls=%fused_computation.144 | convolution fusion | flops 2952790016 | bytes 10747904 | tf_op jit(solution)/shard_map/dot_general | solution.py:395
  194.9 26.3 %all-gather.11.cloned.1.call-done = bf16[1024,1024]{1,0:T(8,128)(2,1)} async-done(((bf16[128,1024]{1,0:T(8,128)(2,1)}), bf16[1024,1024]{1,0:T(8,128)(2,1)}) %all-gather.11.cloned.1.call-update) | async-done | bytes 2097168 | tf_op jit(solution)/shard_map/all_gather | solution.py:461
  221.2 10.3 %convert_reduce_fusion = (f32[1024]{0:T(1024)S(1)}, bf16[1408,1024]{1,0:T(8,128)(2,1)S(1)}) fusion(f32[1408,1024]{1,0:T(8,128)} %fusion.48, f32[1024]{0:T(1024)S(1)} %bitcast.204, bf16[1408,1024]{1,0:T(8,128)(2,1)} %bitcast.145, bf16[1024,1024]{1,0:T(8,128)(2,1)} %all-gather.11.cloned.1.call-done), kind=kOutput, calls=%fused_computation.10 | convolution fusion | flops 2985950208 | bytes 13639680 | tf_op jit(solution)/shard_map/dot_general | solution.py:399
  233.0 4.7 convolution_convert_fusion.5
  238.3 8.8 %convolution_convert_fusion.2 = bf16[1408,1024]{1,0:T(8,128)(2,1)} fusion(bf16[1024,1024]{1,0:T(8,128)(2,1)} %all-gather.11.cloned.1.call-done, f32[1408,1024]{1,0:T(8,128)} %fusion.48, f32[1024]{0:T(1024)S(1)} %bitcast.205), kind=kOutput, calls=%fused_computation.14 | convolution fusion | flops 2968649728 | bytes 10752000 | tf_op jit(solution)/shard_map/dot_general | solution.py:395
  247.1 25.5 %scatter_8.1 = f32[2,176,1024]{2,1,0:T(8,128)} custom-call(bf16[4,2,176,1024]{3,2,1,0:T(8,128)(2,1)} %bitcast.150), custom_call_target="tpu_custom_call" | custom-call | tf_op jit(solution)/shard_map/scatter_8/pallas_call | solution.py:179
  272.6 6.4 %convolution_convert_fusion.1 = bf16[1408,1024]{1,0:T(8,128)(2,1)} fusion(bf16[1408,1024]{1,0:T(8,128)(2,1)} %copy-done.30, bf16[1024,1024]{1,0:T(8,128)(2,1)S(1)} %copy-done.23), kind=kOutput, calls=%fused_computation.13 | convolution fusion | flops 2954231808 | bytes 7864320 | tf_op jit(solution)/shard_map/dot_general | solution.py:399
  279.0 23.4 %scatter_10.1 = f32[2,176,1024]{2,1,0:T(8,128)} custom-call(bf16[4,2,176,1024]{3,2,1,0:T(8,128)(2,1)} %bitcast.149), custom_call_target="tpu_custom_call" | custom-call | tf_op jit(solution)/shard_map/scatter_10/pallas_call | solution.py:179
  312.8 3.4 convolution_convert_fusion.6
  319.2 12.8 %direct_11.1.do_ref = bf16[4,2,176,256]{3,2,1,0:T(8,128)(2,1)} custom-call(bf16[4,2,176,256]{3,2,1,0:T(8,128)(2,1)} %bitcast.156), custom_call_target="tpu_custom_call" | custom-call | tf_op jit(solution)/shard_map/direct_11/pallas_call | solution.py:50
  332.0 29.6 %attend_back.1 = (bf16[4,2,176,768]{3,2,1,0:T(8,128)(2,1)}, f32[2,2,8,128]{3,2,1,0:T(8,128)}) custom-call(f32[4,2,176,768]{3,2,1,0:T(8,128)} %fusion.13.p_ref, bf16[4,2,176,256]{3,2,1,0:T(8,128)(2,1)} %direct_11.1.do_ref, f32[2,1,384]{2,1,0:T(1,128)} %pad_maximum_fusion.2.b_ref, f32[2,1,128]{2,1,0:T(1,128)} %bitcast.198, ...), custom_call_target="tpu_custom_call" | custom-call | tf_op jit(solution)/shard_map/attend_back/pallas_call | solution.py:347
  362.3 6.2 %convolution_convert_fusion = bf16[1408,1024]{1,0:T(8,128)(2,1)} fusion(bf16[1408,768]{1,0:T(8,128)(2,1)} %bitcast.207, bf16[1024,768]{1,0:T(8,128)(2,1)} %all-gather.5.cloned.1.call-done), kind=kOutput, calls=%fused_computation.12 | convolution fusion | flops 2216034304 | bytes 6619136 | tf_op jit(solution)/shard_map/dot_general | solution.py:399
  368.6 22.0 %scatter_12.1 = f32[2,176,1024]{2,1,0:T(8,128)} custom-call(bf16[4,2,176,1024]{3,2,1,0:T(8,128)(2,1)} %bitcast.151), custom_call_target="tpu_custom_call" | custom-call | tf_op jit(solution)/shard_map/scatter_12/pallas_call | solution.py:179
  394.5 7.8 %direct_15.1 = f32[4,128,128]{2,1,0:T(8,128)} custom-call(f32[128,128]{1,0:T(8,128)} %pad_bitcast_fusion.1.x_ref), custom_call_target="tpu_custom_call" | custom-call | tf_op jit(solution)/shard_map/direct_15/pallas_call | solution.py:50
  404.1 9.1 %convolution_convert_fusion.4 = bf16[1024,1024]{1,0:T(8,128)(2,1)} fusion(bf16[1408,1024]{1,0:T(8,128)(2,1)} %bitcast.146, f32[1408,1024]{1,0:T(8,128)} %fusion.48, f32[1024]{0:T(1024)S(1)} %bitcast.206), kind=kOutput, calls=%fused_computation.29 | convolution fusion | flops 2968256512 | bytes 10752000 | tf_op jit(solution)/shard_map/dot_general | solution.py:403
  414.2 17.4 %direct_16.1 = f32[8,104,128]{2,1,0:T(8,128)} custom-call(f32[8,104,128]{2,1,0:T(8,128)} %bitcast.162), custom_call_target="tpu_custom_call" | custom-call | tf_op jit(solution)/shard_map/direct_16/pallas_call | solution.py:50
  435.9 4.0 bitcast_convert_fusion
  440.0 27.4 %scatter_13.1 = f32[4,32,768]{2,1,0:T(8,128)} custom-call(bf16[8,4,32,768]{3,2,1,0:T(8,128)(2,1)} %bitcast.164), custom_call_target="tpu_custom_call" | custom-call | tf_op jit(solution)/shard_map/scatter_13/pallas_call | solution.py:179
  473.5 8.4 %direct_17.1 = f32[8,8,128]{2,1,0:T(8,128)} custom-call(f32[8,8,128]{2,1,0:T(8,128)} %bitcast.188), custom_call_target="tpu_custom_call" | custom-call | tf_op jit(solution)/shard_map/direct_17/pallas_call | solution.py:50
  483.3 9.4 %direct_18.1 = f32[4,8,128]{2,1,0:T(8,128)} custom-call(f32[8,128]{1,0:T(8,128)} %bitcast.196), custom_call_target="tpu_custom_call" | custom-call | tf_op jit(solution)/shard_map/direct_18/pallas_call | solution.py:50
  498.3 12.5 %direct_14.1 = bf16[4,32,2816]{2,1,0:T(8,128)(2,1)} custom-call(bf16[4,32,2816]{2,1,0:T(8,128)(2,1)} %pad_maximum_fusion.1.x_ref), custom_call_target="tpu_custom_call" | custom-call | tf_op jit(solution)/shard_map/direct_14/pallas_call | solution.py:50
  (241 shorter events, 75.1 us)
Async XLA Ops:
  7.2 2.5 copy-start.17
  7.2 112.5 %all-gather.5.cloned.1.call-start = ((), (), s32[]{:S(2)}) async-start(), calls=%async_computation.3 | async-start | bytes 1769472 | tf_op jit(solution)/shard_map/all_gather | solution.py:458
  11.0 18.2 %copy-start.18 = (f32[128,1024]{1,0:T(8,128)S(1)}, f32[128,1024]{1,0:T(8,128)}, u32[]{:S(2)}) copy-start(f32[128,1024]{1,0:T(8,128)} %param.29) | copy-start | bytes 1572868
  24.6 5.4 %copy-start.24 = (f32[32]{0:T(128)S(1)}, f32[32]{0:T(128)}, u32[]{:S(2)}) copy-start(f32[32]{0:T(128)} %param.23) | copy-start | bytes 388
  24.6 5.4 %copy-start.25 = (f32[32]{0:T(128)S(1)}, f32[32]{0:T(128)}, u32[]{:S(2)}) copy-start(f32[32]{0:T(128)} %param.24) | copy-start | bytes 388
  24.6 5.4 %copy-start.26 = (f32[32]{0:T(128)S(1)}, f32[32]{0:T(128)}, u32[]{:S(2)}) copy-start(f32[32]{0:T(128)} %param.26) | copy-start | bytes 388
  24.6 5.4 %copy-start.27 = (f32[128]{0:T(128)S(1)}, f32[128]{0:T(128)}, u32[]{:S(2)}) copy-start(f32[128]{0:T(128)} %param.28) | copy-start | bytes 1540
  24.6 5.4 %copy-start.28 = (f32[32]{0:T(128)S(1)}, f32[32]{0:T(128)}, u32[]{:S(2)}) copy-start(f32[32]{0:T(128)} %param.30) | copy-start | bytes 388
  24.6 5.4 %copy-start.19 = (f32[2,1024]{1,0:T(2,128)S(1)}, f32[2,1024]{1,0:T(2,128)}, u32[]{:S(2)}) copy-start(f32[2,1024]{1,0:T(2,128)} %param.18) | copy-start | bytes 24580
  26.3 14.6 %copy-start.20 = (f32[192]{0:T(256)S(1)}, f32[192]{0:T(256)}, u32[]{:S(2)}) copy-start(f32[192]{0:T(256)} %param.21) | copy-start | bytes 2308
  26.3 14.7 %copy-start.8 = (f32[32,6144]{1,0:T(8,128)S(1)}, f32[32,6144]{1,0:T(8,128)}, u32[]{:S(2)}) copy-start(f32[32,6144]{1,0:T(8,128)} %param.20) | copy-start | bytes 2359300
  26.3 133.5 %all-gather.7.cloned.1.call-start = ((), (), s32[]{:S(2)}) async-start(), calls=%async_computation.4 | async-start | bytes 2359296 | tf_op jit(solution)/shard_map/all_gather | solution.py:459
  28.3 158.4 %all-gather.9.cloned.1.call-start = ((), (), s32[]{:S(2)}) async-start(), calls=%async_computation.5 | async-start | bytes 2359296 | tf_op jit(solution)/shard_map/all_gather | solution.py:460
  29.1 192.1 %all-gather.11.cloned.1.call-start = ((), (), s32[]{:S(2)}) async-start(), calls=%async_computation.6 | async-start | bytes 2359296 | tf_op jit(solution)/shard_map/all_gather | solution.py:461
  29.9 466.4 %reduce-scatter.4.cloned.1.call-start = ((), (), s32[]{:S(2)}) async-start(), calls=%async_computation.7 | async-start | bytes 2359296 | tf_op jit(solution)/shard_map/reduce_scatter | solution.py:538
  41.3 26.8 %copy-start.29 = (f32[16]{0:T(128)S(1)}, f32[16]{0:T(128)}, u32[]{:S(2)}) copy-start(f32[16]{0:T(128)} %param.31) | copy-start | bytes 196
  41.3 26.8 %copy-start.21 = (s32[2,10]{1,0:T(2,128)S(1)}, s32[2,10]{1,0:T(2,128)}, u32[]{:S(2)}) copy-start(s32[2,10]{1,0:T(2,128)} %param.19) | copy-start | bytes 244
  41.3 28.1 %copy-start.16 = (bf16[2,170,1024]{2,0,1:T(2,128)(2,1)S(1)}, bf16[2,170,1024]{2,0,1:T(2,128)(2,1)}, u32[]{:S(2)}) copy-start(bf16[2,170,1024]{2,0,1:T(2,128)(2,1)} %param.16) | copy-start | bytes 2088964
  159.8 2.8 copy-start.12
  221.2 11.8 %copy-start.11 = (bf16[4,2,176,1024]{3,2,1,0:T(8,128)(2,1)S(1)}, bf16[4,2,176,1024]{3,2,1,0:T(8,128)(2,1)}, u32[]{:S(2)}) copy-start(bf16[4,2,176,1024]{3,2,1,0:T(8,128)(2,1)} %gather_7.1) | copy-start | bytes 8650756
  237.8 258.5 %reduce-scatter.6.cloned.1.call-start = ((), (), s32[]{:S(2)}) async-start(), calls=%async_computation.8 | async-start | bytes 2359296 | tf_op jit(solution)/shard_map/reduce_scatter | solution.py:549
  247.1 25.5 %copy-start.23 = (bf16[1024,1024]{1,0:T(8,128)(2,1)S(1)}, bf16[1024,1024]{1,0:T(8,128)(2,1)}, u32[]{:S(2)}) copy-start(bf16[1024,1024]{1,0:T(8,128)(2,1)} %all-gather.9.cloned.1.call-done) | copy-start | bytes 6291460
  302.4 1.9 copy-start
  305.7 3.4 copy-start.13
  311.8 204.8 %reduce-scatter.8.cloned.1.call-start = ((), (), s32[]{:S(2)}) async-start(), calls=%async_computation.9 | async-start | bytes 2359296 | tf_op jit(solution)/shard_map/reduce_scatter | solution.py:533
  390.8 2.2 copy-start.2
  431.6 2.3 copy-start.5
  432.8 3.0 copy-start.22
  433.9 2.0 copy-start.10
  439.9 28.5 %copy-start.3 = (f32[2,176,1024]{2,1,0:T(8,128)S(1)}, f32[2,176,1024]{2,1,0:T(8,128)}, u32[]{:S(2)}) copy-start(f32[2,176,1024]{2,1,0:T(8,128)} %scatter_12.1) | copy-start | bytes 4325380
  470.0 1.7 copy-start.9
  510.7 2.0 copy-start.4
  (6 other events, 7.4 us)
Sparse Core Ops, SparseCore 0:
  26.4 43.8 all-gather.4
  73.0 47.5 all-gather.6
  123.3 47.6 all-gather.8
  173.5 47.6 all-gather.10
  237.9 67.5 reduce-scatter.3
  311.9 64.6 reduce-scatter.5
  413.4 73.4 reduce-scatter.7

commit v2 on v1

v2 whole, which is shorter than its diff:
```python
import functools

import jax
import jax.numpy as jnp
from jax import lax
from jax.experimental import pallas as pl
from jax.experimental.pallas import tpu as pltpu
from jax.sharding import PartitionSpec as P

HIGH = lax.Precision.HIGHEST
MESH = pl.DeviceIdType.MESH
bf16 = jnp.bfloat16
f32 = jnp.float32
VM = pltpu.VMEM
LIMIT = 56 << 20


class Plan:
    def __init__(self, ins, out, scratch, peers, count, bind, out_space=VM):
        self.ins, self.out, self.out_space = ins, out, out_space
        self.scratch, self.peers, self.count, self.bind = scratch, peers, count, bind


def remote(src, dst, send, recv, axis, peer):
    return pltpu.make_async_remote_copy(
        src_ref=src, dst_ref=dst, send_sem=send, recv_sem=recv, device_id={axis: peer}, device_id_type=MESH
    )


def each(low, high, run):
    def once(i, carry):
        run(i)
        return carry

    lax.fori_loop(low, high, once, 0)


def direct(x, axis, everyone=False, src_rel=False, dst_rel=False):
    n = lax.axis_size(axis)

    def bind(x_ref, out_ref, send, recv):
        me = lax.axis_index(axis)

        def copy(j):
            src = x_ref if everyone else x_ref.at[j if src_rel else me ^ j]
            return remote(src, out_ref.at[j if dst_rel else me], send.at[j], recv.at[j], axis, me ^ j)

        def start():
            for j in range(1, n):
                copy(j).start()
            out_ref[0 if dst_rel else me] = x_ref[...] if everyone else x_ref[0 if src_rel else me]

        def finish():
            for j in range(1, n):
                copy(j).wait()

        return start, None, finish

    shape = ((n,) + x.shape) if everyone else x.shape
    sems = pltpu.SemaphoreType.DMA((n,))
    peers = [(axis, j) for j in range(1, n)]
    return Plan([x], jax.ShapeDtypeStruct(shape, x.dtype), [sems, sems], peers, 0, bind)


def two_level(axis, n):
    return [(axis, 1)] + [(axis, 2 * o) for o in range(1, n // 2)]


def gather(x, axis, rel, inside=False):
    n = lax.axis_size(axis)
    outer = n // 2
    chunks = x.shape[0]

    def bind(x_ref, out_ref, own, send, recv):
        me = lax.axis_index(axis)

        def place(sender, j, c):
            block = j if rel else sender
            return out_ref.at[c, block] if inside else out_ref.at[block, c]

        def keep(c):
            return pltpu.make_async_copy(x_ref.at[c], place(me, 0, c), own.at[c])

        def push(j, c):
            return remote(x_ref.at[c], place(me, j, c), send.at[j, c], recv.at[j, c], axis, me ^ j)

        def hand(j, c):
            far = me ^ j
            return remote(
                place(far, j, c), place(far, j + 1, c), send.at[j + 1, c], recv.at[j + 1, c], axis, me ^ 1
            )

        def start():
            def first(c):
                for o in range(1, outer):
                    push(2 * o, c).start()

            def second(c):
                push(1, c).start()
                keep(c).start()

            each(0, chunks, first)
            each(0, chunks, second)

        def step(c):
            for o in range(1, outer):
                push(2 * o, c).wait_recv()
                hand(2 * o, c).start()

        def finish():
            def last(c):
                for o in range(1, outer):
                    push(2 * o, c).wait_send()
                    hand(2 * o, c).wait()
                push(1, c).wait()
                keep(c).wait()

            each(0, chunks, last)

        return start, step, finish

    sems = pltpu.SemaphoreType.DMA((n, chunks))
    shape = (chunks, n) + x.shape[1:] if inside else (n,) + x.shape
    out = jax.ShapeDtypeStruct(shape, x.dtype)
    scratch = [pltpu.SemaphoreType.DMA((chunks,)), sems, sems]
    return Plan([x], out, scratch, two_level(axis, n), chunks, bind, pl.ANY)


def scatter_sum(x, axis, rel, dtype=jnp.float32, inside=False):
    n = lax.axis_size(axis)
    outer = n // 2
    chunks = x.shape[0 if inside else 1]

    def bind(x_ref, out_ref, near_buf, send_buf, far_buf, s1, r1, s2, r2):
        me = lax.axis_index(axis)

        def part(j, c):
            block = j if rel else me ^ j
            return x_ref.at[c, block] if inside else x_ref.at[block, c]

        def near(o, c):
            return remote(part(2 * o + 1, c), near_buf.at[o, c], s1.at[o, c], r1.at[o, c], axis, me ^ 1)

        def far(o, c):
            return remote(send_buf.at[o, c], far_buf.at[o, c], s2.at[o, c], r2.at[o, c], axis, me ^ (2 * o))

        def start():
            def first(c):
                for o in range(1, outer):
                    near(o, c).start()

            each(0, chunks, first)
            each(0, chunks, lambda c: near(0, c).start())

        def step(c):
            for o in range(1, outer):
                near(o, c).wait_recv()
                total = part(2 * o, c)[...].astype(f32) + near_buf[o, c].astype(f32)
                send_buf[o, c] = total.astype(send_buf.dtype)
                far(o, c).start()

        def finish():
            def last(c):
                near(0, c).wait_recv()
                total = part(0, c)[...].astype(f32) + near_buf[0, c].astype(f32)
                for o in range(1, outer):
                    far(o, c).wait_recv()
                    total = total + far_buf[o, c].astype(f32)
                out_ref[c] = total.astype(dtype)
                for o in range(outer):
                    near(o, c).wait_send()
                for o in range(1, outer):
                    far(o, c).wait_send()

            each(0, chunks, last)

        return start, step, finish

    inner = (chunks,) + x.shape[2:]
    half = VM((outer,) + inner, x.dtype)
    sems = pltpu.SemaphoreType.DMA((outer, chunks))
    out = jax.ShapeDtypeStruct(inner, dtype)
    return Plan([x], out, [half, half, half, sems, sems, sems, sems], two_level(axis, n), chunks, bind)


class Session:
    def __init__(self, plans, more_peers=()):
        self.plans = plans
        self.ins = [x for p in plans for x in p.ins]
        self.outs = [p.out for p in plans]
        self.in_specs = [pl.BlockSpec(memory_space=VM)] * len(self.ins)
        self.out_specs = [pl.BlockSpec(memory_space=p.out_space) for p in plans]
        self.scratch = [scr for p in plans for scr in p.scratch]
        self.peers = sorted({peer for p in plans for peer in p.peers} | set(more_peers))

    def greet(self):
        barrier = pltpu.get_barrier_semaphore()
        for axis, j in self.peers:
            pl.semaphore_signal(barrier, inc=1, device_id={axis: lax.axis_index(axis) ^ j}, device_id_type=MESH)
        pl.semaphore_wait(barrier, len(self.peers))

    def bind(self, ins, outs, scratch):
        at_in = at_scr = 0
        self.bound = []
        for p, out in zip(self.plans, outs):
            mine = ins[at_in : at_in + len(p.ins)]
            own = scratch[at_scr : at_scr + len(p.scratch)]
            self.bound.append((p.count,) + p.bind(*mine, out, *own))
            at_in += len(p.ins)
            at_scr += len(p.scratch)

    def start(self):
        for _, start, _, _ in self.bound:
            start()

    def steps(self, i, total):
        for count, _, step, _ in self.bound:
            if count == total:
                step(i)
            elif count:
                each((i * count) // total, ((i + 1) * count) // total, step)

    def finish(self):
        for _, _, _, finish in self.bound:
            finish()


def params(cid):
    return pltpu.CompilerParams(collective_id=cid, has_side_effects=True, vmem_limit_bytes=LIMIT)


def exchange(cid, *plans):
    session = Session(plans)
    ins, outs = len(session.ins), len(plans)
    turns = max(p.count for p in plans)

    def kernel(*refs):
        session.greet()
        session.bind(refs[:ins], refs[ins : ins + outs], refs[ins + outs :])
        session.start()
        if turns:
            each(0, turns, lambda i: session.steps(i, turns))
        session.finish()

    got = pl.pallas_call(
        kernel,
        out_shape=tuple(session.outs),
        in_specs=session.in_specs,
        out_specs=tuple(session.out_specs),
        scratch_shapes=session.scratch,
        compiler_params=params(cid),
        name=f"exchange_{cid}",
    )(*session.ins)
    return got[0] if len(plans) == 1 else got


def half_sums(values, low_half):
    first = jnp.sum(jnp.where(low_half, values, 0.0), axis=-1, keepdims=True)
    second = jnp.sum(jnp.where(low_half, 0.0, values), axis=-1, keepdims=True)
    return jnp.where(low_half, first, second)


def dot(a, b, dims):
    return lax.dot_general(a, b, (dims, ((), ())), preferred_element_type=f32)


def lanes(start, size):
    return pl.ds(pl.multiple_of(start, 128), size)


def load_heads(p_ref, bias, g, p, rows):
    both = p_ref[:, g, :, lanes(p * 384, 384)].reshape(rows, 384)
    query = both[:, :128] + bias[:, :128]
    key = both[:, 128:256]
    value = both[:, 256:] + bias[:, 256:]
    low_half = lax.broadcasted_iota(jnp.int32, (rows, 128), 1) < 64
    r_query = lax.rsqrt(half_sums(query * query, low_half) + 1e-06)
    r_key = lax.rsqrt(half_sums(key * key, low_half) + 1e-06)
    return query, key, value, low_half, r_query, r_key


def attend(cid, packed, bias, scale, sid_k, sid_q, plans):
    blocks, images, rows_b, wide = packed.shape
    pairs = wide // 384
    rows = blocks * rows_b
    turns = images * pairs
    width = pairs * 128 * blocks
    session = Session(plans, [("seq", j) for j in range(1, blocks)])
    ins, outs = 5 + len(session.ins), 1 + len(plans)

    def kernel(*refs):
        p_ref, b_ref, es_ref, sk_ref, sq_ref = refs[:5]
        o_ref = refs[ins]
        k_buf, v_buf, o_buf, o_send, o_recv = refs[ins + outs : ins + outs + 5]
        me = lax.axis_index("seq")
        session.greet()
        session.bind(refs[5:ins], refs[ins + 1 : ins + outs], refs[ins + outs + 5 :])
        session.start()

        def ship(i, j):
            g, p = i // pairs, i % pairs
            return remote(
                o_buf.at[i, j],
                o_ref.at[g, :, lanes((me * pairs + p) * 128, 128)],
                o_send.at[j, i],
                o_recv.at[j, i],
                "seq",
                me ^ j,
            )

        def turn(i):
            g, p = i // pairs, i % pairs
            query, key, value, low_half, r_query, r_key = load_heads(p_ref, b_ref[p], g, p, rows)
            query_low = query * r_query * es_ref[p]
            k_buf[...] = (key * r_key).astype(bf16).reshape(blocks, rows_b, 128)
            v_buf[...] = value.astype(bf16).reshape(blocks, rows_b, 128)
            sid_q = sq_ref[g]
            parts = []
            for h in range(2):
                mine = low_half if h == 0 else jnp.logical_not(low_half)
                q_t = jnp.transpose(jnp.where(mine, query_low, 0.0)).astype(bf16)

                def step(b, carry, q_t=q_t):
                    total, acc = carry
                    scores = dot(k_buf[b], q_t, ((1,), (0,)))
                    expo = jnp.where(sk_ref[g, b] <= sid_q, jnp.exp(scores), 0.0)
                    total = total + jnp.sum(expo, axis=0, keepdims=True)
                    acc = acc + dot(v_buf[b], expo.astype(bf16), ((0,), (0,)))
                    return total, acc

                total, acc = lax.fori_loop(
                    0, blocks, step, (jnp.zeros((1, rows), f32), jnp.zeros((128, rows), f32))
                )
                parts.append((acc / total)[64 * h : 64 * h + 64])
            out = jnp.transpose(jnp.concatenate(parts, axis=0)).astype(bf16).reshape(blocks, rows_b, 128)
            o_buf[i] = out
            o_ref[g, :, lanes((me * pairs + p) * 128, 128)] = out[0]
            for j in range(1, blocks):
                ship(i, j).start()
            session.steps(i, turns)

        each(0, turns, turn)
        session.finish()

        def last(i):
            for j in range(1, blocks):
                ship(i, j).wait()

        each(0, turns, last)

    full = pl.BlockSpec(memory_space=VM)
    sems = pltpu.SemaphoreType.DMA((blocks, turns))
    return pl.pallas_call(
        kernel,
        out_shape=tuple([jax.ShapeDtypeStruct((images, rows_b, width), bf16)] + session.outs),
        in_specs=[full] * 5 + session.in_specs,
        out_specs=tuple([full] + session.out_specs),
        scratch_shapes=[
            VM((blocks, rows_b, 128), bf16),
            VM((blocks, rows_b, 128), bf16),
            VM((turns, blocks, rows_b, 128), bf16),
            sems,
            sems,
        ]
        + session.scratch,
        compiler_params=params(cid),
        name="attend",
    )(packed, bias, scale, sid_k, sid_q, *session.ins)


def attend_back(cid, packed, d_out, bias, scale, sid_k, sid_q, plans):
    blocks, images, rows_b, wide = packed.shape
    pairs = wide // 384
    rows = blocks * rows_b
    turns = images * pairs
    session = Session(plans, [("seq", j) for j in range(1, blocks)])
    ins, outs = 6 + len(session.ins), 2 + len(plans)

    def kernel(*refs):
        p_ref, do_ref, b_ref, es_ref, sk_ref, sq_ref = refs[:6]
        dp_ref, st_ref = refs[ins : ins + 2]
        k_buf, v_buf, e_buf, g_buf, dk_buf, dv_buf, do_buf, o_send, o_recv = refs[ins + outs : ins + outs + 9]
        me = lax.axis_index("seq")
        session.greet()

        def ship(i, j):
            g, p = i // pairs, i % pairs
            return remote(
                do_ref.at[g, :, lanes(((me ^ j) * pairs + p) * 128, 128)],
                do_buf.at[i, j],
                o_send.at[j, i],
                o_recv.at[j, i],
                "seq",
                me ^ j,
            )

        def send(i):
            for j in range(1, blocks):
                ship(i, j).start()

        each(0, turns, send)
        session.bind(refs[6:ins], refs[ins + 2 : ins + outs], refs[ins + outs + 9 :])
        session.start()

        def turn(i):
            g, p = i // pairs, i % pairs
            query, key, value, low_half, r_query, r_key = load_heads(p_ref, b_ref[p], g, p, rows)
            scale_row = es_ref[p]
            q_unit = query * r_query
            k_unit = key * r_key
            q_full = q_unit * scale_row
            k_buf[...] = k_unit.astype(bf16).reshape(blocks, rows_b, 128)
            v_buf[...] = value.astype(bf16).reshape(blocks, rows_b, 128)
            do_buf[i, 0] = do_ref[g, :, lanes((me * pairs + p) * 128, 128)]
            for j in range(1, blocks):
                ship(i, j).wait_recv()
            d_out = do_buf[i].reshape(rows, 128).astype(f32)
            sid_q = sq_ref[g]
            parts = []
            for h in range(2):
                mine = low_half if h == 0 else jnp.logical_not(low_half)
                q_f = jnp.where(mine, q_full, 0.0)
                do_f = jnp.where(mine, d_out, 0.0)
                q_h = q_f.astype(bf16)
                do_h = do_f.astype(bf16)
                q_t = jnp.transpose(q_f).astype(bf16)
                do_t = jnp.transpose(do_f).astype(bf16)

                def first(b, carry, q_t=q_t, do_t=do_t):
                    total, mixed = carry
                    scores = dot(k_buf[b], q_t, ((1,), (0,)))
                    expo = jnp.where(sk_ref[g, b] <= sid_q, jnp.exp(scores), 0.0)
                    grad = dot(v_buf[b], do_t, ((1,), (0,)))
                    e_buf[b] = expo
                    g_buf[b] = grad
                    total = total + jnp.sum(expo, axis=0, keepdims=True)
                    mixed = mixed + jnp.sum(expo * grad, axis=0, keepdims=True)
                    return total, mixed

                zero = jnp.zeros((1, rows), f32)
                total, mixed = lax.fori_loop(0, blocks, first, (zero, zero))
                inverse = 1.0 / total
                delta = mixed * inverse

                def second(b, acc, inverse=inverse, delta=delta, q_h=q_h, do_h=do_h, h=h):
                    probs = e_buf[b] * inverse
                    scores_grad = (probs * (g_buf[b] - delta)).astype(bf16)
                    dv = dot(probs.astype(bf16), do_h, ((1,), (0,)))
                    dk = dot(scores_grad, q_h, ((1,), (0,)))
                    if h == 0:
                        dv_buf[b] = dv
                        dk_buf[b] = dk
                    else:
                        dv_buf[b] = dv_buf[b] + dv
                        dk_buf[b] = dk_buf[b] + dk
                    return acc + dot(k_buf[b], scores_grad, ((0,), (0,)))

                acc = lax.fori_loop(0, blocks, second, jnp.zeros((128, rows), f32))
                parts.append(acc[64 * h : 64 * h + 64])
            dq = jnp.transpose(jnp.concatenate(parts, axis=0)).astype(bf16).astype(f32)
            dk = dk_buf[...].reshape(rows, 128).astype(bf16).astype(f32)
            dv = dv_buf[...].reshape(rows, 128).astype(bf16).astype(f32)
            dq_raw = scale_row * r_query * (dq - q_unit * half_sums(q_unit * dq, low_half))
            dk_raw = r_key * (dk - k_unit * half_sums(k_unit * dk, low_half))
            together = jnp.concatenate([dq_raw, dk_raw, dv], axis=1).astype(bf16)
            dp_ref[:, g, :, lanes(p * 384, 384)] = together.reshape(blocks, rows_b, 384)
            sums = [
                jnp.sum(dq_raw, axis=0, keepdims=True),
                jnp.sum(dv, axis=0, keepdims=True),
                jnp.sum(dq * q_full, axis=0, keepdims=True),
                jnp.zeros((5, 128), f32),
            ]
            st_ref[i] = jnp.concatenate(sums, axis=0)
            session.steps(i, turns)

        each(0, turns, turn)
        session.finish()

        def last(i):
            for j in range(1, blocks):
                ship(i, j).wait_send()

        each(0, turns, last)

    full = pl.BlockSpec(memory_space=VM)
    sems = pltpu.SemaphoreType.DMA((blocks, turns))
    return pl.pallas_call(
        kernel,
        out_shape=tuple(
            [jax.ShapeDtypeStruct(packed.shape, bf16), jax.ShapeDtypeStruct((turns, 8, 128), f32)] + session.outs
        ),
        in_specs=[full] * 6 + session.in_specs,
        out_specs=tuple([full] * 2 + session.out_specs),
        scratch_shapes=[
            VM((blocks, rows_b, 128), bf16),
            VM((blocks, rows_b, 128), bf16),
            VM((blocks, rows_b, rows), f32),
            VM((blocks, rows_b, rows), f32),
            VM((blocks, rows_b, 128), f32),
            VM((blocks, rows_b, 128), f32),
            VM((turns, blocks, rows_b, 128), bf16),
            sems,
            sems,
        ]
        + session.scratch,
        compiler_params=params(cid),
        name="attend_back",
    )(packed, d_out, bias, scale, sid_k, sid_q, *session.ins)


def normalize(values):
    centered = values - jnp.mean(values, axis=-1, keepdims=True)
    return centered * lax.rsqrt(jnp.mean(centered * centered, axis=-1, keepdims=True) + 1e-06)


def norm_back(values, grad_rows):
    return jax.vjp(normalize, values)[1](grad_rows)[0]


def gelu_tanh(values):
    return jax.nn.gelu(values, approximate=True)


def pad_to(x, size, axis):
    widths = [(0, 0)] * x.ndim
    widths[axis] = (0, size - x.shape[axis])
    return jnp.pad(x, widths)


def flat_rows(vector):
    size = -(-vector.shape[-1] // 1024) * 1024
    vector = pad_to(vector, size, vector.ndim - 1)
    return vector.reshape(vector.shape[:-1] + (size // 128, 128))


def mm(a, b):
    return jnp.dot(a, b, preferred_element_type=f32)


def mm_nt(a, b):
    return lax.dot_general(a, b, (((1,), (1,)), ((), ())), preferred_element_type=f32)


def mm_tn(a, b):
    return lax.dot_general(a, b, (((0,), (0,)), ((), ())), preferred_element_type=f32)


def body(
    tokens,
    cotangent,
    condition,
    scale_sizes,
    mod_weight,
    mod_bias,
    attn_weight,
    query_bias,
    value_bias,
    out_weight,
    out_bias,
    expand_weight,
    expand_bias,
    shrink_weight,
    shrink_bias,
    log_scale,
):
    images, rows, width = tokens.shape
    heads = log_scale.shape[0]
    headdim = width // heads
    seq_n = lax.axis_size("seq")
    img_n = lax.axis_size("img")
    seq_i = lax.axis_index("seq")
    img_i = lax.axis_index("img")
    rank = img_i * seq_n + seq_i
    ranks = img_n * seq_n
    own = width // ranks
    rows_p = -(-rows // 16) * 16
    dim_l = width // seq_n
    pairs = dim_l // 128
    hidden = expand_bias.shape[0] * ranks
    hid_l = hidden // seq_n
    hid_o = hidden // ranks
    mods = mod_weight.shape[1]
    mod_o = mods // ranks

    mod_l = mods // seq_n
    blk = own * seq_n

    attn_cut = (
        attn_weight.astype(bf16)
        .reshape(own, 3, seq_n, pairs, 128)
        .transpose(2, 0, 3, 1, 4)
        .reshape(seq_n, own, 3 * dim_l)
    )
    exp_cut = (
        expand_weight.astype(bf16)
        .reshape(own, img_n, seq_n, hid_o)
        .transpose(2, 0, 1, 3)
        .reshape(seq_n, own, hid_l)
    )
    mod_cut = mod_weight.astype(bf16).reshape(own, seq_n, mod_l).transpose(1, 0, 2)
    silu_cond = jax.nn.silu(condition).astype(bf16).astype(f32)
    small_bias = jnp.concatenate([query_bias, value_bias, out_bias, shrink_bias, expand_bias, mod_bias])
    small_bias = small_bias.astype(bf16).astype(f32)
    bias_n = small_bias.shape[0]
    cond_cut = silu_cond.reshape(images, img_n, blk).transpose(1, 0, 2).reshape(img_n, images * blk)
    small = jnp.concatenate([cond_cut, jnp.broadcast_to(small_bias[None], (img_n, bias_n))], axis=1)
    cut, small_all, out_img = exchange(
        1,
        direct(jnp.concatenate([mod_cut, attn_cut, exp_cut], axis=2), "seq"),
        direct(flat_rows(small), "img"),
        gather(out_weight.astype(bf16)[None], "img", False),
    )
    out_img = out_img.reshape(img_n, own, width)
    cut = cut.reshape(blk, mod_l + 3 * dim_l + hid_l)
    modw_cut = cut[:, :mod_l]
    attn_b = cut[:, mod_l : mod_l + 3 * dim_l]
    exp_b = cut[:, mod_l + 3 * dim_l :]

    def weight_chunks(x):
        step = max(blk // 4, 8)
        return x.reshape(x.shape[:-2] + (blk // step, step, x.shape[-1]))

    def hidden_chunks(x):
        step = max(hid_o // 4, 8)
        return x.reshape(x.shape[:-2] + (hid_o // step, step, x.shape[-1]))

    small_all = small_all.reshape(img_n, -1)
    cond_mine = small_all[:, : images * blk].reshape(img_n * images, blk).astype(bf16)
    bias_col = small_all[:, images * blk : images * blk + bias_n]
    mod_part = mm(cond_mine, modw_cut).reshape(img_n, images * mod_l)
    mod_img, out_w = exchange(2, direct(flat_rows(mod_part), "img"), gather(out_img, "seq", False, True))
    mod_img = jnp.sum(mod_img, axis=0)
    out_w = out_w.reshape(width, width)
    mod_img = mod_img.reshape(-1)[: images * mod_l]
    mod_send = flat_rows(jnp.concatenate([mod_img, bias_col.reshape(-1)]))
    mod_all = exchange(3, direct(mod_send, "seq", everyone=True)).reshape(seq_n, -1)
    modulation = mod_all[:, : images * mod_l].reshape(seq_n, images, mod_l).transpose(1, 0, 2)
    bias_all = mod_all[:, images * mod_l : images * mod_l + img_n * bias_n]
    bias_all = bias_all.reshape(seq_n, img_n, bias_n).transpose(1, 0, 2)
    q_bias = bias_all[:, :, :own].reshape(width)
    v_bias = bias_all[:, :, own : 2 * own].reshape(width)
    o_bias = bias_all[:, :, 2 * own : 3 * own].reshape(width)
    s_bias = bias_all[:, :, 3 * own : 4 * own].reshape(width)
    e_bias = bias_all[:, :, 4 * own : 4 * own + hid_o]
    e_bias = lax.dynamic_slice_in_dim(e_bias, seq_i, 1, 1).reshape(hid_l)
    m_bias = bias_all[:, :, 4 * own + hid_o :].reshape(mods)
    modulation = modulation.reshape(images, mods) + m_bias[None]
    qb_l = lax.dynamic_slice_in_dim(q_bias, seq_i * dim_l, dim_l, 0).reshape(pairs, 1, 128)
    vb_l = lax.dynamic_slice_in_dim(v_bias, seq_i * dim_l, dim_l, 0).reshape(pairs, 1, 128)
    pair_bias = jnp.concatenate([qb_l, jnp.zeros_like(qb_l), vb_l], axis=2)
    head_scale = jnp.exp(jnp.repeat(log_scale, headdim))
    pair_scale = lax.dynamic_slice_in_dim(head_scale, seq_i * dim_l, dim_l, 0).reshape(pairs, 1, 128)
    gain_attn, gain_mlp, scale_attn, scale_mlp, shift_attn, shift_mlp = jnp.split(
        modulation[:, None, :], 6, axis=-1
    )

    ends = jnp.cumsum(scale_sizes, axis=-1)
    offset = jnp.arange(rows_p, dtype=jnp.int32)
    place = (seq_i ^ jnp.arange(seq_n, dtype=jnp.int32))[:, None] * rows + offset[None]
    sid = jnp.sum((place[None, :, :, None] >= ends[:, None, None, :]).astype(jnp.int32), axis=-1)
    sid_q = sid.reshape(images, 1, seq_n * rows_p)
    sid_k = jnp.where(offset[None, None] < rows, sid, 1 << 20)[..., None]

    resid_in = pad_to(tokens, rows_p, 1).astype(f32)
    grad_out = pad_to(cotangent, rows_p, 1).astype(f32)
    local = images * rows_p
    all_rows = seq_n * local

    def chunked(x):
        return x.reshape(x.shape[: x.ndim - 3] + (local // 32, 32, width))

    normed_in = normalize(resid_in)
    attn_input = (normed_in * (1.0 + scale_attn) + shift_attn).astype(bf16)
    h1, attn_w = exchange(5, gather(chunked(attn_input), "seq", True), gather(weight_chunks(attn_b), "img", False))
    h1 = h1.reshape(all_rows, width)
    attn_w = attn_w.reshape(width, 3 * dim_l)
    packed = mm(h1, attn_w).reshape(seq_n, images, rows_p, 3 * dim_l)
    grad_shrunk = (grad_out * gain_mlp).astype(bf16)
    context_low, df, exp_w = attend(
        6,
        packed,
        pair_bias,
        pair_scale,
        sid_k,
        sid_q,
        [gather(chunked(grad_shrunk), "seq", True), gather(weight_chunks(exp_b), "img", False)],
    )
    context_low = context_low.reshape(local, width)
    df = df.reshape(all_rows, width)
    exp_w = exp_w.reshape(width, hid_l)
    attn_out = (mm(context_low, out_w) + o_bias).reshape(images, rows_p, width)
    resid_mid = resid_in + gain_attn * attn_out
    normed_mid = normalize(resid_mid)
    mlp_input = (normed_mid * (1.0 + scale_mlp) + shift_mlp).astype(bf16)
    h2, shr_w = exchange(
        7,
        gather(chunked(mlp_input), "seq", True),
        gather(hidden_chunks(shrink_weight.astype(bf16)), "img", False),
    )
    h2 = h2.reshape(all_rows, width)
    shr_w = shr_w.reshape(hid_l, width)
    expanded = mm(h2, exp_w) + e_bias
    activated = gelu_tanh(expanded).astype(bf16)

    shrb_part = jnp.sum(grad_shrunk.astype(f32), axis=(0, 1))
    grad_act = mm_nt(df, shr_w)
    grad_exp = jax.vjp(gelu_tanh, expanded)[1](grad_act)[0].astype(bf16)
    grad_mlp_part = mm_nt(grad_exp, exp_w).astype(bf16).reshape(seq_n, images, rows_p, width)
    shrw_part = mm_tn(activated, df).astype(bf16).reshape(img_n, hid_o, width)
    grad_mlp_input, shrw_own = exchange(
        10,
        scatter_sum(chunked(grad_mlp_part), "seq", True),
        scatter_sum(hidden_chunks(shrw_part), "img", False),
    )
    grad_mlp_input = grad_mlp_input.reshape(images, rows_p, width)
    shrw_own = shrw_own.reshape(hid_o, width)
    expb_part = jnp.sum(grad_exp.astype(f32), axis=0)
    expw_part = mm_tn(h2, grad_exp).astype(bf16).reshape(img_n, blk, hid_l)
    shrunk_part = mm(activated, shr_w).astype(bf16).reshape(seq_n, images, rows_p, width)

    grad_scale_mlp = jnp.sum(grad_mlp_input * normed_mid, axis=1)
    grad_shift_mlp = jnp.sum(grad_mlp_input, axis=1)
    grad_mid = grad_out + norm_back(resid_mid, grad_mlp_input * (1.0 + scale_mlp))
    grad_gain_attn = jnp.sum(grad_mid * attn_out, axis=1)
    grad_attn_out = (grad_mid * gain_attn).astype(bf16)
    outb_part = jnp.sum(grad_attn_out.astype(f32), axis=(0, 1))
    da = grad_attn_out.reshape(local, width)
    grad_context = mm_nt(da, out_w).astype(bf16)
    grad_context = grad_context.reshape(images, rows_p, width)
    outw_part = mm_tn(context_low, da).astype(bf16).reshape(img_n, seq_n, own, width)
    grad_packed, sums, expw_blk, shrunk, outw_blk = attend_back(
        11,
        packed,
        grad_context,
        pair_bias,
        pair_scale,
        sid_k,
        sid_q,
        [
            scatter_sum(weight_chunks(expw_part), "img", False, bf16),
            scatter_sum(chunked(shrunk_part), "seq", True),
            scatter_sum(outw_part, "seq", False, bf16, True),
        ],
    )
    shrunk = shrunk.reshape(images, rows_p, width) + s_bias
    layer_out = (resid_mid + gain_mlp * shrunk).astype(bf16)
    grad_gain_mlp = jnp.sum(grad_out * shrunk, axis=1)
    sums = jnp.sum(sums.reshape(images, pairs, 8, 128), axis=0)
    qb_part = sums[:, 0].reshape(dim_l)
    vb_part = sums[:, 1].reshape(dim_l)
    logs_part = jnp.sum(sums[:, 2].reshape(dim_l // headdim, headdim), axis=1)
    grad_packed = grad_packed.reshape(all_rows, 3 * dim_l)
    grad_in_part = mm_nt(grad_packed, attn_w).astype(bf16).reshape(seq_n, images, rows_p, width)
    attnw_part = mm_tn(h1, grad_packed).astype(bf16)
    grad_attn_input, attnw_blk, outw_own = exchange(
        12,
        scatter_sum(chunked(grad_in_part), "seq", True),
        scatter_sum(weight_chunks(attnw_part.reshape(img_n, blk, 3 * dim_l)), "img", False, bf16),
        scatter_sum(outw_blk.reshape(img_n, 1, own, width), "img", False),
    )
    outw_own = outw_own.reshape(own, width)
    grad_attn_input = grad_attn_input.reshape(images, rows_p, width)
    grad_scale_attn = jnp.sum(grad_attn_input * normed_in, axis=1)
    grad_shift_attn = jnp.sum(grad_attn_input, axis=1)
    token_grad = grad_mid + norm_back(resid_in, grad_attn_input * (1.0 + scale_attn))
    token_grad = token_grad.astype(bf16)

    grad_mod = jnp.concatenate(
        [grad_gain_attn, grad_gain_mlp, grad_scale_attn, grad_scale_mlp, grad_shift_attn, grad_shift_mlp],
        axis=-1,
    )
    grad_mod = grad_mod.reshape(images, seq_n, mod_l).transpose(1, 0, 2).reshape(seq_n, images * mod_l)
    mine = jnp.concatenate([shrb_part, outb_part, qb_part, vb_part, logs_part])
    mine = jnp.concatenate([grad_mod, jnp.broadcast_to(mine[None], (seq_n, mine.shape[0]))], axis=1)
    seen = exchange(13, direct(flat_rows(mine), "seq")).reshape(seq_n, -1)
    at = images * mod_l
    grad_mod = jnp.sum(seen[:, :at], axis=0)
    shrb_sum = jnp.sum(seen[:, at : at + width], axis=0).reshape(img_n, seq_n, own)
    at += width
    outb_sum = jnp.sum(seen[:, at : at + width], axis=0).reshape(img_n, seq_n, own)
    at += width
    qb_sum = seen[:, at : at + dim_l].reshape(img_n, seq_n, own)
    at += dim_l
    vb_sum = seen[:, at : at + dim_l].reshape(img_n, seq_n, own)
    at += dim_l
    logs_sum = seen[:, at : at + heads // seq_n].reshape(heads)
    bias_mine = jnp.stack([shrb_sum, outb_sum, qb_sum, vb_sum], axis=2)
    bias_mine = lax.dynamic_slice_in_dim(bias_mine, seq_i, 1, 1).reshape(img_n, 4 * own)
    block = jnp.concatenate(
        [
            jnp.broadcast_to(grad_mod[None], (img_n, images * mod_l)),
            bias_mine,
            expb_part.reshape(img_n, hid_o),
            jnp.broadcast_to(logs_sum[None], (img_n, heads)),
        ],
        axis=1,
    )
    got = exchange(14, direct(flat_rows(block), "img")).reshape(img_n, -1)
    at = images * mod_l
    grad_mod_all = got[:, :at].reshape(img_n * images, mod_l)
    tail = jnp.sum(got[:, at:], axis=0)
    shrb_own = tail[:own]
    outb_own = tail[own : 2 * own]
    qb_own = tail[2 * own : 3 * own]
    vb_own = tail[3 * own : 4 * own]
    expb_own = tail[4 * own : 4 * own + hid_o]
    logs_total = tail[4 * own + hid_o : 4 * own + hid_o + heads]

    modw_blk = mm_tn(cond_mine, grad_mod_all.astype(bf16))
    grad_silu = lax.dot_general(
        grad_mod_all, modw_cut.astype(f32), (((1,), (1,)), ((), ())), precision=HIGH
    )
    modb_all = jnp.sum(grad_mod_all, axis=0)
    back_cut = jnp.concatenate(
        [
            modw_blk.astype(bf16).reshape(seq_n, own, mod_l),
            attnw_blk.reshape(seq_n, own, 3 * dim_l),
            expw_blk.reshape(seq_n, own, hid_l),
        ],
        axis=2,
    )
    back_cut, modb_all, grad_silu = exchange(
        15,
        direct(back_cut, "seq"),
        direct(flat_rows(modb_all), "seq", everyone=True),
        direct(flat_rows(grad_silu.reshape(img_n, images * blk)), "img"),
    )
    grad_silu = exchange(16, direct(grad_silu, "seq", everyone=True)).reshape(seq_n, img_n, -1)
    grad_silu = jnp.sum(grad_silu[:, :, : images * blk], axis=0).reshape(img_n, images, blk)
    grad_silu = grad_silu.transpose(1, 0, 2).reshape(images, width)
    cond_grad = jax.vjp(jax.nn.silu, condition)[1](grad_silu)[0]
    back_cut = back_cut.astype(f32)
    modw_own = back_cut[:, :, :mod_l].transpose(1, 0, 2).reshape(own, mods)
    attnw_own = (
        back_cut[:, :, mod_l : mod_l + 3 * dim_l]
        .reshape(seq_n, own, pairs, 3, 128)
        .transpose(1, 3, 0, 2, 4)
        .reshape(own, 3 * width)
    )
    expw_own = (
        back_cut[:, :, mod_l + 3 * dim_l : mod_l + 3 * dim_l + hid_l]
        .reshape(seq_n, own, img_n, hid_o)
        .transpose(1, 2, 0, 3)
        .reshape(own, hidden)
    )
    modb_all = modb_all.reshape(seq_n, -1)[:, :mod_l].reshape(mods)
    modb_own = lax.dynamic_slice_in_dim(modb_all, rank * mod_o, mod_o, 0)
    return (
        layer_out[:, :rows],
        token_grad[:, :rows],
        cond_grad,
        modw_own,
        modb_own,
        attnw_own,
        qb_own,
        vb_own,
        outw_own,
        outb_own,
        expw_own,
        expb_own,
        shrw_own,
        shrb_own,
        logs_total,
    )


def solution(mesh):
    both = P(("img", "seq"))
    rows = P(("img", "seq"), None)
    return jax.shard_map(
        body,
        mesh=mesh,
        in_specs=(
            P("img", "seq", None),
            P("img", "seq", None),
            P("img", None),
            P("img", None),
            rows,
            both,
            rows,
            both,
            both,
            rows,
            both,
            rows,
            both,
            rows,
            both,
            P(),
        ),
        out_specs=(
            P("img", "seq", None),
            P("img", "seq", None),
            P("img", None),
            rows,
            both,
            rows,
            both,
            both,
            rows,
            both,
            rows,
            both,
            rows,
            both,
            P(),
        ),
        check_vma=False,
    )
```

time: 533 us -> 423 us (0.79)
  Pallas kernels: 338 us -> 300 us
  waiting for transfers between devices: 27.1 us -> 0 us
  matrix products: 75.3 us -> 58.5 us
  between operations: 15.4 us -> 1.82 us
  local copies, waits for them, and re-layouts: 39.8 us -> 31.5 us
    pallas_call x20 -> x13, Pallas kernels: 338 us -> 300 us  [the longest x11 209 us: exchange(): pl.pallas_call(kernel, out_shape=tuple(session.outs), in_specs=session.in...]
    all_gather x4 -> x0, waiting for transfers between devices: 26.4 us -> none  [the longest x1 26.3 us: body(): lax.all_gather(shrink_weight.astype(bf16), 'img', axis=0, tiled=True)]
    dot_general x4, matrix products: 26.3 us -> 17.3 us  [mm_nt(): lax.dot_general(a, b, (((1,), (1,)), ((), ())), preferred_element_type=f32)]
    unnamed x85 -> x80, local copies, waits for them, and re-layouts: 16.7 us -> 13.9 us
    dot_general x4 -> x5, matrix products: 20.5 us -> 18.3 us  [mm_tn(): lax.dot_general(a, b, (((0,), (0,)), ((), ())), preferred_element_type=f32)]
  transfers between devices with their start and end apart: 7 -> 0, of which waited for: 1 -> 0; matrix products, arithmetic and copies ran while one was open for 22% -> 0% of each run, Pallas kernels for 62% -> 0%
where the time goes in v2:
time: 423 us; the launch traced here: 418 us
  Pallas kernels  300 us (71%)
  matrix products  58.5 us (14%)
  local copies, waits for them, and re-layouts  31.5 us (7%)
  other arithmetic  26.2 us (6%)
    pallas_call x11, Pallas kernels, exchange(): pl.pallas_call(kernel, out_shape=tuple(session.outs), in_specs=session.in...  209 us
    pallas_call x1, Pallas kernels, attend_back(): pl.pallas_call(kernel, out_shape=tuple([jax.ShapeDtypeStruct(packed.shape...  54.2 us
    pallas_call x1, Pallas kernels, attend(): pl.pallas_call(kernel, out_shape=tuple([jax.ShapeDtypeStruct((images, row...  36.9 us
    dot_general x5, matrix products, mm(): return jnp.dot(a, b, preferred_element_type=f32)  21.5 us
    dot_general x5, matrix products, mm_tn(): lax.dot_general(a, b, (((0,), (0,)), ((), ())), preferred_element_type=f32)  18.3 us
    dot_general x4, matrix products, mm_nt(): lax.dot_general(a, b, (((1,), (1,)), ((), ())), preferred_element_type=f32)  17.3 us
    unnamed x80, local copies, waits for them, and re-layouts  13.9 us

profile of v2, /device:TPU:1, one launch (start us, length us, event | category | flops | bytes accessed | tf_op | source)
XLA Modules:
  0.0 418.2 jit_solution(14195593010533772396)
XLA Ops:
  9.4 1.5 convert_bitcast_fusion.refs_2_
  14.9 19.0 %exchange_1.1 = (bf16[4,32,3328]{2,1,0:T(8,128)(2,1)}, f32[8,8,128]{2,1,0:T(8,128)}, bf16[8,1,32,1024]{3,2,1,0:T(8,128)(2,1)}) custom-call(bf16[4,32,3328]{2,1,0:T(8,128)(2,1)} %pad_maximum_fusion.refs_0_, f32[8,8,128]{2,1,0:T(8,128)} %bitcast.259, bf16[1,32,1024]{2,1,0:T(8,128)(2,1)} %convert_bitcast_fusion.refs_2_), custom_call_target="tpu_custom_call" | custom-call | tf_op jit(solution)/shard_map/exchange_1/pallas_call | solution.py:245
  36.5 1.6 slice.154
  38.2 1.7 slice.157
  42.1 19.1 %exchange_2.1 = (f32[8,24,128]{2,1,0:T(8,128)}, bf16[8,4,32,1024]{3,2,1,0:T(8,128)(2,1)}) custom-call(f32[8,24,128]{2,1,0:T(8,128)} %reshape.458.refs_0_, bf16[8,32,1024]{2,1,0:T(8,128)(2,1)} %bitcast.239), custom_call_target="tpu_custom_call" | custom-call | tf_op jit(solution)/shard_map/exchange_2/pallas_call | solution.py:245
  62.7 5.2 %exchange_3.1 = f32[4,56,128]{2,1,0:T(8,128)} custom-call(f32[56,128]{1,0:T(8,128)} %fusion.27.refs_0_), custom_call_target="tpu_custom_call" | custom-call | tf_op jit(solution)/shard_map/exchange_3/pallas_call | solution.py:245
  71.9 27.1 %exchange_5.1 = (bf16[4,11,32,1024]{3,2,1,0:T(8,128)(2,1)}, bf16[8,4,32,768]{3,2,1,0:T(8,128)(2,1)}) custom-call(bf16[11,32,1024]{2,1,0:T(8,128)(2,1)} %bitcast.209, bf16[4,32,768]{2,1,0:T(8,128)(2,1)} %bitcast.231), custom_call_target="tpu_custom_call" | custom-call | tf_op jit(solution)/shard_map/exchange_5/pallas_call | solution.py:245
  99.0 6.7 %fusion.45.refs_0_ = f32[4,2,176,768]{3,2,1,0:T(8,128)} fusion(bf16[4,2,176,1024]{3,2,1,0:T(8,128)(2,1)} %bitcast.279, bf16[1024,768,1,1]{1,0,3,2:T(8,128)(2,1)} %bitcast.293), kind=kOutput, calls=%fused_computation.157 | convolution fusion | flops 2214592512 | bytes 8781824 | tf_op jit(solution)/shard_map/dot_general | solution.py:537
  105.7 36.9 %attend.1 = (bf16[2,176,1024]{2,1,0:T(8,128)(2,1)}, bf16[4,11,32,1024]{3,2,1,0:T(8,128)(2,1)}, bf16[8,4,32,1024]{3,2,1,0:T(8,128)(2,1)}) custom-call(f32[4,2,176,768]{3,2,1,0:T(8,128)} %fusion.45.refs_0_, f32[2,1,384]{2,1,0:T(1,128)} %pad_maximum_fusion.4.refs_1_.refs_2_, f32[2,1,128]{2,1,0:T(1,128)} %bitcast.271, ...), custom_call_target="tpu_custom_call" | custom-call | tf_op jit(solution)/shard_map/attend/pallas_call | solution.py:353
  142.6 2.7 convolution_add_fusion
  147.1 35.6 %exchange_7.1 = (bf16[4,11,32,1024]{3,2,1,0:T(8,128)(2,1)}, bf16[8,4,32,1024]{3,2,1,0:T(8,128)(2,1)}) custom-call(bf16[11,32,1024]{2,1,0:T(8,128)(2,1)} %bitcast.208, bf16[4,32,1024]{2,1,0:T(8,128)(2,1)} %bitcast.229), custom_call_target="tpu_custom_call" | custom-call | tf_op jit(solution)/shard_map/exchange_7/pallas_call | solution.py:245
  182.7 5.8 %fusion.46 = f32[1408,1024]{1,0:T(8,128)S(1)} fusion(bf16[1408,1024]{1,0:T(8,128)(2,1)} %bitcast.283, bf16[1024,1024]{1,0:T(8,128)(2,1)} %bitcast.289), kind=kOutput, calls=%fused_computation.158 | convolution fusion | flops 2952790016 | bytes 10747904 | tf_op jit(solution)/shard_map/dot_general | solution.py:537
  188.5 5.1 %convolution_convert_fusion.5 = bf16[1024,1024]{1,0:T(8,128)(2,1)} fusion(bf16[1408,1024]{1,0:T(8,128)(2,1)S(1)} %bitcast.281, f32[1408,1024]{1,0:T(8,128)S(1)} %fusion.46, f32[1024]{0:T(1024)S(1)} %dynamic-slice_bitcast_fusion), kind=kOutput, calls=%fused_computation.29 | convolution fusion | flops 2968256512 | bytes 10752000 | tf_op jit(solution)/shard_map/dot_general | solution.py:545
  193.6 6.9 %convert_reduce_fusion = (f32[1024]{0:T(1024)S(1)}, bf16[1408,1024]{1,0:T(8,128)(2,1)S(1)}) fusion(f32[1408,1024]{1,0:T(8,128)S(1)} %fusion.46, f32[1024]{0:T(1024)S(1)} %dynamic-slice_bitcast_fusion, bf16[1408,1024]{1,0:T(8,128)(2,1)S(1)} %bitcast.282, bf16[1024,1024]{1,0:T(8,128)(2,1)S(1)} %bitcast.291), kind=kOutput, calls=%fused_computation.9 | convolution fusion | flops 2985950208 | bytes 13639680 | tf_op jit(solution)/shard_map/dot_general | solution.py:541
  200.5 5.2 %convolution_convert_fusion.1 = bf16[1408,1024]{1,0:T(8,128)(2,1)} fusion(bf16[1024,1024]{1,0:T(8,128)(2,1)S(1)} %bitcast.292, f32[1408,1024]{1,0:T(8,128)S(1)} %fusion.46, f32[1024]{0:T(1024)S(1)} %dynamic-slice_bitcast_fusion), kind=kOutput, calls=%fused_computation.13 | convolution fusion | flops 2968649728 | bytes 10752000 | tf_op jit(solution)/shard_map/dot_general | solution.py:537
  205.7 4.7 %convolution_convert_fusion.4 = bf16[1024,1024]{1,0:T(8,128)(2,1)} fusion(bf16[1408,1024]{1,0:T(8,128)(2,1)S(1)} %bitcast.284, bf16[1408,1024]{1,0:T(8,128)(2,1)S(1)} %get-tuple-element.142), kind=kOutput, calls=%fused_computation.28 | convolution fusion | flops 2953838592 | bytes 7864320 | tf_op jit(solution)/shard_map/dot_general | solution.py:545
  210.4 4.5 %convolution_convert_fusion.2 = bf16[1408,1024]{1,0:T(8,128)(2,1)} fusion(bf16[1408,1024]{1,0:T(8,128)(2,1)S(1)} %get-tuple-element.142, bf16[1024,1024]{1,0:T(8,128)(2,1)S(1)} %bitcast.290), kind=kOutput, calls=%fused_computation.14 | convolution fusion | flops 2954231808 | bytes 7864320 | tf_op jit(solution)/shard_map/dot_general | solution.py:541
  214.9 33.6 %exchange_10.1 = (f32[11,32,1024]{2,1,0:T(8,128)}, f32[4,32,1024]{2,1,0:T(8,128)}) custom-call(bf16[4,11,32,1024]{3,2,1,0:T(8,128)(2,1)} %bitcast.207, bf16[8,4,32,1024]{3,2,1,0:T(8,128)(2,1)} %bitcast.213), custom_call_target="tpu_custom_call" | custom-call | tf_op jit(solution)/shard_map/exchange_10/pallas_call | solution.py:245
  248.5 1.9 fusion.37
  253.5 1.8 convolution_convert_fusion.7
  255.3 2.7 bitcast_convert_fusion
  257.9 54.2 %attend_back.1 = (bf16[4,2,176,768]{3,2,1,0:T(8,128)(2,1)}, f32[4,8,128]{2,1,0:T(8,128)}, bf16[4,32,1024]{2,1,0:T(8,128)(2,1)}, f32[11,32,1024]{2,1,0:T(8,128)}, bf16[8,32,1024]{2,1,0:T(8,128)(2,1)}) custom-call(f32[4,2,176,768]{3,2,1,0:T(8,128)} %fusion.45.refs_0_, bf16[2,176,1024]{2,1,0:T(8,128)(2,1)} %bitcast.237, ...), custom_call_target="tpu_custom_call" | custom-call | tf_op jit(solution)/shard_map/attend_back/pallas_call | solution.py:487
  312.2 5.6 %convolution_convert_fusion.6 = bf16[1024,768]{1,0:T(8,128)(2,1)} fusion(bf16[1408,1024]{1,0:T(8,128)(2,1)S(1)} %bitcast.280, bf16[1408,768]{1,0:T(8,128)(2,1)} %bitcast.285), kind=kOutput, calls=%fused_computation.30 | convolution fusion | flops 2215378944 | bytes 6619136 | tf_op jit(solution)/shard_map/dot_general | solution.py:545
  317.8 4.0 convolution_convert_fusion
  321.9 32.2 %exchange_12.1 = (f32[11,32,1024]{2,1,0:T(8,128)}, bf16[4,32,768]{2,1,0:T(8,128)(2,1)}, f32[1,32,1024]{2,1,0:T(8,128)}) custom-call(bf16[4,11,32,1024]{3,2,1,0:T(8,128)(2,1)} %bitcast.206, bf16[8,4,32,768]{3,2,1,0:T(8,128)(2,1)} %bitcast.222, bf16[8,1,32,1024]{3,2,1,0:T(8,128)(2,1)} %bitcast.238), custom_call_target="tpu_custom_call" | custom-call | tf_op jit(solution)/shard_map/exchange_12/pallas_call | solution.py:245
  354.7 1.6 copy.107
  356.6 2.1 fusion.15
  359.6 1.6 copy.108
  361.9 7.7 %exchange_13.1 = f32[4,48,128]{2,1,0:T(8,128)} custom-call(f32[4,48,128]{2,1,0:T(8,128)} %bitcast.249), custom_call_target="tpu_custom_call" | custom-call | tf_op jit(solution)/shard_map/exchange_13/pallas_call | solution.py:245
  371.9 8.1 %exchange_14.1 = f32[8,32,128]{2,1,0:T(8,128)} custom-call(f32[8,32,128]{2,1,0:T(8,128)} %bitcast.241), custom_call_target="tpu_custom_call" | custom-call | tf_op jit(solution)/shard_map/exchange_14/pallas_call | solution.py:245
  386.6 15.9 %exchange_15.1 = (bf16[4,32,3328]{2,1,0:T(8,128)(2,1)}, f32[4,16,128]{2,1,0:T(8,128)}, f32[8,8,128]{2,1,0:T(8,128)}) custom-call(bf16[4,32,3328]{2,1,0:T(8,128)(2,1)} %pad_maximum_fusion.1.refs_0_, f32[16,128]{1,0:T(8,128)} %pad_bitcast_fusion.4.refs_1_, f32[8,8,128]{2,1,0:T(8,128)} %bitcast.257), custom_call_target="tpu_custom_call" | custom-call | tf_op jit(solution)/shard_map/exchange_15/pallas_call | solution.py:245
  404.0 5.6 %exchange_16.1 = f32[4,8,8,128]{3,2,1,0:T(8,128)} custom-call(f32[8,8,128]{2,1,0:T(8,128)} %get-tuple-element.60.refs_0_), custom_call_target="tpu_custom_call" | custom-call | tf_op jit(solution)/shard_map/exchange_16/pallas_call | solution.py:245
  (219 shorter events, 48.5 us)
Async XLA Ops:
  0.6 11.7 %copy-start.7 = (f32[32,4096]{1,0:T(8,128)S(1)}, f32[32,4096]{1,0:T(8,128)}, u32[]{:S(2)}) copy-start(f32[32,4096]{1,0:T(8,128)} %param.27) | copy-start | bytes 1572868
  12.0 1.0 copy-start.8
  12.2 1.7 copy-start.4
  14.9 25.0 %copy-start.5 = (bf16[2,170,1024]{2,0,1:T(2,128)(2,1)S(1)}, bf16[2,170,1024]{2,0,1:T(2,128)(2,1)}, u32[]{:S(2)}) copy-start(bf16[2,170,1024]{2,0,1:T(2,128)(2,1)} %param.16) | copy-start | bytes 2088964
  38.2 2.5 copy-start.6
  182.7 5.8 %copy-start.16 = (bf16[4,11,32,1024]{3,2,1,0:T(8,128)(2,1)S(1)}, bf16[4,11,32,1024]{3,2,1,0:T(8,128)(2,1)}, u32[]{:S(2)}) copy-start(bf16[4,11,32,1024]{3,2,1,0:T(8,128)(2,1)} %get-tuple-element.48) | copy-start | bytes 8650756
  188.5 5.1 %copy-start.21 = (bf16[8,4,32,1024]{3,2,1,0:T(8,128)(2,1)S(1)}, bf16[8,4,32,1024]{3,2,1,0:T(8,128)(2,1)}, u32[]{:S(2)}) copy-start(bf16[8,4,32,1024]{3,2,1,0:T(8,128)(2,1)} %get-tuple-element.49) | copy-start | bytes 6291460
  200.5 5.2 %copy-start.17 = (bf16[4,11,32,1024]{3,2,1,0:T(8,128)(2,1)S(1)}, bf16[4,11,32,1024]{3,2,1,0:T(8,128)(2,1)}, u32[]{:S(2)}) copy-start(bf16[4,11,32,1024]{3,2,1,0:T(8,128)(2,1)} %get-tuple-element.50) | copy-start | bytes 8650756
  205.7 4.7 %copy-start.20 = (bf16[8,4,32,1024]{3,2,1,0:T(8,128)(2,1)S(1)}, bf16[8,4,32,1024]{3,2,1,0:T(8,128)(2,1)}, u32[]{:S(2)}) copy-start(bf16[8,4,32,1024]{3,2,1,0:T(8,128)(2,1)} %get-tuple-element.51) | copy-start | bytes 6291460
  248.5 1.9 copy-start
  251.9 1.6 copy-start.19
  253.5 1.8 copy-start.23
  257.9 54.2 %copy-start.15 = (bf16[4,11,32,1024]{3,2,1,0:T(8,128)(2,1)S(1)}, bf16[4,11,32,1024]{3,2,1,0:T(8,128)(2,1)}, u32[]{:S(2)}) copy-start(bf16[4,11,32,1024]{3,2,1,0:T(8,128)(2,1)} %get-tuple-element.44) | copy-start | bytes 8650756
  312.2 5.6 %copy-start.18 = (bf16[4,2,176,768]{3,2,1,0:T(8,128)(2,1)S(1)}, bf16[4,2,176,768]{3,2,1,0:T(8,128)(2,1)}, u32[]{:S(2)}) copy-start(bf16[4,2,176,768]{3,2,1,0:T(8,128)(2,1)} %get-tuple-element.54) | copy-start | bytes 6488068
  312.2 5.6 %copy-start.22 = (bf16[8,4,32,768]{3,2,1,0:T(8,128)(2,1)S(1)}, bf16[8,4,32,768]{3,2,1,0:T(8,128)(2,1)}, u32[]{:S(2)}) copy-start(bf16[8,4,32,768]{3,2,1,0:T(8,128)(2,1)} %get-tuple-element.45) | copy-start | bytes 4718596
  321.8 32.2 %copy-start.3 = (f32[11,32,1024]{2,1,0:T(8,128)S(1)}, f32[11,32,1024]{2,1,0:T(8,128)}, u32[]{:S(2)}) copy-start(f32[11,32,1024]{2,1,0:T(8,128)} %get-tuple-element.53) | copy-start | bytes 4325380
  354.4 1.9 copy-start.14
  356.5 2.3 copy-start.1
  370.6 15.0 %copy-start.10 = (bf16[4,32,1024]{2,1,0:T(8,128)(2,1)S(1)}, bf16[4,32,1024]{2,1,0:T(8,128)(2,1)}, u32[]{:S(2)}) copy-start(bf16[4,32,1024]{2,1,0:T(8,128)(2,1)} %get-tuple-element.59) | copy-start | bytes 786436
  370.6 15.0 %copy-start.11 = (bf16[4,32,768]{2,1,0:T(8,128)(2,1)S(1)}, bf16[4,32,768]{2,1,0:T(8,128)(2,1)}, u32[]{:S(2)}) copy-start(bf16[4,32,768]{2,1,0:T(8,128)(2,1)} %get-tuple-element.58) | copy-start | bytes 589828
  385.6 24.9 %copy-start.13 = (f32[2,1024]{1,0:T(2,128)S(1)}, f32[2,1024]{1,0:T(2,128)}, u32[]{:S(2)}) copy-start(f32[2,1024]{1,0:T(2,128)} %param.18) | copy-start | bytes 24580
  411.2 2.5 copy-start.2
  415.4 1.0 copy-start.12
  415.5 1.7 copy-start.9

commit v3 on v2

--- a/solution.py
+++ b/solution.py
@@ -1,4 +1,4 @@
-import functools
+from types import SimpleNamespace
 
 import jax
 import jax.numpy as jnp
@@ -19,6 +19,11 @@
     def __init__(self, ins, out, scratch, peers, count, bind, out_space=VM):
         self.ins, self.out, self.out_space = ins, out, out_space
         self.scratch, self.peers, self.count, self.bind = scratch, peers, count, bind
+        self.window = None
+
+    def during(self, low, high):
+        self.window = (low, high)
+        return self
 
 
 def remote(src, dst, send, recv, axis, peer):
@@ -35,89 +40,100 @@
     lax.fori_loop(low, high, once, 0)
 
 
-def direct(x, axis, everyone=False, src_rel=False, dst_rel=False):
+def direct_ops(axis, x_ref, out_ref, send, recv, everyone=False, src_rel=False, dst_rel=False):
     n = lax.axis_size(axis)
-
-    def bind(x_ref, out_ref, send, recv):
-        me = lax.axis_index(axis)
-
-        def copy(j):
-            src = x_ref if everyone else x_ref.at[j if src_rel else me ^ j]
-            return remote(src, out_ref.at[j if dst_rel else me], send.at[j], recv.at[j], axis, me ^ j)
-
-        def start():
-            for j in range(1, n):
-                copy(j).start()
-            out_ref[0 if dst_rel else me] = x_ref[...] if everyone else x_ref[0 if src_rel else me]
-
-        def finish():
-            for j in range(1, n):
-                copy(j).wait()
-
-        return start, None, finish
-
-    shape = ((n,) + x.shape) if everyone else x.shape
-    sems = pltpu.SemaphoreType.DMA((n,))
-    peers = [(axis, j) for j in range(1, n)]
-    return Plan([x], jax.ShapeDtypeStruct(shape, x.dtype), [sems, sems], peers, 0, bind)
+    me = lax.axis_index(axis)
+
+    def copy(j):
+        src = x_ref if everyone else x_ref.at[j if src_rel else me ^ j]
+        return remote(src, out_ref.at[j if dst_rel else me], send.at[j], recv.at[j], axis, me ^ j)
+
+    def start():
+        for j in range(1, n):
+            copy(j).start()
+        out_ref[0 if dst_rel else me] = x_ref[...] if everyone else x_ref[0 if src_rel else me]
+
+    def finish():
+        for j in range(1, n):
+            copy(j).wait()
+
+    return start, finish
 
 
 def two_level(axis, n):
     return [(axis, 1)] + [(axis, 2 * o) for o in range(1, n // 2)]
 
 
+def gather_ops(axis, rel, x_ref, out_ref, own, send, recv, inside=False):
+    n = lax.axis_size(axis)
+    outer = n // 2
+    chunks = x_ref.shape[0]
+    me = lax.axis_index(axis)
+
+    def place(sender, j, c):
+        block = j if rel else sender
+        return out_ref.at[c, block] if inside else out_ref.at[block, c]
+
+    def keep(c):
+        return pltpu.make_async_copy(x_ref.at[c], place(me, 0, c), own.at[c])
+
+    def push(j, c):
+        return remote(x_ref.at[c], place(me, j, c), send.at[j, c], recv.at[j, c], axis, me ^ j)
+
+    def hand(j, c):
+        far = me ^ j
+        return remote(place(far, j, c), place(far, j + 1, c), send.at[j + 1, c], recv.at[j + 1, c], axis, me ^ 1)
+
+    def start():
+        def first(c):
+            for o in range(1, outer):
+                push(2 * o, c).start()
+
+        def second(c):
+            push(1, c).start()
+            if own is not None:
+                keep(c).start()
+
+        each(0, chunks, first)
+        each(0, chunks, second)
+
+    def step(c):
+        for o in range(1, outer):
+            push(2 * o, c).wait_recv()
+            hand(2 * o, c).start()
+
+    def near():
+        each(0, chunks, lambda c: push(1, c).wait_recv())
+
+    def handed(o):
+        each(0, chunks, lambda c: hand(2 * o, c).wait_recv())
+
+    def sent():
+        def last(c):
+            for o in range(1, outer):
+                push(2 * o, c).wait_send()
+                hand(2 * o, c).wait_send()
+            push(1, c).wait_send()
+            if own is not None:
+                keep(c).wait()
+
+        each(0, chunks, last)
+
+    def finish():
+        near()
+        for o in range(1, outer):
+            handed(o)
+        sent()
+
+    return SimpleNamespace(start=start, step=step, near=near, handed=handed, sent=sent, finish=finish)
+
+
 def gather(x, axis, rel, inside=False):
     n = lax.axis_size(axis)
-    outer = n // 2
     chunks = x.shape[0]
 
     def bind(x_ref, out_ref, own, send, recv):
-        me = lax.axis_index(axis)
-
-        def place(sender, j, c):
-            block = j if rel else sender
-            return out_ref.at[c, block] if inside else out_ref.at[block, c]
-
-        def keep(c):
-            return pltpu.make_async_copy(x_ref.at[c], place(me, 0, c), own.at[c])
-
-        def push(j, c):
-            return remote(x_ref.at[c], place(me, j, c), send.at[j, c], recv.at[j, c], axis, me ^ j)
-
-        def hand(j, c):
-            far = me ^ j
-            return remote(
-                place(far, j, c), place(far, j + 1, c), send.at[j + 1, c], recv.at[j + 1, c], axis, me ^ 1
-            )
-
-        def start():
-            def first(c):
-                for o in range(1, outer):
-                    push(2 * o, c).start()
-
-            def second(c):
-                push(1, c).start()
-                keep(c).start()
-
-            each(0, chunks, first)
-            each(0, chunks, second)
-
-        def step(c):
-            for o in range(1, outer):
-                push(2 * o, c).wait_recv()
-                hand(2 * o, c).start()
-
-        def finish():
-            def last(c):
-                for o in range(1, outer):
-                    push(2 * o, c).wait_send()
-                    hand(2 * o, c).wait()
-                push(1, c).wait()
-                keep(c).wait()
-
-            each(0, chunks, last)
-
-        return start, step, finish
+        return gather_ops(axis, rel, x_ref, out_ref, own, send, recv, inside)
 
     sems = pltpu.SemaphoreType.DMA((n, chunks))
     shape = (chunks, n) + x.shape[1:] if inside else (n,) + x.shape
@@ -126,61 +142,79 @@
     return Plan([x], out, scratch, two_level(axis, n), chunks, bind, pl.ANY)
 
 
+def scatter_ops(axis, rel, x_ref, out_ref, near_buf, send_buf, far_buf, s1, r1, s2, r2, inside=False):
+    n = lax.axis_size(axis)
+    outer = n // 2
+    chunks = out_ref.shape[0]
+    me = lax.axis_index(axis)
+
+    def part(j, c):
+        block = j if rel else me ^ j
+        return x_ref.at[c, block] if inside else x_ref.at[block, c]
+
+    def near(o, c):
+        return remote(part(2 * o + 1, c), near_buf.at[o, c], s1.at[o, c], r1.at[o, c], axis, me ^ 1)
+
+    def far(o, c):
+        return remote(send_buf.at[o, c], far_buf.at[o, c], s2.at[o, c], r2.at[o, c], axis, me ^ (2 * o))
+
+    def start_outer():
+        def first(c):
+            for o in range(1, outer):
+                near(o, c).start()
+
+        each(0, chunks, first)
+
+    def start_inner():
+        each(0, chunks, lambda c: near(0, c).start())
+
+    def start():
+        start_outer()
+        start_inner()
+
+    def step(c):
+        for o in range(1, outer):
+            near(o, c).wait_recv()
+            total = part(2 * o, c)[...].astype(f32) + near_buf[o, c].astype(f32)
+            send_buf[o, c] = total.astype(send_buf.dtype)
+            far(o, c).start()
+
+    def finish():
+        def last(c):
+            near(0, c).wait_recv()
+            total = part(0, c)[...].astype(f32) + near_buf[0, c].astype(f32)
+            for o in range(1, outer):
+                far(o, c).wait_recv()
+                total = total + far_buf[o, c].astype(f32)
+            out_ref[c] = total.astype(out_ref.dtype)
+            for o in range(outer):
+                near(o, c).wait_send()
+            for o in range(1, outer):
+                far(o, c).wait_send()
+
+        each(0, chunks, last)
+
+    return SimpleNamespace(
+        start=start, start_outer=start_outer, start_inner=start_inner, step=step, finish=finish
+    )
+
+
+def scatter_scratch(n, inner, dtype):
+    half = VM((n // 2,) + inner, dtype)
+    sems = pltpu.SemaphoreType.DMA((n // 2, inner[0]))
+    return [half, half, half, sems, sems, sems, sems]
+
+
 def scatter_sum(x, axis, rel, dtype=jnp.float32, inside=False):
     n = lax.axis_size(axis)
-    outer = n // 2
     chunks = x.shape[0 if inside else 1]
-
-    def bind(x_ref, out_ref, near_buf, send_buf, far_buf, s1, r1, s2, r2):
-        me = lax.axis_index(axis)
-
-        def part(j, c):
-            block = j if rel else me ^ j
-            return x_ref.at[c, block] if inside else x_ref.at[block, c]
-
-        def near(o, c):
-            return remote(part(2 * o + 1, c), near_buf.at[o, c], s1.at[o, c], r1.at[o, c], axis, me ^ 1)
-
-        def far(o, c):
-            return remote(send_buf.at[o, c], far_buf.at[o, c], s2.at[o, c], r2.at[o, c], axis, me ^ (2 * o))
-
-        def start():
-            def first(c):
-                for o in range(1, outer):
-                    near(o, c).start()
-
-            each(0, chunks, first)
-            each(0, chunks, lambda c: near(0, c).start())
-
-        def step(c):
-            for o in range(1, outer):
-                near(o, c).wait_recv()
-                total = part(2 * o, c)[...].astype(f32) + near_buf[o, c].astype(f32)
-                send_buf[o, c] = total.astype(send_buf.dtype)
-                far(o, c).start()
-
-        def finish():
-            def last(c):
-                near(0, c).wait_recv()
-                total = part(0, c)[...].astype(f32) + near_buf[0, c].astype(f32)
-                for o in range(1, outer):
-                    far(o, c).wait_recv()
-                    total = total + far_buf[o, c].astype(f32)
-                out_ref[c] = total.astype(dtype)
-                for o in range(outer):
-                    near(o, c).wait_send()
-                for o in range(1, outer):
-                    far(o, c).wait_send()
-
-            each(0, chunks, last)
-
-        return start, step, finish
-
     inner = (chunks,) + x.shape[2:]
-    half = VM((outer,) + inner, x.dtype)
-    sems = pltpu.SemaphoreType.DMA((outer, chunks))
+
+    def bind(*refs):
+        return scatter_ops(axis, rel, *refs, inside=inside)
+
     out = jax.ShapeDtypeStruct(inner, dtype)
-    return Plan([x], out, [half, half, half, sems, sems, sems, sems], two_level(axis, n), chunks, bind)
+    return Plan([x], out, scatter_scratch(n, inner, x.dtype), two_level(axis, n), chunks, bind)
 
 
 class Session:
@@ -205,41 +239,278 @@
         for p, out in zip(self.plans, outs):
             mine = ins[at_in : at_in + len(p.ins)]
             own = scratch[at_scr : at_scr + len(p.scratch)]
-            self.bound.append((p.count,) + p.bind(*mine, out, *own))
+            self.bound.append((p.count, p.window, p.bind(*mine, out, *own)))
             at_in += len(p.ins)
             at_scr += len(p.scratch)
 
     def start(self):
-        for _, start, _, _ in self.bound:
-            start()
+        for _, _, ops in self.bound:
+            ops.start()
 
     def steps(self, i, total):
-        for count, _, step, _ in self.bound:
-            if count == total:
-                step(i)
-            elif count:
-                each((i * count) // total, ((i + 1) * count) // total, step)
+        for count, window, ops in self.bound:
+            low, high = window or (0, total)
+            span = high - low
+
+            def some(ops=ops, count=count, low=low, span=span):
+                if count == span:
+                    ops.step(i - low)
+                else:
+                    each(((i - low) * count) // span, ((i - low + 1) * count) // span, ops.step)
+
+            if not count:
+                continue
+            if span == total:
+                some()
+            else:
+                pl.when(jnp.logical_and(i >= low, i < high))(some)
 
     def finish(self):
-        for _, _, _, finish in self.bound:
-            finish()
+        for _, _, ops in self.bound:
+            ops.finish()
+
+
+def everyone_else(*axes):
+    return [(axis, j) for axis in axes for j in range(1, lax.axis_size(axis))]
+
+
+def pairs_of_sems(*axes):
+    return [pltpu.SemaphoreType.DMA((lax.axis_size(axis),)) for axis in axes for _ in range(2)]
 
 
 def params(cid):
     return pltpu.CompilerParams(collective_id=cid, has_side_effects=True, vmem_limit_bytes=LIMIT)
 
 
-def exchange(cid, *plans):
+def opening(cid, mod_cut, attn_cut, exp_cut, small, images, plans):
+    seq_n, own, mod_l = mod_cut.shape
+    img_n, rows, _ = small.shape
+    head = seq_n * images
+    tiles = mod_l // 128
+    slim = -(-tiles * images // 8) * 8
+    session = Session(plans)
+    session.peers = everyone_else("img", "seq")
+    ins, outs = 4 + len(session.ins), 6 + len(plans)
+
+    def kernel(*refs):
+        mod_ref, attn_ref, exp_ref, small_ref = refs[:4]
+        modo_ref, bias_ref, lhs_ref, modw_ref, attnw_ref, expw_ref = refs[ins : ins + 6]
+        small_all, part_buf, part_all, sum_buf = refs[ins + outs : ins + outs + 4]
+        sems = refs[ins + outs + 4 : ins + outs + 18]
+        session.greet()
+        small_go, small_end = direct_ops("img", small_ref, small_all, *sems[:2])
+        mod_go, mod_end = direct_ops("seq", mod_ref, modw_ref, *sems[2:4])
+        attn_go, attn_end = direct_ops("seq", attn_ref, attnw_ref, *sems[4:6])
+        exp_go, exp_end = direct_ops("seq", exp_ref, expw_ref, *sems[12:14])
+        session.bind(refs[4:ins], refs[ins + 6 : ins + outs], refs[ins + outs + 18 :])
+        small_go()
+        mod_go()
+        attn_go()
+        exp_go()
+        session.start()
+        part_buf[...] = jnp.zeros_like(part_buf)
+        small_end()
+        bias_go, bias_end = direct_ops("seq", small_all.at[:, head:], bias_ref, *sems[6:8], everyone=True)
+        bias_go()
+        for i in range(img_n):
+            for q in range(seq_n):
+                lhs_ref[q, i * images : (i + 1) * images] = small_all[i, q * images : (q + 1) * images]
+        mod_end()
+        part = jnp.zeros((img_n * images, mod_l), f32)
+        for q in range(seq_n):
+            part = part + dot(lhs_ref[q][:, :own].astype(bf16), modw_ref[q], ((1,), (0,)))
+        for i in range(img_n):
+            for t in range(tiles):
+                part_buf[i, t * images : (t + 1) * images] = part[
+                    i * images : (i + 1) * images, t * 128 : (t + 1) * 128
+                ]
+        part_go, part_end = direct_ops("img", part_buf, part_all, *sems[8:10])
+        part_go()
+        session.steps(0, 1)
+        part_end()
+        total = part_all[0]
+        for i in range(1, img_n):
+            total = total + part_all[i]
+        sum_buf[...] = total
+        sum_go, sum_end = direct_ops("seq", sum_buf, modo_ref, *sems[10:12], everyone=True)
+        sum_go()
+        bias_end()
+        sum_end()
+        attn_end()
+        exp_end()
+        session.finish()
+
+    full = pl.BlockSpec(memory_space=VM)
+    return pl.pallas_call(
+        kernel,
+        out_shape=tuple(
+            [
+                jax.ShapeDtypeStruct((seq_n, slim, 128), f32),
+                jax.ShapeDtypeStruct((seq_n, img_n, rows - head, 128), f32),
+                jax.ShapeDtypeStruct((seq_n, img_n * images, 128), f32),
+                jax.ShapeDtypeStruct(mod_cut.shape, bf16),
+                jax.ShapeDtypeStruct(attn_cut.shape, bf16),
+                jax.ShapeDtypeStruct(exp_cut.shape, bf16),
+            ]
+            + session.outs
+        ),
+        in_specs=[full] * 4 + session.in_specs,
+        out_specs=tuple([full] * 6 + session.out_specs),
+        scratch_shapes=[
+            VM(small.shape, f32),
+            VM((img_n, slim, 128), f32),
+            VM((img_n, slim, 128), f32),
+            VM((slim, 128), f32),
+        ]
+        + pairs_of_sems("img", "seq", "seq", "seq", "img", "seq", "seq")
+        + session.scratch,
+        compiler_params=params(cid),
+        name="opening",
+    )(mod_cut, attn_cut, exp_cut, small, *session.ins)
+
+
+def closing(cid, mine, expb, lhs, modw, back, images, pairs):
+    seq_n, own, mod_l = modw.shape
+    img_n = expb.shape[0]
+    rows = mine.shape[1]
+    head = seq_n * images
+    tiles = mod_l // 128
+    slim = -(-tiles * images // 8) * 8
+    share = img_n // seq_n
+    cut = back.shape[2]
+    dim_l = pairs * 128
+    width = dim_l * seq_n
+    hid_l = cut - 3 * dim_l
+    hid_o = hid_l // img_n
+    aligned = hid_o % 128 == 0
+    flat = -(-tiles // 8) * 8
+
+    def kernel(
+        mine_ref, expb_ref, lhs_ref, modw_ref, back_ref,
+        modw_own, attn_own, exp_own, bias_ref, modb_ref, cond_ref,
+        seen, block, got, dd, mw_send, mw_recv, mb_send, gs_send, gs_all, gs_seen, back_all, *sems
+    ):
+        barrier = Session([], everyone_else("img", "seq"))
+        barrier.greet()
+        mine_go, mine_end = direct_ops("seq", mine_ref, seen, *sems[:2])
+        back_go, back_end = direct_ops("seq", back_ref, back_all, *sems[2:4])
+        mine_go()
+        back_go()
+        block[...] = jnp.zeros_like(block)
+        gs_send[...] = jnp.zeros_like(gs_send)
+        mb_send[...] = jnp.zeros_like(mb_send)
+        mine_end()
+        total = seen[0]
+        for q in range(1, seq_n):
+            total = total + seen[q]
+        at = slim + 2 * img_n
+        for i in range(img_n):
+            block[i, :slim] = total[:slim]
+            block[i, slim : slim + 1] = total[slim + i : slim + i + 1]
+            block[i, slim + 1 : slim + 2] = total[slim + img_n + i : slim + img_n + i + 1]
+            row = at + 8 + i % share
+            block[i, slim + 2 : slim + 3] = seen[i // share, row : row + 1]
+            block[i, slim + 3 : slim + 4] = seen[i // share, row + share : row + share + 1]
+            block[i, slim + 4 : slim + 5] = expb_ref[i : i + 1]
+            block[i, slim + 5 : slim + 6] = total[at : at + 1]
+        img_go, img_end = direct_ops("img", block, got, *sems[4:6])
+        img_go()
+        back_end()
+        for q in range(seq_n):
+            for p in range(pairs):
+                for k in range(3):
+                    to = k * width + q * dim_l + p * 128
+                    at_c = p * 384 + k * 128
+                    attn_own[:, to : to + 128] = back_all[q, :, at_c : at_c + 128].astype(f32)
+            if aligned:
+                for i in range(img_n):
+                    to = (i * seq_n + q) * hid_o
+                    at_c = 3 * dim_l + i * hid_o
+                    exp_own[:, to : to + hid_o] = back_all[q, :, at_c : at_c + hid_o].astype(f32)
+            else:
+                exp_own[:, q * hid_l : (q + 1) * hid_l] = back_all[q, :, 3 * dim_l :].astype(f32)
+        img_end()
+        sums = got[0]
+        for i in range(1, img_n):
+            sums = sums + got[i]
+        bias_ref[...] = sums[slim:]
+        for t in range(tiles):
+            mb_send[t : t + 1] = jnp.sum(sums[t * images : (t + 1) * images], axis=0, keepdims=True)
+            for i in range(img_n):
+                dd[i * images : (i + 1) * images, t * 128 : (t + 1) * 128] = got[i, t * images : (t + 1) * images]
+        grad = dd[...]
+        high = grad.astype(bf16)
+        low = (grad - high.astype(f32)).astype(bf16)
+        for q in range(seq_n):
+            out = dot(high, modw_ref[q], ((1,), (1,))) + dot(low, modw_ref[q], ((1,), (1,)))
+            for i in range(img_n):
+                gs_send[i, q * images : (q + 1) * images, :own] = out[i * images : (i + 1) * images]
+        gs_go, gs_end = direct_ops("img", gs_send, gs_all, *sems[6:8])
+        gs_go()
+        for q in range(seq_n):
+            mw_send[q] = dot(lhs_ref[q][:, :own].astype(bf16), high, ((0,), (0,))).astype(bf16)
+        mb_go, mb_end = direct_ops("seq", mb_send, modb_ref, *sems[10:12], everyone=True)
+        mb_go()
+        gs_end()
+        all_go, all_end = direct_ops("seq", gs_all, gs_seen, *sems[12:14], everyone=True)
+        all_go()
+        mw_go, mw_end = direct_ops("seq", mw_send, mw_recv, *sems[8:10])
+        mw_go()
+        mb_end()
+        all_end()
+        out = gs_seen[0]
+        for q in range(1, seq_n):
+            out = out + gs_seen[q]
+        cond_ref[...] = out
+        mw_end()
+        for q in range(seq_n):
+            modw_own[:, q * mod_l : (q + 1) * mod_l] = mw_recv[q].astype(f32)
+
+    full = pl.BlockSpec(memory_space=VM)
+    got = pl.pallas_call(
+        kernel,
+        out_shape=(
+            jax.ShapeDtypeStruct((own, mod_l * seq_n), f32),
+            jax.ShapeDtypeStruct((own, 3 * width), f32),
+            jax.ShapeDtypeStruct((own, hid_l * seq_n), f32),
+            jax.ShapeDtypeStruct((8, 128), f32),
+            jax.ShapeDtypeStruct((seq_n, flat, 128), f32),
+            jax.ShapeDtypeStruct((img_n, head, 128), f32),
+        ),
+        in_specs=[full] * 5,
+        out_specs=(full,) * 6,
+        scratch_shapes=[
+            VM((seq_n, rows, 128), f32),
+            VM((img_n, slim + 8, 128), f32),
+            VM((img_n, slim + 8, 128), f32),
+            VM((img_n * images, mod_l), f32),
+            VM((seq_n, own, mod_l), bf16),
+            VM((seq_n, own, mod_l), bf16),
+            VM((flat, 128), f32),
+            VM((img_n, head, 128), f32),
+            VM((img_n, head, 128), f32),
+            VM((seq_n, img_n, head, 128), f32),
+            VM(back.shape, bf16),
+        ]
+        + pairs_of_sems("seq", "seq", "img", "img", "seq", "seq", "seq"),
+        compiler_params=params(cid),
+        name="closing",
+    )(mine, expb, lhs, modw, back)
+    got = list(got)
+    if not aligned:
+        got[2] = got[2].reshape(own, seq_n, img_n, hid_o).transpose(0, 2, 1, 3).reshape(own, hid_l * seq_n)
+    return got
+
+
+def exchange(cid, turns, *plans):
     session = Session(plans)
     ins, outs = len(session.ins), len(plans)
-    turns = max(p.count for p in plans)
 
     def kernel(*refs):
         session.greet()
         session.bind(refs[:ins], refs[ins : ins + outs], refs[ins + outs :])
         session.start()
-        if turns:
-            each(0, turns, lambda i: session.steps(i, turns))
+        each(0, turns, lambda i: session.steps(i, turns))
         session.finish()
 
     got = pl.pallas_call(
@@ -508,6 +779,172 @@
     )(packed, d_out, bias, scale, sid_k, sid_q, *session.ins)
 
 
+def gelu_both(x):
+    root = 0.7978845608028654
+    square = x * x
+    bent = jnp.tanh(root * x * (1.0 + 0.044715 * square))
+    half = 0.5 * (1.0 + bent)
+    slope = half + 0.5 * x * (1.0 - bent * bent) * (root * (1.0 + 3 * 0.044715 * square))
+    return x * half, slope
+
+
+def feed_forward(cid, mlp_input, grad_parts, shr_own, exp_w, e_bias):
+    seq_n, img_n = lax.axis_size("seq"), lax.axis_size("img")
+    outer = seq_n // 2
+    chunks, size, width = mlp_input.shape
+    rows = chunks * size
+    hid_l = exp_w.shape[1]
+    images = len(grad_parts)
+    rows_p = rows // images
+    w_chunks, w_size, _ = shr_own.shape
+    hid_o = w_chunks * w_size
+    tile = 256
+    blocks_per_tile = tile // hid_o
+    session = Session([], two_level("seq", seq_n) + two_level("img", img_n))
+
+    def kernel(x_ref, *refs):
+        df_refs = refs[:images]
+        shr_ref, exp_ref, eb_ref, dh2_ref, dshr_own, f_ref, dexp_ref, expb_ref = refs[images : images + 8]
+        h2, df, shr, act, slope, dshr, dh2, df_sem, hs, hr, ss, sr, sk, *more = refs[images + 8 :]
+        session.greet()
+        h2_in = gather_ops("seq", True, x_ref, h2, None, hs, hr)
+        shr_in = gather_ops("img", False, shr_ref, shr, sk, ss, sr)
+        dh2_out = scatter_ops("seq", True, dh2, dh2_ref, *more[:7])
+        dshr_out = scatter_ops("img", False, dshr, dshr_own, *more[7:14])
+        h2_in.start()
+        shr_in.start()
+        loads = [pltpu.make_async_copy(ref, df.at[:, g], df_sem.at[g]) for g, ref in enumerate(df_refs)]
+        for load in loads:
+            load.start()
+        h2[0] = x_ref[...]
+        expb_ref[...] = jnp.zeros_like(expb_ref)
+
+        def columns(t):
+            return lanes(t * tile, tile)
+
+        def expand(j):
+            def run(t):
+                u = dot(h2[j].reshape(rows, width), exp_ref[:, columns(t)], ((1,), (0,))) + eb_ref[:, columns(t)]
+                value, grad = gelu_both(u)
+                act[j, :, columns(t)] = value.astype(bf16)
+                slope[j, :, columns(t)] = grad.astype(bf16)
+
+            each(0, hid_l // tile, run)
+
+        def back_act(j):
+            def run(t):
+                weight = shr[pl.ds(t * blocks_per_tile, blocks_per_tile)].reshape(tile, width)
+                grad = dot(df[j].reshape(rows, width), weight, ((1,), (1,)))
+                grad = (slope[j, :, columns(t)].astype(f32) * grad).astype(bf16)
+                slope[j, :, columns(t)] = grad
+                expb_ref[:, columns(t)] += jnp.sum(grad.astype(f32), axis=0, keepdims=True)
+
+            each(0, hid_l // tile, run)
+
+        def back_input(j):
+            def run(t):
+                weight = exp_ref[pl.ds(pl.multiple_of(t * tile, tile), tile), :]
+                part = dot(slope[j], weight, ((1,), (1,)))
+                dh2[j, :, :, columns(t)] = part.astype(bf16).reshape(chunks, size, tile)
+
+            each(0, width // tile, run)
+
+        def shrink(j):
+            def run(t):
+                weight = shr[:, :, :, columns(t)].reshape(hid_l, tile)
+                part = dot(act[j], weight, ((1,), (0,)))
+                f_ref[j, :, :, columns(t)] = part.astype(bf16).reshape(chunks, size, tile)
+
+            each(0, width // tile, run)
+
+        def shrink_grad(t):
+            left = act[:, :, columns(t)].reshape(seq_n * rows, tile)
+            part = dot(left, df[...].reshape(seq_n * rows, width), ((0,), (0,)))
+            part = part.astype(bf16).reshape(blocks_per_tile, w_chunks, w_size, width)
+            dshr[pl.ds(t * blocks_per_tile, blocks_per_tile)] = part
+
+        def expand_grad(t):
+            left = h2[:, :, :, columns(t)].reshape(seq_n * rows, tile)
+            part = dot(left, slope[...].reshape(seq_n * rows, hid_l), ((0,), (0,)))
+            dexp_ref[pl.ds(pl.multiple_of(t * tile, tile), tile), :] = part.astype(bf16)
+
+        expand(0)
+        h2_in.near()
+        expand(1)
+        half = chunks // 2
+        each(0, half, h2_in.step)
+        each(0, w_chunks // 2, shr_in.step)
+        each(half, chunks, h2_in.step)
+        for o in range(1, outer):
+            expand(2 * o)
+        each(w_chunks // 2, w_chunks, shr_in.step)
+        for o in range(1, outer):
+            h2_in.handed(o)
+            expand(2 * o + 1)
+        for load in loads:
+            load.wait()
+        each(0, hid_l // tile, shrink_grad)
+        shr_in.near()
+        for o in range(1, img_n // 2):
+            shr_in.handed(o)
+        shr_in.sent()
+        dshr_out.start()
+        for o in range(1, outer):
+            for j in (2 * o + 1, 2 * o):
+                back_act(j)
+                back_input(j)
+        dh2_out.start_outer()
+        each(0, chunks, dh2_out.step)
+        each(0, w_chunks // 2, dshr_out.step)
+        for j in (1, 0):
+            back_act(j)
+            back_input(j)
+        dh2_out.start_inner()
+        each(w_chunks // 2, w_chunks, dshr_out.step)
+        h2_in.sent()
+        for j in range(seq_n):
+            shrink(j)
+        each(0, width // tile, expand_grad)
+        dh2_out.finish()
+        dshr_out.finish()
+
+    full = pl.BlockSpec(memory_space=VM)
+    any_space = pl.BlockSpec(memory_space=pl.ANY)
+    seq_sems = pltpu.SemaphoreType.DMA((seq_n, chunks))
+    img_sems = pltpu.SemaphoreType.DMA((img_n, w_chunks))
+    return pl.pallas_call(
+        kernel,
+        out_shape=(
+            jax.ShapeDtypeStruct(mlp_input.shape, f32),
+            jax.ShapeDtypeStruct(shr_own.shape, f32),
+            jax.ShapeDtypeStruct((seq_n,) + mlp_input.shape, bf16),
+            jax.ShapeDtypeStruct(exp_w.shape, bf16),
+            jax.ShapeDtypeStruct((1, hid_l), f32),
+        ),
+        in_specs=[full] + [any_space] * images + [full] * 3,
+        out_specs=(full,) * 5,
+        scratch_shapes=[
+            VM((seq_n,) + mlp_input.shape, bf16),
+            VM((seq_n, images, rows_p, width), bf16),
+            VM((img_n,) + shr_own.shape, bf16),
+            VM((seq_n, rows, hid_l), bf16),
+            VM((seq_n, rows, hid_l), bf16),
+            VM((img_n,) + shr_own.shape, bf16),
+            VM((seq_n,) + mlp_input.shape, bf16),
+            pltpu.SemaphoreType.DMA((images,)),
+            seq_sems,
+            seq_sems,
+            img_sems,
+            img_sems,
+            pltpu.SemaphoreType.DMA((w_chunks,)),
+        ]
+        + scatter_scratch(seq_n, mlp_input.shape, bf16)
+        + scatter_scratch(img_n, shr_own.shape, bf16),
+        compiler_params=params(cid),
+        name="feed_forward",
+    )(mlp_input, *grad_parts, shr_own, exp_w, e_bias)
+
+
 def normalize(values):
     centered = values - jnp.mean(values, axis=-1, keepdims=True)
     return centered * lax.rsqrt(jnp.mean(centered * centered, axis=-1, keepdims=True) + 1e-06)
@@ -515,22 +952,12 @@
 
 def norm_back(values, grad_rows):
     return jax.vjp(normalize, values)[1](grad_rows)[0]
-
-
-def gelu_tanh(values):
-    return jax.nn.gelu(values, approximate=True)
 
 
 def pad_to(x, size, axis):
     widths = [(0, 0)] * x.ndim
     widths[axis] = (0, size - x.shape[axis])
     return jnp.pad(x, widths)
-
-
-def flat_rows(vector):
-    size = -(-vector.shape[-1] // 1024) * 1024
-    vector = pad_to(vector, size, vector.ndim - 1)
-    return vector.reshape(vector.shape[:-1] + (size // 128, 128))
 
 
 def mm(a, b):
@@ -600,43 +1027,38 @@
     mod_cut = mod_weight.astype(bf16).reshape(own, seq_n, mod_l).transpose(1, 0, 2)
     silu_cond = jax.nn.silu(condition).astype(bf16).astype(f32)
     small_bias = jnp.concatenate([query_bias, value_bias, out_bias, shrink_bias, expand_bias, mod_bias])
-    small_bias = small_bias.astype(bf16).astype(f32)
+    small_bias = lax.reduce_precision(small_bias, 8, 7)
     bias_n = small_bias.shape[0]
-    cond_cut = silu_cond.reshape(images, img_n, blk).transpose(1, 0, 2).reshape(img_n, images * blk)
-    small = jnp.concatenate([cond_cut, jnp.broadcast_to(small_bias[None], (img_n, bias_n))], axis=1)
-    cut, small_all, out_img = exchange(
+    bias_rows = -(-bias_n // 1024) * 8
+    small_bias = pad_to(small_bias, bias_rows * 128, 0).reshape(1, bias_rows, 128)
+    cond_cut = silu_cond.reshape(images, img_n, seq_n, own).transpose(1, 2, 0, 3).reshape(img_n, seq_n * images, own)
+    small = jnp.concatenate(
+        [pad_to(cond_cut, 128, 2), jnp.broadcast_to(small_bias, (img_n, bias_rows, 128))], axis=1
+    )
+    mod_all, bias_all, cond_rows, modw_cut, attn_b, exp_b, out_img = opening(
         1,
-        direct(jnp.concatenate([mod_cut, attn_cut, exp_cut], axis=2), "seq"),
-        direct(flat_rows(small), "img"),
-        gather(out_weight.astype(bf16)[None], "img", False),
+        mod_cut,
+        attn_cut,
+        exp_cut,
+        small,
+        images,
+        [gather(out_weight.astype(bf16)[None], "img", False)],
     )
     out_img = out_img.reshape(img_n, own, width)
-    cut = cut.reshape(blk, mod_l + 3 * dim_l + hid_l)
-    modw_cut = cut[:, :mod_l]
-    attn_b = cut[:, mod_l : mod_l + 3 * dim_l]
-    exp_b = cut[:, mod_l + 3 * dim_l :]
+    attn_b = attn_b.reshape(blk, 3 * dim_l)
+    exp_b = exp_b.reshape(blk, hid_l)
 
     def weight_chunks(x):
         step = max(blk // 4, 8)
         return x.reshape(x.shape[:-2] + (blk // step, step, x.shape[-1]))
 
     def hidden_chunks(x):
-        step = max(hid_o // 4, 8)
+        step = max(hid_o // 4, 16)
         return x.reshape(x.shape[:-2] + (hid_o // step, step, x.shape[-1]))
 
-    small_all = small_all.reshape(img_n, -1)
-    cond_mine = small_all[:, : images * blk].reshape(img_n * images, blk).astype(bf16)
-    bias_col = small_all[:, images * blk : images * blk + bias_n]
-    mod_part = mm(cond_mine, modw_cut).reshape(img_n, images * mod_l)
-    mod_img, out_w = exchange(2, direct(flat_rows(mod_part), "img"), gather(out_img, "seq", False, True))
-    mod_img = jnp.sum(mod_img, axis=0)
-    out_w = out_w.reshape(width, width)
-    mod_img = mod_img.reshape(-1)[: images * mod_l]
-    mod_send = flat_rows(jnp.concatenate([mod_img, bias_col.reshape(-1)]))
-    mod_all = exchange(3, direct(mod_send, "seq", everyone=True)).reshape(seq_n, -1)
-    modulation = mod_all[:, : images * mod_l].reshape(seq_n, images, mod_l).transpose(1, 0, 2)
-    bias_all = mod_all[:, images * mod_l : images * mod_l + img_n * bias_n]
-    bias_all = bias_all.reshape(seq_n, img_n, bias_n).transpose(1, 0, 2)
+    tiles = mod_l // 128
+    modulation = mod_all[:, : tiles * images].reshape(seq_n, tiles, images, 128).transpose(2, 0, 1, 3)
+    bias_all = bias_all.reshape(seq_n, img_n, bias_rows * 128)[:, :, :bias_n].transpose(1, 0, 2)
     q_bias = bias_all[:, :, :own].reshape(width)
     v_bias = bias_all[:, :, own : 2 * own].reshape(width)
     o_bias = bias_all[:, :, 2 * own : 3 * own].reshape(width)
@@ -671,52 +1093,55 @@
 
     normed_in = normalize(resid_in)
     attn_input = (normed_in * (1.0 + scale_attn) + shift_attn).astype(bf16)
-    h1, attn_w = exchange(5, gather(chunked(attn_input), "seq", True), gather(weight_chunks(attn_b), "img", False))
+    grad_shrunk = (grad_out * gain_mlp).astype(bf16)
+    grad_chunks = grad_shrunk.reshape(images, rows_p // 16, 16, width)
+    turns = 16
+    first = images // 2
+    h1, attn_w, *df_first = exchange(
+        5,
+        turns,
+        gather(chunked(attn_input), "seq", True).during(0, turns * 2 // 3),
+        gather(weight_chunks(attn_b), "img", False),
+        *[gather(grad_chunks[g], "seq", True).during(turns * 2 // 3, turns) for g in range(first)],
+    )
     h1 = h1.reshape(all_rows, width)
     attn_w = attn_w.reshape(width, 3 * dim_l)
     packed = mm(h1, attn_w).reshape(seq_n, images, rows_p, 3 * dim_l)
-    grad_shrunk = (grad_out * gain_mlp).astype(bf16)
-    context_low, df, exp_w = attend(
+    later = images * pairs // 2
+    context_low, out_w, exp_w, *df_second = attend(
         6,
         packed,
         pair_bias,
         pair_scale,
         sid_k,
         sid_q,
-        [gather(chunked(grad_shrunk), "seq", True), gather(weight_chunks(exp_b), "img", False)],
+        [
+            gather(out_img, "seq", False, True).during(0, later),
+            gather(weight_chunks(exp_b), "img", False),
+        ]
+        + [gather(grad_chunks[g], "seq", True).during(later, 2 * later) for g in range(first, images)],
     )
     context_low = context_low.reshape(local, width)
-    df = df.reshape(all_rows, width)
+    out_w = out_w.reshape(width, width)
     exp_w = exp_w.reshape(width, hid_l)
     attn_out = (mm(context_low, out_w) + o_bias).reshape(images, rows_p, width)
     resid_mid = resid_in + gain_attn * attn_out
     normed_mid = normalize(resid_mid)
     mlp_input = (normed_mid * (1.0 + scale_mlp) + shift_mlp).astype(bf16)
-    h2, shr_w = exchange(
+    df_parts = [x.reshape(seq_n, rows_p, width) for x in df_first + df_second]
+    shrb_part = jnp.sum(grad_shrunk.astype(f32), axis=(0, 1))
+    grad_mlp_input, shrw_own, shrunk_part, expw_part, expb_part = feed_forward(
         7,
-        gather(chunked(mlp_input), "seq", True),
-        gather(hidden_chunks(shrink_weight.astype(bf16)), "img", False),
-    )
-    h2 = h2.reshape(all_rows, width)
-    shr_w = shr_w.reshape(hid_l, width)
-    expanded = mm(h2, exp_w) + e_bias
-    activated = gelu_tanh(expanded).astype(bf16)
-
-    shrb_part = jnp.sum(grad_shrunk.astype(f32), axis=(0, 1))
-    grad_act = mm_nt(df, shr_w)
-    grad_exp = jax.vjp(gelu_tanh, expanded)[1](grad_act)[0].astype(bf16)
-    grad_mlp_part = mm_nt(grad_exp, exp_w).astype(bf16).reshape(seq_n, images, rows_p, width)
-    shrw_part = mm_tn(activated, df).astype(bf16).reshape(img_n, hid_o, width)
-    grad_mlp_input, shrw_own = exchange(
-        10,
-        scatter_sum(chunked(grad_mlp_part), "seq", True),
-        scatter_sum(hidden_chunks(shrw_part), "img", False),
+        chunked(mlp_input),
+        df_parts,
+        hidden_chunks(shrink_weight.astype(bf16)),
+        exp_w,
+        e_bias.reshape(1, hid_l),
     )
     grad_mlp_input = grad_mlp_input.reshape(images, rows_p, width)
     shrw_own = shrw_own.reshape(hid_o, width)
-    expb_part = jnp.sum(grad_exp.astype(f32), axis=0)
-    expw_part = mm_tn(h2, grad_exp).astype(bf16).reshape(img_n, blk, hid_l)
-    shrunk_part = mm(activated, shr_w).astype(bf16).reshape(seq_n, images, rows_p, width)
+    expb_part = expb_part.reshape(hid_l)
+    expw_part = expw_part.reshape(img_n, blk, hid_l)
 
     grad_scale_mlp = jnp.sum(grad_mlp_input * normed_mid, axis=1)
     grad_shift_mlp = jnp.sum(grad_mlp_input, axis=1)
@@ -738,7 +1163,7 @@
         sid_q,
         [
             scatter_sum(weight_chunks(expw_part), "img", False, bf16),
-            scatter_sum(chunked(shrunk_part), "seq", True),
+            scatter_sum(shrunk_part, "seq", True),
             scatter_sum(outw_part, "seq", False, bf16, True),
         ],
     )
@@ -754,6 +1179,7 @@
     attnw_part = mm_tn(h1, grad_packed).astype(bf16)
     grad_attn_input, attnw_blk, outw_own = exchange(
         12,
+        local // 32,
         scatter_sum(chunked(grad_in_part), "seq", True),
         scatter_sum(weight_chunks(attnw_part.reshape(img_n, blk, 3 * dim_l)), "img", False, bf16),
         scatter_sum(outw_blk.reshape(img_n, 1, own, width), "img", False),
@@ -769,82 +1195,41 @@
         [grad_gain_attn, grad_gain_mlp, grad_scale_attn, grad_scale_mlp, grad_shift_attn, grad_shift_mlp],
         axis=-1,
     )
-    grad_mod = grad_mod.reshape(images, seq_n, mod_l).transpose(1, 0, 2).reshape(seq_n, images * mod_l)
-    mine = jnp.concatenate([shrb_part, outb_part, qb_part, vb_part, logs_part])
-    mine = jnp.concatenate([grad_mod, jnp.broadcast_to(mine[None], (seq_n, mine.shape[0]))], axis=1)
-    seen = exchange(13, direct(flat_rows(mine), "seq")).reshape(seq_n, -1)
-    at = images * mod_l
-    grad_mod = jnp.sum(seen[:, :at], axis=0)
-    shrb_sum = jnp.sum(seen[:, at : at + width], axis=0).reshape(img_n, seq_n, own)
-    at += width
-    outb_sum = jnp.sum(seen[:, at : at + width], axis=0).reshape(img_n, seq_n, own)
-    at += width
-    qb_sum = seen[:, at : at + dim_l].reshape(img_n, seq_n, own)
-    at += dim_l
-    vb_sum = seen[:, at : at + dim_l].reshape(img_n, seq_n, own)
-    at += dim_l
-    logs_sum = seen[:, at : at + heads // seq_n].reshape(heads)
-    bias_mine = jnp.stack([shrb_sum, outb_sum, qb_sum, vb_sum], axis=2)
-    bias_mine = lax.dynamic_slice_in_dim(bias_mine, seq_i, 1, 1).reshape(img_n, 4 * own)
-    block = jnp.concatenate(
+    grad_mod = grad_mod.reshape(images, seq_n, tiles, 128).transpose(1, 2, 0, 3).reshape(seq_n, tiles * images, 128)
+    grad_mod = pad_to(grad_mod, -(-tiles * images // 8) * 8, 1)
+
+    def lined(vector, count):
+        return pad_to(vector.reshape(count, -1), 128, 1)
+
+    heads_l = heads // seq_n
+    logs_row = lax.dynamic_update_slice_in_dim(jnp.zeros((128,), f32), logs_part, seq_i * heads_l, 0)
+    bias_mine = jnp.concatenate(
         [
-            jnp.broadcast_to(grad_mod[None], (img_n, images * mod_l)),
-            bias_mine,
-            expb_part.reshape(img_n, hid_o),
-            jnp.broadcast_to(logs_sum[None], (img_n, heads)),
-        ],
-        axis=1,
-    )
-    got = exchange(14, direct(flat_rows(block), "img")).reshape(img_n, -1)
-    at = images * mod_l
-    grad_mod_all = got[:, :at].reshape(img_n * images, mod_l)
-    tail = jnp.sum(got[:, at:], axis=0)
-    shrb_own = tail[:own]
-    outb_own = tail[own : 2 * own]
-    qb_own = tail[2 * own : 3 * own]
-    vb_own = tail[3 * own : 4 * own]
-    expb_own = tail[4 * own : 4 * own + hid_o]
-    logs_total = tail[4 * own + hid_o : 4 * own + hid_o + heads]
-
-    modw_blk = mm_tn(cond_mine, grad_mod_all.astype(bf16))
-    grad_silu = lax.dot_general(
-        grad_mod_all, modw_cut.astype(f32), (((1,), (1,)), ((), ())), precision=HIGH
-    )
-    modb_all = jnp.sum(grad_mod_all, axis=0)
+            lined(shrb_part, img_n),
+            lined(outb_part, img_n),
+            pad_to(logs_row[None], 8, 0),
+            lined(qb_part, img_n // seq_n),
+            lined(vb_part, img_n // seq_n),
+        ]
+    )
+    bias_mine = pad_to(bias_mine, -(-bias_mine.shape[0] // 8) * 8, 0)
+    mine = jnp.concatenate([grad_mod, jnp.broadcast_to(bias_mine[None], (seq_n,) + bias_mine.shape)], axis=1)
     back_cut = jnp.concatenate(
-        [
-            modw_blk.astype(bf16).reshape(seq_n, own, mod_l),
-            attnw_blk.reshape(seq_n, own, 3 * dim_l),
-            expw_blk.reshape(seq_n, own, hid_l),
-        ],
-        axis=2,
-    )
-    back_cut, modb_all, grad_silu = exchange(
-        15,
-        direct(back_cut, "seq"),
-        direct(flat_rows(modb_all), "seq", everyone=True),
-        direct(flat_rows(grad_silu.reshape(img_n, images * blk)), "img"),
-    )
-    grad_silu = exchange(16, direct(grad_silu, "seq", everyone=True)).reshape(seq_n, img_n, -1)
-    grad_silu = jnp.sum(grad_silu[:, :, : images * blk], axis=0).reshape(img_n, images, blk)
-    grad_silu = grad_silu.transpose(1, 0, 2).reshape(images, width)
+        [attnw_blk.reshape(seq_n, own, 3 * dim_l), expw_blk.reshape(seq_n, own, hid_l)], axis=2
+    )
+    modw_own, attnw_own, expw_own, bias_own, modb_all, cond_sum = closing(
+        13, mine, lined(expb_part, img_n), cond_rows, modw_cut, back_cut, images, pairs
+    )
+
+    def part_of(row):
+        return lax.dynamic_slice_in_dim(bias_own[row], seq_i * own, own, 0)
+
+    shrb_own, outb_own, qb_own, vb_own = part_of(0), part_of(1), part_of(2), part_of(3)
+    expb_own = bias_own[4, :hid_o]
+    logs_total = bias_own[5, :heads]
+    modb_own = lax.dynamic_slice_in_dim(modb_all[:, :tiles].reshape(mods), rank * mod_o, mod_o, 0)
+    grad_silu = cond_sum[:, :, :own].reshape(img_n, seq_n, images, own).transpose(2, 0, 1, 3).reshape(images, width)
     cond_grad = jax.vjp(jax.nn.silu, condition)[1](grad_silu)[0]
-    back_cut = back_cut.astype(f32)
-    modw_own = back_cut[:, :, :mod_l].transpose(1, 0, 2).reshape(own, mods)
-    attnw_own = (
-        back_cut[:, :, mod_l : mod_l + 3 * dim_l]
-        .reshape(seq_n, own, pairs, 3, 128)
-        .transpose(1, 3, 0, 2, 4)
-        .reshape(own, 3 * width)
-    )
-    expw_own = (
-        back_cut[:, :, mod_l + 3 * dim_l : mod_l + 3 * dim_l + hid_l]
-        .reshape(seq_n, own, img_n, hid_o)
-        .transpose(1, 2, 0, 3)
-        .reshape(own, hidden)
-    )
-    modb_all = modb_all.reshape(seq_n, -1)[:, :mod_l].reshape(mods)
-    modb_own = lax.dynamic_slice_in_dim(modb_all, rank * mod_o, mod_o, 0)
     return (
         layer_out[:, :rows],
         token_grad[:, :rows],

time: 423 us -> 354 us (0.84); the launches traced: 418 us -> 354 us
  matrix products: 58.5 us -> 23.5 us
  Pallas kernels: 300 us -> 281 us
  other arithmetic: 26.2 us -> 21.1 us
  local copies, waits for them, and re-layouts: 31.5 us -> 27.1 us
    pallas_call x11 -> x2, Pallas kernels: 209 us -> 64.7 us  [exchange(): pl.pallas_call(kernel, out_shape=tuple(session.outs), in_specs=session.in...]
    pallas_call x0 -> x3, Pallas kernels: none -> 125 us  [the longest x1 74.8 us: feed_forward(): pl.pallas_call(kernel, out_shape=(jax.ShapeDtypeStruct(mlp_input.shape, f...]
    dot_general x5 -> x2, matrix products: 21.5 us -> 9.4 us  [mm(): return jnp.dot(a, b, preferred_element_type=f32)]
    dot_general x4 -> x2, matrix products: 17.3 us -> 5.82 us  [mm_nt(): lax.dot_general(a, b, (((1,), (1,)), ((), ())), preferred_element_type=f32)]
    dot_general x5 -> x2, matrix products: 18.3 us -> 8.29 us  [mm_tn(): lax.dot_general(a, b, (((0,), (0,)), ((), ())), preferred_element_type=f32)]
    unnamed x80 -> x57, local copies, waits for them, and re-layouts: 13.9 us -> 10 us
where the time goes in v3:
time: 354 us
  Pallas kernels  281 us (79%)
  local copies, waits for them, and re-layouts  27.1 us (8%)
  matrix products  23.5 us (7%)
  other arithmetic  21.1 us (6%)
    pallas_call x1, Pallas kernels, feed_forward(): pl.pallas_call(kernel, out_shape=(jax.ShapeDtypeStruct(mlp_input.shape, f...  74.8 us
    pallas_call x2, Pallas kernels, exchange(): pl.pallas_call(kernel, out_shape=tuple(session.outs), in_specs=session.in...  64.7 us
    pallas_call x1, Pallas kernels, attend_back(): pl.pallas_call(kernel, out_shape=tuple([jax.ShapeDtypeStruct(packed.shape...  51.8 us
    pallas_call x1, Pallas kernels, attend(): pl.pallas_call(kernel, out_shape=tuple([jax.ShapeDtypeStruct((images, row...  39.6 us
    pallas_call x1, Pallas kernels, closing(): pl.pallas_call(kernel, out_shape=(jax.ShapeDtypeStruct((own, mod_l * seq_...  27.2 us
    pallas_call x1, Pallas kernels, opening(): pl.pallas_call(kernel, out_shape=tuple([jax.ShapeDtypeStruct((seq_n, slim...  22.6 us
    unnamed x57, local copies, waits for them, and re-layouts  10 us
    dot_general x2, matrix products, mm(): return jnp.dot(a, b, preferred_element_type=f32)  9.4 us

profile of v3, /device:TPU:1, one launch (start us, length us, event | category | flops | bytes accessed | tf_op | source)
XLA Modules:
  0.0 353.5 jit_solution(8972685022480442850)
XLA Ops:
  1.4 0.9 reduce_window_sum.11
  2.3 0.8 concatenate.21
  6.2 1.5 convert_bitcast_fusion.refs_4_
  7.8 1.0 convert_element_type.77
  9.1 0.8 reshape.323.refs_1_
  12.6 22.6 %opening.1 = (f32[4,24,128]{2,1,0:T(8,128)}, f32[4,8,8,128]{3,2,1,0:T(8,128)}, f32[4,16,128]{2,1,0:T(8,128)}, bf16[4,32,1536]{2,1,0:T(8,128)(2,1)}, bf16[4,32,76...) custom-call(bf16[4,32,1536]{2,1,0:T(8,128)(2,1)} %bitcast.140, ...), custom_call_target="tpu_custom_call" | custom-call | tf_op jit(solution)/shard_map/opening/pallas_call | solution.py:344
  35.2 0.9 reshape.330
  40.1 1.0 broadcast_select_fusion.refs_3_.refs_4_
  41.1 1.2 convert_reduce_fusion.2
  42.3 0.9 fusion.30
  43.2 31.6 %exchange_5.1 = (bf16[4,11,32,1024]{3,2,1,0:T(8,128)(2,1)}, bf16[8,4,32,768]{3,2,1,0:T(8,128)(2,1)}, bf16[4,11,16,1024]{3,2,1,0:T(8,128)(2,1)}) custom-call(bf16[11,32,1024]{2,1,0:T(8,128)(2,1)} %bitcast.135, bf16[4,32,768]{2,1,0:T(8,128)(2,1)} %get-tuple-element.50.refs_1_, bf16[11,16,1024]{2,1,0:T(8,128)(2,1)} %bitcast.146), custom_call_target="tpu_custom_call" | custom-call | tf_op jit(solution)/shard_map/exchange_5/pallas_call | solution.py:516
  74.8 6.7 %fusion.34.refs_0_ = f32[4,2,176,768]{3,2,1,0:T(8,128)} fusion(bf16[4,2,176,1024]{3,2,1,0:T(8,128)(2,1)} %bitcast.177, bf16[1024,768,1,1]{1,0,3,2:T(8,128)(2,1)} %bitcast.183), kind=kOutput, calls=%fused_computation.107 | convolution fusion | flops 2214592512 | bytes 8781824 | tf_op jit(solution)/shard_map/dot_general | solution.py:964
  81.5 39.6 %attend.1 = (bf16[2,176,1024]{2,1,0:T(8,128)(2,1)}, bf16[8,4,32,1024]{3,2,1,0:T(8,128)(2,1)}, bf16[8,4,32,1024]{3,2,1,0:T(8,128)(2,1)}, bf16[4,11,16,1024]{3,2,1,0:T(8,128)(2,1)}) custom-call(f32[4,2,176,768]{3,2,1,0:T(8,128)} %fusion.34.refs_0_, f32[2,1,384]{2,1,0:T(1,128)} %pad_maximum_fusion.3.refs_1_.refs_2_, f32[2,1,128]{2,1,0:T(1,128)} %bitcast.168, ...), custom_call_target="tpu_custom_call" | custom-call | tf_op jit(solution)/shard_map/attend/pallas_call | solution.py:624
  121.1 2.7 convolution_add_fusion
  124.4 1.2 add_convert_fusion
  125.6 74.8 %feed_forward.1 = (f32[11,32,1024]{2,1,0:T(8,128)}, f32[4,32,1024]{2,1,0:T(8,128)}, bf16[4,11,32,1024]{3,2,1,0:T(8,128)(2,1)}, bf16[1024,1024]{1,0:T(8,128)(2,1)}, f32[1,1024]{1,0:T(1,128)}) custom-call(bf16[11,32,1024]{2,1,0:T(8,128)(2,1)} %bitcast.133, bf16[4,176,1024]{2,1,0:T(8,128)(2,1)} %bitcast.143, bf16[4,176,1024]{2,1,0:T(8,128)(2,1)} %bitcast.144, ...), custom_call_target="tpu_custom_call" | custom-call | tf_op jit(solution)/shard_map/feed_forward/pallas_call | solution.py:915
  200.5 1.9 fusion.26
  204.0 1.3 copy-done.18
  205.3 1.8 convolution_convert_fusion.2
  207.1 2.6 bitcast_convert_fusion
  209.7 51.8 %attend_back.1 = (bf16[4,2,176,768]{3,2,1,0:T(8,128)(2,1)}, f32[4,8,128]{2,1,0:T(8,128)}, bf16[4,32,1024]{2,1,0:T(8,128)(2,1)}, f32[11,32,1024]{2,1,0:T(8,128)}, bf16[8,32,1024]{2,1,0:T(8,128)(2,1)}) custom-call(f32[4,2,176,768]{3,2,1,0:T(8,128)} %fusion.34.refs_0_, bf16[2,176,1024]{2,1,0:T(8,128)(2,1)} %bitcast.151, ...), custom_call_target="tpu_custom_call" | custom-call | tf_op jit(solution)/shard_map/attend_back/pallas_call | solution.py:758
  261.6 5.7 %convolution_convert_fusion.1 = bf16[1024,768]{1,0:T(8,128)(2,1)} fusion(bf16[1408,1024]{1,0:T(8,128)(2,1)S(1)} %bitcast.178, bf16[1408,768]{1,0:T(8,128)(2,1)} %bitcast.179), kind=kOutput, calls=%fused_computation.14 | convolution fusion | flops 2215378944 | bytes 6619136 | tf_op jit(solution)/shard_map/dot_general | solution.py:972
  267.2 4.0 %convolution_convert_fusion = bf16[1408,1024]{1,0:T(8,128)(2,1)} fusion(bf16[1408,768]{1,0:T(8,128)(2,1)S(1)} %bitcast.180, bf16[1024,768]{1,0:T(8,128)(2,1)S(1)} %bitcast.184), kind=kOutput, calls=%fused_computation.1 | convolution fusion | flops 2216034304 | bytes 6619136 | tf_op jit(solution)/shard_map/dot_general | solution.py:968
  271.3 33.1 %exchange_12.1 = (f32[11,32,1024]{2,1,0:T(8,128)}, bf16[4,32,768]{2,1,0:T(8,128)(2,1)}, f32[1,32,1024]{2,1,0:T(8,128)}) custom-call(bf16[4,11,32,1024]{3,2,1,0:T(8,128)(2,1)} %bitcast.134, bf16[8,4,32,768]{3,2,1,0:T(8,128)(2,1)} %bitcast.139, bf16[8,1,32,1024]{3,2,1,0:T(8,128)(2,1)} %bitcast.153), custom_call_target="tpu_custom_call" | custom-call | tf_op jit(solution)/shard_map/exchange_12/pallas_call | solution.py:516
  305.1 1.6 copy.76
  307.2 2.1 fusion.8
  310.3 1.6 copy.77
  313.3 27.2 %closing.1 = (f32[32,6144]{1,0:T(8,128)}, f32[32,3072]{1,0:T(8,128)}, f32[32,4096]{1,0:T(8,128)}, f32[8,128]{1,0:T(8,128)}, f32[4,16,128]{2,1,0:T(8,128)}, /*index=5*/f32[8,8,128]{2,1,0:T(8,128)}) custom-call(f32[4,56,128]{2,1,0:T(8,128)} %pad_maximum_fusion.1.mine_ref, f32[8,128]{1,0:T(8,128)} %bitcast.171, f32[4,16,128]{2,1,0:T(8,128)} %get-tuple-element.69.lhs_ref, ...), custom_call_target="tpu_custom_call" | custom-call | tf_op jit(solution)/shard_map/closing/pallas_call | solution.py:470
  340.6 0.9 copy.75
  342.2 1.2 slice_bitcast_fusion.4
  343.4 1.4 fusion.33
  348.5 2.1 copy.100
  (137 shorter events, 23.8 us)
Async XLA Ops:
  0.6 9.3 %copy-start.6 = (f32[32,4096]{1,0:T(8,128)S(1)}, f32[32,4096]{1,0:T(8,128)}, u32[]{:S(2)}) copy-start(f32[32,4096]{1,0:T(8,128)} %param.27) | copy-start | bytes 1572868
  9.0 1.9 copy-start.7
  9.9 1.8 copy-start.3
  11.8 27.1 %copy-start.4 = (bf16[2,170,1024]{2,0,1:T(2,128)(2,1)S(1)}, bf16[2,170,1024]{2,0,1:T(2,128)(2,1)}, u32[]{:S(2)}) copy-start(bf16[2,170,1024]{2,0,1:T(2,128)(2,1)} %param.16) | copy-start | bytes 2088964
  38.3 1.3 copy-start.5
  200.4 1.9 copy-start
  203.7 1.6 copy-start.18
  205.3 1.8 copy-start.20
  209.7 51.8 %copy-start.16 = (bf16[4,11,32,1024]{3,2,1,0:T(8,128)(2,1)S(1)}, bf16[4,11,32,1024]{3,2,1,0:T(8,128)(2,1)}, u32[]{:S(2)}) copy-start(bf16[4,11,32,1024]{3,2,1,0:T(8,128)(2,1)} %get-tuple-element.51) | copy-start | bytes 8650756
  261.6 5.7 %copy-start.17 = (bf16[4,2,176,768]{3,2,1,0:T(8,128)(2,1)S(1)}, bf16[4,2,176,768]{3,2,1,0:T(8,128)(2,1)}, u32[]{:S(2)}) copy-start(bf16[4,2,176,768]{3,2,1,0:T(8,128)(2,1)} %get-tuple-element.64) | copy-start | bytes 6488068
  261.6 5.7 %copy-start.19 = (bf16[8,4,32,768]{3,2,1,0:T(8,128)(2,1)S(1)}, bf16[8,4,32,768]{3,2,1,0:T(8,128)(2,1)}, u32[]{:S(2)}) copy-start(bf16[8,4,32,768]{3,2,1,0:T(8,128)(2,1)} %get-tuple-element.52) | copy-start | bytes 4718596
  271.3 33.1 %copy-start.2 = (f32[11,32,1024]{2,1,0:T(8,128)S(1)}, f32[11,32,1024]{2,1,0:T(8,128)}, u32[]{:S(2)}) copy-start(f32[11,32,1024]{2,1,0:T(8,128)} %get-tuple-element.63) | copy-start | bytes 4325380
  305.1 1.6 copy-start.15
  307.2 2.2 copy-start.1
  310.2 2.3 copy-start.11
  310.3 2.2 copy-start.12
  311.8 29.7 %copy-start.14 = (f32[2,1024]{1,0:T(2,128)S(1)}, f32[2,1024]{1,0:T(2,128)}, u32[]{:S(2)}) copy-start(f32[2,1024]{1,0:T(2,128)} %param.18) | copy-start | bytes 24580
  340.5 10.0 %copy-start.10 = (f32[32,3072]{1,0:T(8,128)S(1)}, f32[32,3072]{1,0:T(8,128)}, u32[]{:S(2)}) copy-start(f32[32,3072]{1,0:T(8,128)} %get-tuple-element.186) | copy-start | bytes 1179652
  340.6 10.7 %copy-start.13 = (f32[1,32,1024]{2,1,0:T(8,128)S(1)}, f32[1,32,1024]{2,1,0:T(8,128)}, u32[]{:S(2)}) copy-start(f32[1,32,1024]{2,1,0:T(8,128)} %get-tuple-element.78) | copy-start | bytes 393220
  340.6 11.4 %copy-start.9 = (f32[32,4096]{1,0:T(8,128)S(1)}, f32[32,4096]{1,0:T(8,128)}, u32[]{:S(2)}) copy-start(f32[32,4096]{1,0:T(8,128)} %get-tuple-element.191) | copy-start | bytes 1572868
  350.5 2.2 copy-start.8

commit v4 on v3

--- a/solution.py
+++ b/solution.py
@@ -502,6 +502,226 @@
     return got
 
 
+def opening(cid, mod_cut, attn_cut, exp_cut, small, images, plans):
+    seq_n, own, mod_l = mod_cut.shape
+    img_n, rows, _ = small.shape
+    head = seq_n * images
+    tiles = mod_l // 128
+    slim = -(-tiles * images // 8) * 8
+    session = Session(plans)
+    session.peers = everyone_else("img", "seq")
+    ins, outs = 4 + len(session.ins), 6 + len(plans)
+
+    def kernel(*refs):
+        mod_ref, attn_ref, exp_ref, small_ref = refs[:4]
+        modo_ref, bias_ref, lhs_ref, modw_ref, attnw_ref, expw_ref = refs[ins : ins + 6]
+        small_all, part_buf, part_all, sum_buf = refs[ins + outs : ins + outs + 4]
+        sems = refs[ins + outs + 4 : ins + outs + 18]
+        session.greet()
+        small_go, small_end = direct_ops("img", small_ref, small_all, *sems[:2])
+        mod_go, mod_end = direct_ops("seq", mod_ref, modw_ref, *sems[2:4])
+        attn_go, attn_end = direct_ops("seq", attn_ref, attnw_ref, *sems[4:6])
+        exp_go, exp_end = direct_ops("seq", exp_ref, expw_ref, *sems[12:14])
+        session.bind(refs[4:ins], refs[ins + 6 : ins + outs], refs[ins + outs + 18 :])
+        small_go()
+        mod_go()
+        attn_go()
+        exp_go()
+        session.start()
+        part_buf[...] = jnp.zeros_like(part_buf)
+        small_end()
+        bias_go, bias_end = direct_ops("seq", small_all.at[:, head:], bias_ref, *sems[6:8], everyone=True)
+        bias_go()
+        for i in range(img_n):
+            for q in range(seq_n):
+                lhs_ref[q, i * images : (i + 1) * images] = small_all[i, q * images : (q + 1) * images]
+        mod_end()
+        part = jnp.zeros((img_n * images, mod_l), f32)
+        for q in range(seq_n):
+            part = part + dot(lhs_ref[q][:, :own].astype(bf16), modw_ref[q], ((1,), (0,)))
+        for i in range(img_n):
+            for t in range(tiles):
+                part_buf[i, t * images : (t + 1) * images] = part[
+                    i * images : (i + 1) * images, t * 128 : (t + 1) * 128
+                ]
+        part_go, part_end = direct_ops("img", part_buf, part_all, *sems[8:10])
+        part_go()
+        session.steps(0, 1)
+        part_end()
+        total = part_all[0]
+        for i in range(1, img_n):
+            total = total + part_all[i]
+        sum_buf[...] = total
+        sum_go, sum_end = direct_ops("seq", sum_buf, modo_ref, *sems[10:12], everyone=True)
+        sum_go()
+        bias_end()
+        sum_end()
+        attn_end()
+        exp_end()
+        session.finish()
+
+    full = pl.BlockSpec(memory_space=VM)
+    return pl.pallas_call(
+        kernel,
+        out_shape=tuple(
+            [
+                jax.ShapeDtypeStruct((seq_n, slim, 128), f32),
+                jax.ShapeDtypeStruct((seq_n, img_n, rows - head, 128), f32),
+                jax.ShapeDtypeStruct((seq_n, img_n * images, 128), f32),
+                jax.ShapeDtypeStruct(mod_cut.shape, bf16),
+                jax.ShapeDtypeStruct(attn_cut.shape, bf16),
+                jax.ShapeDtypeStruct(exp_cut.shape, bf16),
+            ]
+            + session.outs
+        ),
+        in_specs=[full] * 4 + session.in_specs,
+        out_specs=tuple([full] * 6 + session.out_specs),
+        scratch_shapes=[
+            VM(small.shape, f32),
+            VM((img_n, slim, 128), f32),
+            VM((img_n, slim, 128), f32),
+            VM((slim, 128), f32),
+        ]
+        + pairs_of_sems("img", "seq", "seq", "seq", "img", "seq", "seq")
+        + session.scratch,
+        compiler_params=params(cid),
+        name="opening",
+    )(mod_cut, attn_cut, exp_cut, small, *session.ins)
+
+
+def closing(cid, mine, expb, lhs, modw, back, images, pairs):
+    seq_n, own, mod_l = modw.shape
+    img_n = expb.shape[0]
+    rows = mine.shape[1]
+    head = seq_n * images
+    tiles = mod_l // 128
+    slim = -(-tiles * images // 8) * 8
+    share = img_n // seq_n
+    cut = back.shape[2]
+    dim_l = pairs * 128
+    width = dim_l * seq_n
+    hid_l = cut - 3 * dim_l
+    hid_o = hid_l // img_n
+    aligned = hid_o % 128 == 0
+    flat = -(-tiles // 8) * 8
+
+    def kernel(
+        mine_ref, expb_ref, lhs_ref, modw_ref, back_ref,
+        modw_own, attn_own, exp_own, bias_ref, modb_ref, cond_ref,
+        seen, block, got, dd, mw_send, mw_recv, mb_send, gs_send, gs_all, gs_seen, back_all, *sems
+    ):
+        barrier = Session([], everyone_else("img", "seq"))
+        barrier.greet()
+        mine_go, mine_end = direct_ops("seq", mine_ref, seen, *sems[:2])
+        back_go, back_end = direct_ops("seq", back_ref, back_all, *sems[2:4])
+        mine_go()
+        back_go()
+        block[...] = jnp.zeros_like(block)
+        gs_send[...] = jnp.zeros_like(gs_send)
+        mb_send[...] = jnp.zeros_like(mb_send)
+        mine_end()
+        total = seen[0]
+        for q in range(1, seq_n):
+            total = total + seen[q]
+        at = slim + 2 * img_n
+        for i in range(img_n):
+            block[i, :slim] = total[:slim]
+            block[i, slim : slim + 1] = total[slim + i : slim + i + 1]
+            block[i, slim + 1 : slim + 2] = total[slim + img_n + i : slim + img_n + i + 1]
+            row = at + 8 + i % share
+            block[i, slim + 2 : slim + 3] = seen[i // share, row : row + 1]
+            block[i, slim + 3 : slim + 4] = seen[i // share, row + share : row + share + 1]
+            block[i, slim + 4 : slim + 5] = expb_ref[i : i + 1]
+            block[i, slim + 5 : slim + 6] = total[at : at + 1]
+        img_go, img_end = direct_ops("img", block, got, *sems[4:6])
+        img_go()
+        back_end()
+        for q in range(seq_n):
+            for p in range(pairs):
+                for k in range(3):
+                    to = k * width + q * dim_l + p * 128
+                    at_c = p * 384 + k * 128
+                    attn_own[:, to : to + 128] = back_all[q, :, at_c : at_c + 128].astype(f32)
+            if aligned:
+                for i in range(img_n):
+                    to = (i * seq_n + q) * hid_o
+                    at_c = 3 * dim_l + i * hid_o
+                    exp_own[:, to : to + hid_o] = back_all[q, :, at_c : at_c + hid_o].astype(f32)
+            else:
+                exp_own[:, q * hid_l : (q + 1) * hid_l] = back_all[q, :, 3 * dim_l :].astype(f32)
+        img_end()
+        sums = got[0]
+        for i in range(1, img_n):
+            sums = sums + got[i]
+        bias_ref[...] = sums[slim:]
+        for t in range(tiles):
+            mb_send[t : t + 1] = jnp.sum(sums[t * images : (t + 1) * images], axis=0, keepdims=True)
+            for i in range(img_n):
+                dd[i * images : (i + 1) * images, t * 128 : (t + 1) * 128] = got[i, t * images : (t + 1) * images]
+        grad = dd[...]
+        high = grad.astype(bf16)
+        low = (grad - high.astype(f32)).astype(bf16)
+        for q in range(seq_n):
+            out = dot(high, modw_ref[q], ((1,), (1,))) + dot(low, modw_ref[q], ((1,), (1,)))
+            for i in range(img_n):
+                gs_send[i, q * images : (q + 1) * images, :own] = out[i * images : (i + 1) * images]
+        gs_go, gs_end = direct_ops("img", gs_send, gs_all, *sems[6:8])
+        gs_go()
+        for q in range(seq_n):
+            mw_send[q] = dot(lhs_ref[q][:, :own].astype(bf16), high, ((0,), (0,))).astype(bf16)
+        mb_go, mb_end = direct_ops("seq", mb_send, modb_ref, *sems[10:12], everyone=True)
+        mb_go()
+        gs_end()
+        all_go, all_end = direct_ops("seq", gs_all, gs_seen, *sems[12:14], everyone=True)
+        all_go()
+        mw_go, mw_end = direct_ops("seq", mw_send, mw_recv, *sems[8:10])
+        mw_go()
+        mb_end()
+        all_end()
+        out = gs_seen[0]
+        for q in range(1, seq_n):
+            out = out + gs_seen[q]
+        cond_ref[...] = out
+        mw_end()
+        for q in range(seq_n):
+            modw_own[:, q * mod_l : (q + 1) * mod_l] = mw_recv[q].astype(f32)
+
+    full = pl.BlockSpec(memory_space=VM)
+    got = pl.pallas_call(
+        kernel,
+        out_shape=(
+            jax.ShapeDtypeStruct((own, mod_l * seq_n), f32),
+            jax.ShapeDtypeStruct((own, 3 * width), f32),
+            jax.ShapeDtypeStruct((own, hid_l * seq_n), f32),
+            jax.ShapeDtypeStruct((8, 128), f32),
+            jax.ShapeDtypeStruct((seq_n, flat, 128), f32),
+            jax.ShapeDtypeStruct((img_n, head, 128), f32),
+        ),
+        in_specs=[full] * 5,
+        out_specs=(full,) * 6,
+        scratch_shapes=[
+            VM((seq_n, rows, 128), f32),
+            VM((img_n, slim + 8, 128), f32),
+            VM((img_n, slim + 8, 128), f32),
+            VM((img_n * images, mod_l), f32),
+            VM((seq_n, own, mod_l), bf16),
+            VM((seq_n, own, mod_l), bf16),
+            VM((flat, 128), f32),
+            VM((img_n, head, 128), f32),
+            VM((img_n, head, 128), f32),
+            VM((seq_n, img_n, head, 128), f32),
+            VM(back.shape, bf16),
+        ]
+        + pairs_of_sems("seq", "seq", "img", "img", "seq", "seq", "seq"),
+        compiler_params=params(cid),
+        name="closing",
+    )(mine, expb, lhs, modw, back)
+    got = list(got)
+    if not aligned:
+        got[2] = got[2].reshape(own, seq_n, img_n, hid_o).transpose(0, 2, 1, 3).reshape(own, hid_l * seq_n)
+    return got
+
+
 def exchange(cid, turns, *plans):
     session = Session(plans)
     ins, outs = len(session.ins), len(plans)
@@ -550,23 +770,38 @@
     return query, key, value, low_half, r_query, r_key
 
 
-def attend(cid, packed, bias, scale, sid_k, sid_q, plans):
-    blocks, images, rows_b, wide = packed.shape
+def attend(cid, attn_input, attn_own, bias, scale, sid_k, sid_q, out_img, exp_own, grad_own):
+    seq_n, img_n = lax.axis_size("seq"), lax.axis_size("img")
+    outer = seq_n // 2
+    chunks, size, width = attn_input.shape
+    local = chunks * size
+    images = sid_q.shape[0]
+    rows_b = local // images
+    rows = seq_n * rows_b
+    wide = attn_own.shape[2]
     pairs = wide // 384
-    rows = blocks * rows_b
     turns = images * pairs
-    width = pairs * 128 * blocks
-    session = Session(plans, [("seq", j) for j in range(1, blocks)])
-    ins, outs = 5 + len(session.ins), 1 + len(plans)
+    tile = 256 if wide % 256 == 0 else 128
+    w_chunks = attn_own.shape[0]
+    plans = [gather(x, "seq", True) for x in grad_own] + [gather(out_img, "seq", False, True), gather(exp_own, "img", False)]
+    session = Session(plans, everyone_else("seq") + two_level("img", img_n))
+    ins, outs = 6 + len(session.ins), 4 + len(plans)
 
     def kernel(*refs):
-        p_ref, b_ref, es_ref, sk_ref, sq_ref = refs[:5]
-        o_ref = refs[ins]
-        k_buf, v_buf, o_buf, o_send, o_recv = refs[ins + outs : ins + outs + 5]
+        x_ref, w_ref, b_ref, es_ref, sk_ref, sq_ref = refs[:6]
+        o_ref, p_out, h_out, w_out = refs[ins : ins + 4]
+        scratch = refs[ins + outs :]
+        h1, attn_w, packed, k_buf, v_buf, o_buf, o_send, o_recv, hs, hr, wk, ws, wr, out_sem = scratch[:14]
         me = lax.axis_index("seq")
         session.greet()
-        session.bind(refs[5:ins], refs[ins + 1 : ins + outs], refs[ins + outs + 5 :])
+        session.bind(refs[6:ins], refs[ins + 4 : ins + outs], scratch[14:])
+        h1_in = gather_ops("seq", True, x_ref, h1, None, hs, hr)
+        w_in = gather_ops("img", False, w_ref, attn_w, wk, ws, wr)
+        h1_in.start()
+        w_in.start()
         session.start()
+        *grads, (out_count, _, out_in), (exp_count, _, exp_in) = session.bound
+        h1[0] = x_ref[...]
 
         def ship(i, j):
             g, p = i // pairs, i % pairs
@@ -579,12 +814,41 @@
                 me ^ j,
             )
 
+        each(0, chunks // 2, h1_in.step)
+        each(0, w_chunks // 2, w_in.step)
+        each(chunks // 2, chunks, h1_in.step)
+        each(w_chunks // 2, w_chunks, w_in.step)
+        h1_in.near()
+        for o in range(1, outer):
+            h1_in.handed(o)
+        w_in.near()
+        for o in range(1, img_n // 2):
+            w_in.handed(o)
+        w_in.sent()
+        quarter = exp_count // 4
+        each(0, quarter, exp_in.step)
+
+        def project(k):
+            j, t = k // (wide // tile), k % (wide // tile)
+            columns = lanes(t * tile, tile)
+            part = dot(h1[j].reshape(local, width), attn_w[:, :, :, columns].reshape(width, tile), ((1,), (0,)))
+            packed[j, :, :, columns] = part.reshape(images, rows_b, tile)
+
+        each(0, seq_n * (wide // tile), project)
+        each(quarter, 2 * quarter, exp_in.step)
+        copies = [
+            pltpu.make_async_copy(src, dst, out_sem.at[n])
+            for n, (src, dst) in enumerate(((packed, p_out), (h1, h_out), (attn_w, w_out)))
+        ]
+        for copy in copies:
+            copy.start()
+
         def turn(i):
             g, p = i // pairs, i % pairs
-            query, key, value, low_half, r_query, r_key = load_heads(p_ref, b_ref[p], g, p, rows)
+            query, key, value, low_half, r_query, r_key = load_heads(packed, b_ref[p], g, p, rows)
             query_low = query * r_query * es_ref[p]
-            k_buf[...] = (key * r_key).astype(bf16).reshape(blocks, rows_b, 128)
-            v_buf[...] = value.astype(bf16).reshape(blocks, rows_b, 128)
+            k_buf[...] = (key * r_key).astype(bf16).reshape(seq_n, rows_b, 128)
+            v_buf[...] = value.astype(bf16).reshape(seq_n, rows_b, 128)
             sid_q = sq_ref[g]
             parts = []
             for h in range(2):
@@ -600,57 +864,114 @@
                     return total, acc
 
                 total, acc = lax.fori_loop(
-                    0, blocks, step, (jnp.zeros((1, rows), f32), jnp.zeros((128, rows), f32))
+                    0, seq_n, step, (jnp.zeros((1, rows), f32), jnp.zeros((128, rows), f32))
                 )
                 parts.append((acc / total)[64 * h : 64 * h + 64])
-            out = jnp.transpose(jnp.concatenate(parts, axis=0)).astype(bf16).reshape(blocks, rows_b, 128)
+            out = jnp.transpose(jnp.concatenate(parts, axis=0)).astype(bf16).reshape(seq_n, rows_b, 128)
             o_buf[i] = out
             o_ref[g, :, lanes((me * pairs + p) * 128, 128)] = out[0]
-            for j in range(1, blocks):
+            for j in range(1, seq_n):
                 ship(i, j).start()
-            session.steps(i, turns)
+
+            @pl.when(i == 0)
+            def _():
+                for count, _, ops in grads:
+                    each(0, count, ops.step)
+
+            half = turns // 2
+
+            @pl.when(i == half - 1)
+            def _():
+                each(2 * quarter, 3 * quarter, exp_in.step)
+
+            @pl.when(i == half)
+            def _():
+                each(0, out_count, out_in.step)
+                each(3 * quarter, exp_count, exp_in.step)
 
         each(0, turns, turn)
         session.finish()
+        h1_in.sent()
+        for copy in copies:
+            copy.wait()
 
         def last(i):
-            for j in range(1, blocks):
+            for j in range(1, seq_n):
                 ship(i, j).wait()
 
         each(0, turns, last)
 
     full = pl.BlockSpec(memory_space=VM)
-    sems = pltpu.SemaphoreType.DMA((blocks, turns))
+    any_space = pl.BlockSpec(memory_space=pl.ANY)
+    sems = pltpu.SemaphoreType.DMA((seq_n, turns))
+    seq_sems = pltpu.SemaphoreType.DMA((seq_n, chunks))
+    img_sems = pltpu.SemaphoreType.DMA((img_n, w_chunks))
+    packed = (seq_n, images, rows_b, wide)
     return pl.pallas_call(
         kernel,
-        out_shape=tuple([jax.ShapeDtypeStruct((images, rows_b, width), bf16)] + session.outs),
-        in_specs=[full] * 5 + session.in_specs,
-        out_specs=tuple([full] + session.out_specs),
+        out_shape=tuple(
+            [
+                jax.ShapeDtypeStruct((images, rows_b, width), bf16),
+                jax.ShapeDtypeStruct(packed, f32),
+                jax.ShapeDtypeStruct((seq_n,) + attn_input.shape, bf16),
+                jax.ShapeDtypeStruct((img_n,) + attn_own.shape, bf16),
+            ]
+            + session.outs
+        ),
+        in_specs=[full] * 6 + session.in_specs,
+        out_specs=tuple([full] + [any_space] * 3 + session.out_specs),
         scratch_shapes=[
-            VM((blocks, rows_b, 128), bf16),
-            VM((blocks, rows_b, 128), bf16),
-            VM((turns, blocks, rows_b, 128), bf16),
+            VM((seq_n,) + attn_input.shape, bf16),
+            VM((img_n,) + attn_own.shape, bf16),
+            VM(packed, f32),
+            VM((seq_n, rows_b, 128), bf16),
+            VM((seq_n, rows_b, 128), bf16),
+            VM((turns, seq_n, rows_b, 128), bf16),
             sems,
             sems,
+            seq_sems,
+            seq_sems,
+            pltpu.SemaphoreType.DMA((w_chunks,)),
+            img_sems,
+            img_sems,
+            pltpu.SemaphoreType.DMA((3,)),
         ]
         + session.scratch,
         compiler_params=params(cid),
         name="attend",
-    )(packed, bias, scale, sid_k, sid_q, *session.ins)
-
-
-def attend_back(cid, packed, d_out, bias, scale, sid_k, sid_q, plans):
-    blocks, images, rows_b, wide = packed.shape
+    )(attn_input, attn_own, bias, scale, sid_k, sid_q, *session.ins)
+
+
+def attend_back(cid, packed, h1, attn_w, d_out, bias, scale, sid_k, sid_q, expw_part, shrunk_part, outw_part):
+    seq_n, images, rows_b, wide = packed.shape
+    img_n = lax.axis_size("img")
+    outer = seq_n // 2
     pairs = wide // 384
-    rows = blocks * rows_b
+    rows = seq_n * rows_b
     turns = images * pairs
-    session = Session(plans, [("seq", j) for j in range(1, blocks)])
-    ins, outs = 6 + len(session.ins), 2 + len(plans)
+    _, chunks, size, width = h1.shape
+    local = chunks * size
+    _, w_chunks, w_size, _ = attn_w.shape
+    own = outw_part.shape[2]
+    tile = 256
+    blocks_per_tile = tile // (w_chunks * w_size)
+    session = Session([], everyone_else("seq") + two_level("img", img_n))
+    mids = [
+        scatter_scratch(img_n, expw_part.shape[1:], bf16),
+        scatter_scratch(seq_n, shrunk_part.shape[1:], bf16),
+        scatter_scratch(seq_n, (img_n, own, width), bf16),
+        scatter_scratch(img_n, (1, own, width), bf16),
+        scatter_scratch(img_n, attn_w.shape[1:], bf16),
+        scatter_scratch(seq_n, h1.shape[1:], bf16),
+    ]
 
     def kernel(*refs):
-        p_ref, do_ref, b_ref, es_ref, sk_ref, sq_ref = refs[:6]
-        dp_ref, st_ref = refs[ins : ins + 2]
-        k_buf, v_buf, e_buf, g_buf, dk_buf, dv_buf, do_buf, o_send, o_recv = refs[ins + outs : ins + outs + 9]
+        p_in, h_in, w_in, do_ref, b_ref, es_ref, sk_ref, sq_ref, expw_ref, f_ref, outw_ref = refs[:11]
+        st_ref, dh1_own, attn_own, expw_own, f_own, outw_own = refs[11:17]
+        scratch = refs[17:]
+        p_ref, h_ref, w_ref, dp_ref, dh1, dattn, out_mid, load_sem = scratch[:8]
+        k_buf, v_buf, e_buf, g_buf, dk_buf, dv_buf, do_buf, o_send, o_recv = scratch[8:17]
+        more = scratch[17:]
         me = lax.axis_index("seq")
         session.greet()
 
@@ -666,12 +987,27 @@
             )
 
         def send(i):
-            for j in range(1, blocks):
+            for j in range(1, seq_n):
                 ship(i, j).start()
 
         each(0, turns, send)
-        session.bind(refs[6:ins], refs[ins + 2 : ins + outs], refs[ins + outs + 9 :])
-        session.start()
+        loads = [
+            pltpu.make_async_copy(src, dst, load_sem.at[n])
+            for n, (src, dst) in enumerate(((p_in, p_ref), (h_in, h_ref), (w_in, w_ref)))
+        ]
+        for load in loads:
+            load.start()
+        exp_out = scatter_ops("img", False, expw_ref, expw_own, *more[:7])
+        f_out = scatter_ops("seq", True, f_ref, f_own, *more[7:14])
+        mid_out = scatter_ops("seq", False, outw_ref, out_mid.at[:, 0], *more[14:21], inside=True)
+        outw_out = scatter_ops("img", False, out_mid, outw_own, *more[21:28])
+        attn_out = scatter_ops("img", False, dattn, attn_own, *more[28:35])
+        dh1_out = scatter_ops("seq", True, dh1, dh1_own, *more[35:42])
+        exp_out.start()
+        mid_out.start()
+        f_out.start()
+        exp_chunks = expw_ref.shape[1]
+        loads[0].wait()
 
         def turn(i):
             g, p = i // pairs, i % pairs
@@ -680,10 +1016,10 @@
             q_unit = query * r_query
             k_unit = key * r_key
             q_full = q_unit * scale_row
-            k_buf[...] = k_unit.astype(bf16).reshape(blocks, rows_b, 128)
-            v_buf[...] = value.astype(bf16).reshape(blocks, rows_b, 128)
+            k_buf[...] = k_unit.astype(bf16).reshape(seq_n, rows_b, 128)
+            v_buf[...] = value.astype(bf16).reshape(seq_n, rows_b, 128)
             do_buf[i, 0] = do_ref[g, :, lanes((me * pairs + p) * 128, 128)]
-            for j in range(1, blocks):
+            for j in range(1, seq_n):
                 ship(i, j).wait_recv()
             d_out = do_buf[i].reshape(rows, 128).astype(f32)
             sid_q = sq_ref[g]
@@ -709,7 +1045,7 @@
                     return total, mixed
 
                 zero = jnp.zeros((1, rows), f32)
-                total, mixed = lax.fori_loop(0, blocks, first, (zero, zero))
+                total, mixed = lax.fori_loop(0, seq_n, first, (zero, zero))
                 inverse = 1.0 / total
                 delta = mixed * inverse
 
@@ -726,7 +1062,7 @@
                         dk_buf[b] = dk_buf[b] + dk
                     return acc + dot(k_buf[b], scores_grad, ((0,), (0,)))
 
-                acc = lax.fori_loop(0, blocks, second, jnp.zeros((128, rows), f32))
+                acc = lax.fori_loop(0, seq_n, second, jnp.zeros((128, rows), f32))
                 parts.append(acc[64 * h : 64 * h + 64])
             dq = jnp.transpose(jnp.concatenate(parts, axis=0)).astype(bf16).astype(f32)
             dk = dk_buf[...].reshape(rows, 128).astype(bf16).astype(f32)
@@ -734,7 +1070,7 @@
             dq_raw = scale_row * r_query * (dq - q_unit * half_sums(q_unit * dq, low_half))
             dk_raw = r_key * (dk - k_unit * half_sums(k_unit * dk, low_half))
             together = jnp.concatenate([dq_raw, dk_raw, dv], axis=1).astype(bf16)
-            dp_ref[:, g, :, lanes(p * 384, 384)] = together.reshape(blocks, rows_b, 384)
+            dp_ref[:, g, :, lanes(p * 384, 384)] = together.reshape(seq_n, rows_b, 384)
             sums = [
                 jnp.sum(dq_raw, axis=0, keepdims=True),
                 jnp.sum(dv, axis=0, keepdims=True),
@@ -742,41 +1078,101 @@
                 jnp.zeros((5, 128), f32),
             ]
             st_ref[i] = jnp.concatenate(sums, axis=0)
-            session.steps(i, turns)
+
+            @pl.when(i == 0)
+            def _():
+                each(0, img_n, mid_out.step)
+                each(0, chunks, f_out.step)
+
+            each((i * exp_chunks) // turns, ((i + 1) * exp_chunks) // turns, exp_out.step)
 
         each(0, turns, turn)
-        session.finish()
+        mid_out.finish()
+        outw_out.start()
+        for load in loads[1:]:
+            load.wait()
+
+        def columns(t):
+            return lanes(t * tile, tile)
+
+        def weight_grad(t):
+            left = h_ref[:, :, :, columns(t)].reshape(seq_n * local, tile)
+            part = dot(left, dp_ref[...].reshape(seq_n * local, wide), ((0,), (0,)))
+            dattn[pl.ds(t * blocks_per_tile, blocks_per_tile)] = part.astype(bf16).reshape(
+                blocks_per_tile, w_chunks, w_size, wide
+            )
+
+        def input_grad(j):
+            def run(t):
+                weight = w_ref[pl.ds(t * blocks_per_tile, blocks_per_tile)].reshape(tile, wide)
+                part = dot(dp_ref[j].reshape(local, wide), weight, ((1,), (1,)))
+                dh1[j, :, :, columns(t)] = part.astype(bf16).reshape(chunks, size, tile)
+
+            each(0, width // tile, run)
+
+        each(0, width // tile, weight_grad)
+        attn_out.start()
+        outw_out.step(0)
+        exp_out.finish()
+        for o in range(1, outer):
+            for j in (2 * o + 1, 2 * o):
+                input_grad(j)
+        dh1_out.start_outer()
+        each(0, chunks, dh1_out.step)
+        each(0, w_chunks // 2, attn_out.step)
+        for j in (1, 0):
+            input_grad(j)
+        dh1_out.start_inner()
+        each(w_chunks // 2, w_chunks, attn_out.step)
+        outw_out.finish()
+        f_out.finish()
+        dh1_out.finish()
+        attn_out.finish()
 
         def last(i):
-            for j in range(1, blocks):
+            for j in range(1, seq_n):
                 ship(i, j).wait_send()
 
         each(0, turns, last)
 
     full = pl.BlockSpec(memory_space=VM)
-    sems = pltpu.SemaphoreType.DMA((blocks, turns))
+    any_space = pl.BlockSpec(memory_space=pl.ANY)
+    sems = pltpu.SemaphoreType.DMA((seq_n, turns))
     return pl.pallas_call(
         kernel,
-        out_shape=tuple(
-            [jax.ShapeDtypeStruct(packed.shape, bf16), jax.ShapeDtypeStruct((turns, 8, 128), f32)] + session.outs
+        out_shape=(
+            jax.ShapeDtypeStruct((turns, 8, 128), f32),
+            jax.ShapeDtypeStruct(h1.shape[1:], f32),
+            jax.ShapeDtypeStruct(attn_w.shape[1:], bf16),
+            jax.ShapeDtypeStruct(expw_part.shape[1:], bf16),
+            jax.ShapeDtypeStruct(shrunk_part.shape[1:], f32),
+            jax.ShapeDtypeStruct((1, own, width), f32),
         ),
-        in_specs=[full] * 6 + session.in_specs,
-        out_specs=tuple([full] * 2 + session.out_specs),
+        in_specs=[any_space] * 3 + [full] * 8,
+        out_specs=(full,) * 6,
         scratch_shapes=[
-            VM((blocks, rows_b, 128), bf16),
-            VM((blocks, rows_b, 128), bf16),
-            VM((blocks, rows_b, rows), f32),
-            VM((blocks, rows_b, rows), f32),
-            VM((blocks, rows_b, 128), f32),
-            VM((blocks, rows_b, 128), f32),
-            VM((turns, blocks, rows_b, 128), bf16),
+            VM(packed.shape, f32),
+            VM(h1.shape, bf16),
+            VM(attn_w.shape, bf16),
+            VM(packed.shape, bf16),
+            VM(h1.shape, bf16),
+            VM(attn_w.shape, bf16),
+            VM((img_n, 1, own, width), bf16),
+            pltpu.SemaphoreType.DMA((3,)),
+            VM((seq_n, rows_b, 128), bf16),
+            VM((seq_n, rows_b, 128), bf16),
+            VM((seq_n, rows_b, rows), f32),
+            VM((seq_n, rows_b, rows), f32),
+            VM((seq_n, rows_b, 128), f32),
+            VM((seq_n, rows_b, 128), f32),
+            VM((turns, seq_n, rows_b, 128), bf16),
             sems,
             sems,
         ]
-        + session.scratch,
+        + [x for scratch in mids for x in scratch],
         compiler_params=params(cid),
         name="attend_back",
-    )(packed, d_out, bias, scale, sid_k, sid_q, *session.ins)
+    )(packed, h1, attn_w, d_out, bias, scale, sid_k, sid_q, expw_part, shrunk_part, outw_part)
 
 
 def gelu_both(x):
@@ -788,14 +1184,15 @@
     return x * half, slope
 
 
-def feed_forward(cid, mlp_input, grad_parts, shr_own, exp_w, e_bias):
+def feed_forward(cid, mlp_input, grad_parts, grad_own, shr_own, exp_w, e_bias):
     seq_n, img_n = lax.axis_size("seq"), lax.axis_size("img")
     outer = seq_n // 2
     chunks, size, width = mlp_input.shape
     rows = chunks * size
     hid_l = exp_w.shape[1]
-    images = len(grad_parts)
-    rows_p = rows // images
+    ready, later = len(grad_parts), len(grad_own)
+    images = ready + later
+    g_chunks, g_size, _ = grad_own[0].shape
     w_chunks, w_size, _ = shr_own.shape
     hid_o = w_chunks * w_size
     tile = 256
@@ -806,6 +1203,10 @@
         df_refs = refs[:images]
         shr_ref, exp_ref, eb_ref, dh2_ref, dshr_own, f_ref, dexp_ref, expb_ref = refs[images : images + 8]
         h2, df, shr, act, slope, dshr, dh2, df_sem, hs, hr, ss, sr, sk, *more = refs[images + 8 :]
+        df_in = [
+            gather_ops("seq", True, df_refs[ready + g], df.at[:, ready + g], *more[14 + 3 * g : 17 + 3 * g])
+            for g in range(later)
+        ]
         session.greet()
         h2_in = gather_ops("seq", True, x_ref, h2, None, hs, hr)
         shr_in = gather_ops("img", False, shr_ref, shr, sk, ss, sr)
@@ -813,7 +1214,9 @@
         dshr_out = scatter_ops("img", False, dshr, dshr_own, *more[7:14])
         h2_in.start()
         shr_in.start()
-        loads = [pltpu.make_async_copy(ref, df.at[:, g], df_sem.at[g]) for g, ref in enumerate(df_refs)]
+        for ops in df_in:
+            ops.start()
+        loads = [pltpu.make_async_copy(ref, df.at[:, g], df_sem.at[g]) for g, ref in enumerate(df_refs[:ready])]
         for load in loads:
             load.start()
         h2[0] = x_ref[...]
@@ -878,9 +1281,13 @@
         for o in range(1, outer):
             expand(2 * o)
         each(w_chunks // 2, w_chunks, shr_in.step)
+        for ops in df_in:
+            each(0, g_chunks, ops.step)
         for o in range(1, outer):
             h2_in.handed(o)
             expand(2 * o + 1)
+        for ops in df_in:
+            ops.finish()
         for load in loads:
             load.wait()
         each(0, hid_l // tile, shrink_grad)
@@ -912,6 +1319,7 @@
     any_space = pl.BlockSpec(memory_space=pl.ANY)
     seq_sems = pltpu.SemaphoreType.DMA((seq_n, chunks))
     img_sems = pltpu.SemaphoreType.DMA((img_n, w_chunks))
+    grad_sems = pltpu.SemaphoreType.DMA((seq_n, g_chunks))
     return pl.pallas_call(
         kernel,
         out_shape=(
@@ -921,17 +1329,17 @@
             jax.ShapeDtypeStruct(exp_w.shape, bf16),
             jax.ShapeDtypeStruct((1, hid_l), f32),
         ),
-        in_specs=[full] + [any_space] * images + [full] * 3,
+        in_specs=[full] + [any_space] * ready + [full] * (later + 3),
         out_specs=(full,) * 5,
         scratch_shapes=[
             VM((seq_n,) + mlp_input.shape, bf16),
-            VM((seq_n, images, rows_p, width), bf16),
+            VM((seq_n, images, g_chunks, g_size, width), bf16),
             VM((img_n,) + shr_own.shape, bf16),
             VM((seq_n, rows, hid_l), bf16),
             VM((seq_n, rows, hid_l), bf16),
             VM((img_n,) + shr_own.shape, bf16),
             VM((seq_n,) + mlp_input.shape, bf16),
-            pltpu.SemaphoreType.DMA((images,)),
+            pltpu.SemaphoreType.DMA((max(ready, 1),)),
             seq_sems,
             seq_sems,
             img_sems,
@@ -939,10 +1347,11 @@
             pltpu.SemaphoreType.DMA((w_chunks,)),
         ]
         + scatter_scratch(seq_n, mlp_input.shape, bf16)
-        + scatter_scratch(img_n, shr_own.shape, bf16),
+        + scatter_scratch(img_n, shr_own.shape, bf16)
+        + [pltpu.SemaphoreType.DMA((g_chunks,)), grad_sems, grad_sems] * later,
         compiler_params=params(cid),
         name="feed_forward",
-    )(mlp_input, *grad_parts, shr_own, exp_w, e_bias)
+    )(mlp_input, *grad_parts, *grad_own, shr_own, exp_w, e_bias)
 
 
 def normalize(values):
@@ -1086,7 +1495,6 @@
     resid_in = pad_to(tokens, rows_p, 1).astype(f32)
     grad_out = pad_to(cotangent, rows_p, 1).astype(f32)
     local = images * rows_p
-    all_rows = seq_n * local
 
     def chunked(x):
         return x.reshape(x.shape[: x.ndim - 3] + (local // 32, 32, width))
@@ -1095,32 +1503,20 @@
     attn_input = (normed_in * (1.0 + scale_attn) + shift_attn).astype(bf16)
     grad_shrunk = (grad_out * gain_mlp).astype(bf16)
     grad_chunks = grad_shrunk.reshape(images, rows_p // 16, 16, width)
-    turns = 16
-    first = images // 2
-    h1, attn_w, *df_first = exchange(
+    ready = images // 2
+    context_low, packed, h1, attn_w, *gathered = attend(
         5,
-        turns,
-        gather(chunked(attn_input), "seq", True).during(0, turns * 2 // 3),
-        gather(weight_chunks(attn_b), "img", False),
-        *[gather(grad_chunks[g], "seq", True).during(turns * 2 // 3, turns) for g in range(first)],
-    )
-    h1 = h1.reshape(all_rows, width)
-    attn_w = attn_w.reshape(width, 3 * dim_l)
-    packed = mm(h1, attn_w).reshape(seq_n, images, rows_p, 3 * dim_l)
-    later = images * pairs // 2
-    context_low, out_w, exp_w, *df_second = attend(
-        6,
-        packed,
+        chunked(attn_input),
+        weight_chunks(attn_b),
         pair_bias,
         pair_scale,
         sid_k,
         sid_q,
-        [
-            gather(out_img, "seq", False, True).during(0, later),
-            gather(weight_chunks(exp_b), "img", False),
-        ]
-        + [gather(grad_chunks[g], "seq", True).during(later, 2 * later) for g in range(first, images)],
+        out_img,
+        weight_chunks(exp_b),
+        [grad_chunks[g] for g in range(ready)],
     )
+    df_ready, out_w, exp_w = gathered[:ready], gathered[ready], gathered[ready + 1]
     context_low = context_low.reshape(local, width)
     out_w = out_w.reshape(width, width)
     exp_w = exp_w.reshape(width, hid_l)
@@ -1128,12 +1524,12 @@
     resid_mid = resid_in + gain_attn * attn_out
     normed_mid = normalize(resid_mid)
     mlp_input = (normed_mid * (1.0 + scale_mlp) + shift_mlp).astype(bf16)
-    df_parts = [x.reshape(seq_n, rows_p, width) for x in df_first + df_second]
     shrb_part = jnp.sum(grad_shrunk.astype(f32), axis=(0, 1))
     grad_mlp_input, shrw_own, shrunk_part, expw_part, expb_part = feed_forward(
         7,
         chunked(mlp_input),
-        df_parts,
+        df_ready,
+        [grad_chunks[g] for g in range(ready, images)],
         hidden_chunks(shrink_weight.astype(bf16)),
         exp_w,
         e_bias.reshape(1, hid_l),
@@ -1153,19 +1549,19 @@
     grad_context = mm_nt(da, out_w).astype(bf16)
     grad_context = grad_context.reshape(images, rows_p, width)
     outw_part = mm_tn(context_low, da).astype(bf16).reshape(img_n, seq_n, own, width)
-    grad_packed, sums, expw_blk, shrunk, outw_blk = attend_back(
+    sums, grad_attn_input, attnw_blk, expw_blk, shrunk, outw_own = attend_back(
         11,
         packed,
+        h1,
+        attn_w,
         grad_context,
         pair_bias,
         pair_scale,
         sid_k,
         sid_q,
-        [
-            scatter_sum(weight_chunks(expw_part), "img", False, bf16),
-            scatter_sum(shrunk_part, "seq", True),
-            scatter_sum(outw_part, "seq", False, bf16, True),
-        ],
+        weight_chunks(expw_part),
+        shrunk_part,
+        outw_part,
     )
     shrunk = shrunk.reshape(images, rows_p, width) + s_bias
     layer_out = (resid_mid + gain_mlp * shrunk).astype(bf16)
@@ -1174,16 +1570,6 @@
     qb_part = sums[:, 0].reshape(dim_l)
     vb_part = sums[:, 1].reshape(dim_l)
     logs_part = jnp.sum(sums[:, 2].reshape(dim_l // headdim, headdim), axis=1)
-    grad_packed = grad_packed.reshape(all_rows, 3 * dim_l)
-    grad_in_part = mm_nt(grad_packed, attn_w).astype(bf16).reshape(seq_n, images, rows_p, width)
-    attnw_part = mm_tn(h1, grad_packed).astype(bf16)
-    grad_attn_input, attnw_blk, outw_own = exchange(
-        12,
-        local // 32,
-        scatter_sum(chunked(grad_in_part), "seq", True),
-        scatter_sum(weight_chunks(attnw_part.reshape(img_n, blk, 3 * dim_l)), "img", False, bf16),
-        scatter_sum(outw_blk.reshape(img_n, 1, own, width), "img", False),
-    )
     outw_own = outw_own.reshape(own, width)
     grad_attn_input = grad_attn_input.reshape(images, rows_p, width)
     grad_scale_attn = jnp.sum(grad_attn_input * normed_in, axis=1)

time: 354 us -> 319 us (0.901)
  Pallas kernels: 281 us -> 261 us
  matrix products: 23.5 us -> 7.21 us
    pallas_call x3 -> x1, Pallas kernels: 116 us -> 71.5 us  [attend_back(): pl.pallas_call(kernel, out_shape=(jax.ShapeDtypeStruct((turns, 8, 128), f...]
    pallas_call x1, Pallas kernels: 39.6 us -> 63.3 us  [attend(): pl.pallas_call(kernel, out_shape=tuple([jax.ShapeDtypeStruct((images, row...]
    dot_general x2 -> x1, matrix products: 9.4 us -> 2.74 us  [mm(): return jnp.dot(a, b, preferred_element_type=f32)]
    dot_general x2 -> x1, matrix products: 8.29 us -> 2.67 us  [mm_tn(): lax.dot_general(a, b, (((0,), (0,)), ((), ())), preferred_element_type=f32)]
    dot_general x2 -> x1, matrix products: 5.82 us -> 1.8 us  [mm_nt(): lax.dot_general(a, b, (((1,), (1,)), ((), ())), preferred_element_type=f32)]
    unnamed x57 -> x49, local copies, waits for them, and re-layouts: 10 us -> 10 us
where the time goes in v4:
time: 319 us; the launch traced here: 318 us
  Pallas kernels  261 us (82%)
  local copies, waits for them, and re-layouts  27 us (8%)
  other arithmetic  22.3 us (7%)
  matrix products  7.21 us (2%)
    pallas_call x1, Pallas kernels, feed_forward(): pl.pallas_call(kernel, out_shape=(jax.ShapeDtypeStruct(mlp_input.shape, f...  76.2 us
    pallas_call x1, Pallas kernels, attend_back(): pl.pallas_call(kernel, out_shape=(jax.ShapeDtypeStruct((turns, 8, 128), f...  71.5 us
    pallas_call x1, Pallas kernels, attend(): pl.pallas_call(kernel, out_shape=tuple([jax.ShapeDtypeStruct((images, row...  63.3 us
    pallas_call x1, Pallas kernels, closing(): pl.pallas_call(kernel, out_shape=(jax.ShapeDtypeStruct((own, mod_l * seq_...  27.1 us
    pallas_call x1, Pallas kernels, opening(): pl.pallas_call(kernel, out_shape=tuple([jax.ShapeDtypeStruct((seq_n, slim...  22.6 us
    unnamed x49, local copies, waits for them, and re-layouts  10 us

profile of v4, /device:TPU:1, one launch (start us, length us, event | category | flops | bytes accessed | tf_op | source)
XLA Modules:
  0.0 318.4 jit_solution(8778537774635266659)
XLA Ops:
  1.4 0.9 reduce_window_sum.11
  2.3 0.8 concatenate.21
  6.2 1.5 convert_bitcast_fusion.refs_4_
  7.8 1.0 convert_element_type.71
  9.1 0.8 reshape.302.refs_1_
  10.2 0.8 reshape.304.refs_2_
  12.5 22.6 %opening.1 = (f32[4,24,128]{2,1,0:T(8,128)}, f32[4,8,8,128]{3,2,1,0:T(8,128)}, f32[4,16,128]{2,1,0:T(8,128)}, bf16[4,32,1536]{2,1,0:T(8,128)(2,1)}, bf16[4,32,76...) custom-call(bf16[4,32,1536]{2,1,0:T(8,128)(2,1)} %bitcast.119, ...), custom_call_target="tpu_custom_call" | custom-call | tf_op jit(solution)/shard_map/opening/pallas_call | solution.py:564
  35.2 0.9 reshape.309
  36.9 0.8 broadcast_add_fusion.1
  40.1 1.0 broadcast_select_fusion.refs_4_.refs_6_
  41.1 1.2 convert_reduce_fusion.2
  42.3 0.9 fusion.30
  43.2 63.3 %attend.1 = (bf16[2,176,1024]{2,1,0:T(8,128)(2,1)}, f32[4,2,176,768]{3,2,1,0:T(8,128)}, bf16[4,11,32,1024]{3,2,1,0:T(8,128)(2,1)}, bf16[8,4,32,768]{3,2,1,0:T(8,...) custom-call(bf16[11,32,1024]{2,1,0:T(8,128)(2,1)} %bitcast.115, ...), custom_call_target="tpu_custom_call" | custom-call | tf_op jit(solution)/shard_map/attend/pallas_call | solution.py:910
  106.5 2.7 convolution_add_fusion
  109.9 1.2 add_convert_fusion
  111.1 76.2 %feed_forward.1 = (f32[11,32,1024]{2,1,0:T(8,128)}, f32[4,32,1024]{2,1,0:T(8,128)}, bf16[4,11,32,1024]{3,2,1,0:T(8,128)(2,1)}, bf16[1024,1024]{1,0:T(8,128)(2,1)}, f32[1,1024]{1,0:T(1,128)}) custom-call(bf16[11,32,1024]{2,1,0:T(8,128)(2,1)} %bitcast.114, bf16[4,11,16,1024]{3,2,1,0:T(8,128)(2,1)} %get-tuple-element.56.refs_0_, ...), custom_call_target="tpu_custom_call" | custom-call | tf_op jit(solution)/shard_map/feed_forward/pallas_call | solution.py:1323
  187.2 1.9 fusion.26
  190.7 1.3 copy-done.15
  192.0 1.8 convolution_convert_fusion
  193.8 2.7 bitcast_convert_fusion
  196.5 71.5 %attend_back.1 = (f32[4,8,128]{2,1,0:T(8,128)}, f32[11,32,1024]{2,1,0:T(8,128)}, bf16[4,32,768]{2,1,0:T(8,128)(2,1)}, bf16[4,32,1024]{2,1,0:T(8,128)(2,1)}, f32[...) custom-call(f32[4,2,176,768]{3,2,1,0:T(8,128)} %get-tuple-element.53.refs_0_, ...), custom_call_target="tpu_custom_call" | custom-call | tf_op jit(solution)/shard_map/attend_back/pallas_call | solution.py:1141
  268.0 1.7 fusion.12
  270.1 1.6 copy.76
  272.2 2.1 fusion.8
  275.3 1.6 copy.77
  277.5 0.8 pad_maximum_fusion.back_ref
  278.3 27.1 %closing.1 = (f32[32,6144]{1,0:T(8,128)}, f32[32,3072]{1,0:T(8,128)}, f32[32,4096]{1,0:T(8,128)}, f32[8,128]{1,0:T(8,128)}, f32[4,16,128]{2,1,0:T(8,128)}, /*index=5*/f32[8,8,128]{2,1,0:T(8,128)}) custom-call(f32[4,56,128]{2,1,0:T(8,128)} %pad_maximum_fusion.1.mine_ref, f32[8,128]{1,0:T(8,128)} %bitcast.147, f32[4,16,128]{2,1,0:T(8,128)} %get-tuple-element.65.lhs_ref, ...), custom_call_target="tpu_custom_call" | custom-call | tf_op jit(solution)/shard_map/closing/pallas_call | solution.py:690
  305.5 0.9 copy.75
  307.0 1.2 slice_bitcast_fusion.4
  308.2 1.4 fusion.33
  313.3 2.1 copy.99
  316.8 0.8 copy.102
  (124 shorter events, 20.1 us)
Async XLA Ops:
  0.6 9.3 %copy-start.5 = (f32[32,4096]{1,0:T(8,128)S(1)}, f32[32,4096]{1,0:T(8,128)}, u32[]{:S(2)}) copy-start(f32[32,4096]{1,0:T(8,128)} %param.27) | copy-start | bytes 1572868
  9.0 1.9 copy-start.6
  9.9 1.8 copy-start.2
  11.8 27.1 %copy-start.3 = (bf16[2,170,1024]{2,0,1:T(2,128)(2,1)S(1)}, bf16[2,170,1024]{2,0,1:T(2,128)(2,1)}, u32[]{:S(2)}) copy-start(bf16[2,170,1024]{2,0,1:T(2,128)(2,1)} %param.16) | copy-start | bytes 2088964
  38.3 1.3 copy-start.4
  187.2 1.9 copy-start
  190.4 1.6 copy-start.15
  192.0 1.8 copy-start.16
  270.1 1.6 copy-start.14
  272.2 2.2 copy-start.1
  275.2 2.3 copy-start.10
  275.2 2.2 copy-start.11
  276.8 29.6 %copy-start.13 = (f32[2,1024]{1,0:T(2,128)S(1)}, f32[2,1024]{1,0:T(2,128)}, u32[]{:S(2)}) copy-start(f32[2,1024]{1,0:T(2,128)} %param.18) | copy-start | bytes 24580
  305.4 10.0 %copy-start.9 = (f32[32,3072]{1,0:T(8,128)S(1)}, f32[32,3072]{1,0:T(8,128)}, u32[]{:S(2)}) copy-start(f32[32,3072]{1,0:T(8,128)} %get-tuple-element.182) | copy-start | bytes 1179652
  305.4 10.7 %copy-start.12 = (f32[1,32,1024]{2,1,0:T(8,128)S(1)}, f32[1,32,1024]{2,1,0:T(8,128)}, u32[]{:S(2)}) copy-start(f32[1,32,1024]{2,1,0:T(8,128)} %get-tuple-element.74) | copy-start | bytes 393220
  305.5 11.3 %copy-start.8 = (f32[32,4096]{1,0:T(8,128)S(1)}, f32[32,4096]{1,0:T(8,128)}, u32[]{:S(2)}) copy-start(f32[32,4096]{1,0:T(8,128)} %get-tuple-element.187) | copy-start | bytes 1572868
  315.4 2.2 copy-start.7

commit v5 on v4

--- a/solution.py
+++ b/solution.py
@@ -12,7 +12,7 @@
 bf16 = jnp.bfloat16
 f32 = jnp.float32
 VM = pltpu.VMEM
-LIMIT = 56 << 20
+LIMIT = 62 << 20
 
 
 class Plan:
@@ -142,15 +142,18 @@
     return Plan([x], out, scratch, two_level(axis, n), chunks, bind, pl.ANY)
 
 
-def scatter_ops(axis, rel, x_ref, out_ref, near_buf, send_buf, far_buf, s1, r1, s2, r2, inside=False):
+def scatter_ops(axis, rel, x_ref, out_ref, near_buf, send_buf, far_buf, s1, r1, s2, r2, inside=False, held=None):
     n = lax.axis_size(axis)
     outer = n // 2
     chunks = out_ref.shape[0]
     me = lax.axis_index(axis)
 
-    def part(j, c):
+    def part(j, c, ref=x_ref):
         block = j if rel else me ^ j
-        return x_ref.at[c, block] if inside else x_ref.at[block, c]
+        return ref.at[c, block] if inside else ref.at[block, c]
+
+    def mine(j, c):
+        return part(j, c, x_ref if held is None else held)[...].astype(f32)
 
     def near(o, c):
         return remote(part(2 * o + 1, c), near_buf.at[o, c], s1.at[o, c], r1.at[o, c], axis, me ^ 1)
@@ -175,14 +178,14 @@
     def step(c):
         for o in range(1, outer):
             near(o, c).wait_recv()
-            total = part(2 * o, c)[...].astype(f32) + near_buf[o, c].astype(f32)
+            total = mine(2 * o, c) + near_buf[o, c].astype(f32)
             send_buf[o, c] = total.astype(send_buf.dtype)
             far(o, c).start()
 
     def finish():
         def last(c):
             near(0, c).wait_recv()
-            total = part(0, c)[...].astype(f32) + near_buf[0, c].astype(f32)
+            total = mine(0, c) + near_buf[0, c].astype(f32)
             for o in range(1, outer):
                 far(o, c).wait_recv()
                 total = total + far_buf[o, c].astype(f32)
@@ -203,18 +206,6 @@
     half = VM((n // 2,) + inner, dtype)
     sems = pltpu.SemaphoreType.DMA((n // 2, inner[0]))
     return [half, half, half, sems, sems, sems, sems]
-
-
-def scatter_sum(x, axis, rel, dtype=jnp.float32, inside=False):
-    n = lax.axis_size(axis)
-    chunks = x.shape[0 if inside else 1]
-    inner = (chunks,) + x.shape[2:]
-
-    def bind(*refs):
-        return scatter_ops(axis, rel, *refs, inside=inside)
-
-    out = jax.ShapeDtypeStruct(inner, dtype)
-    return Plan([x], out, scatter_scratch(n, inner, x.dtype), two_level(axis, n), chunks, bind)
 
 
 class Session:
@@ -282,32 +273,59 @@
     return pltpu.CompilerParams(collective_id=cid, has_side_effects=True, vmem_limit_bytes=LIMIT)
 
 
-def opening(cid, mod_cut, attn_cut, exp_cut, small, images, plans):
-    seq_n, own, mod_l = mod_cut.shape
+def opening(cid, mod_w, attn_w, exp_w, out_w, small, seq_n, images, pairs, early):
+    raw = mod_w.dtype == f32
+    own, width = out_w.shape
+    dim_l = pairs * 128
     img_n, rows, _ = small.shape
+    cuts = [x.size // (seq_n * own) for x in (mod_w, attn_w, exp_w)]
+    mod_l, _, hid_l = cuts
+    hid_o = hid_l // img_n
     head = seq_n * images
     tiles = mod_l // 128
     slim = -(-tiles * images // 8) * 8
-    session = Session(plans)
-    session.peers = everyone_else("img", "seq")
-    ins, outs = 4 + len(session.ins), 6 + len(plans)
-
-    def kernel(*refs):
-        mod_ref, attn_ref, exp_ref, small_ref = refs[:4]
-        modo_ref, bias_ref, lhs_ref, modw_ref, attnw_ref, expw_ref = refs[ins : ins + 6]
-        small_all, part_buf, part_all, sum_buf = refs[ins + outs : ins + outs + 4]
-        sems = refs[ins + outs + 4 : ins + outs + 18]
+    count = max(early, 1)
+    shapes = [(seq_n, own, c) for c in cuts]
+    session = Session([], everyone_else("img", "seq"))
+
+    def kernel(
+        mod_in, attn_in, exp_in, out_in, small_ref,
+        modo_ref, bias_ref, lhs_ref, modw_ref, attnw_ref, expw_ref, early_ref, outw_ref,
+        small_all, part_buf, part_all, sum_buf, *more
+    ):
+        if raw:
+            mod_ref, attn_ref, exp_ref, out_ref, *sems = more
+            out_ref[0] = out_in[...].astype(bf16)
+            for q in range(seq_n):
+                mod_ref[q] = mod_in[:, q * mod_l : (q + 1) * mod_l].astype(bf16)
+        else:
+            mod_ref, attn_ref, exp_ref = mod_in, attn_in, exp_in
+            out_ref, *sems = more
+            out_ref[0] = out_in[...].astype(bf16)
+        early_in = gather_ops("img", False, attnw_ref.at[:count], early_ref, *sems[14:17])
+        out_go = gather_ops("img", False, out_ref, outw_ref, *sems[17:20])
         session.greet()
         small_go, small_end = direct_ops("img", small_ref, small_all, *sems[:2])
         mod_go, mod_end = direct_ops("seq", mod_ref, modw_ref, *sems[2:4])
         attn_go, attn_end = direct_ops("seq", attn_ref, attnw_ref, *sems[4:6])
         exp_go, exp_end = direct_ops("seq", exp_ref, expw_ref, *sems[12:14])
-        session.bind(refs[4:ins], refs[ins + 6 : ins + outs], refs[ins + outs + 18 :])
         small_go()
         mod_go()
+        if raw:
+            for q in range(seq_n):
+                for p in range(pairs):
+                    for k in range(3):
+                        at = k * width + q * dim_l + p * 128
+                        to = p * 384 + k * 128
+                        attn_ref[q, :, to : to + 128] = attn_in[:, at : at + 128].astype(bf16)
         attn_go()
+        if raw:
+            for q in range(seq_n):
+                for i in range(img_n):
+                    at = (i * seq_n + q) * hid_o
+                    exp_ref[q, :, i * hid_o : (i + 1) * hid_o] = exp_in[:, at : at + hid_o].astype(bf16)
         exp_go()
-        session.start()
+        out_go.start()
         part_buf[...] = jnp.zeros_like(part_buf)
         small_end()
         bias_go, bias_end = direct_ops("seq", small_all.at[:, head:], bias_ref, *sems[6:8], everyone=True)
@@ -326,7 +344,10 @@
                 ]
         part_go, part_end = direct_ops("img", part_buf, part_all, *sems[8:10])
         part_go()
-        session.steps(0, 1)
+        out_go.step(0)
+        attn_end()
+        if early:
+            early_in.start()
         part_end()
         total = part_all[0]
         for i in range(1, img_n):
@@ -334,39 +355,73 @@
         sum_buf[...] = total
         sum_go, sum_end = direct_ops("seq", sum_buf, modo_ref, *sems[10:12], everyone=True)
         sum_go()
+        if early:
+            each(0, early, early_in.step)
         bias_end()
         sum_end()
-        attn_end()
         exp_end()
-        session.finish()
+        out_go.finish()
+        if early:
+            early_in.finish()
 
     full = pl.BlockSpec(memory_space=VM)
+    any_space = pl.BlockSpec(memory_space=pl.ANY)
+    sending = [VM(x, bf16) for x in shapes] if raw else []
     return pl.pallas_call(
         kernel,
-        out_shape=tuple(
-            [
-                jax.ShapeDtypeStruct((seq_n, slim, 128), f32),
-                jax.ShapeDtypeStruct((seq_n, img_n, rows - head, 128), f32),
-                jax.ShapeDtypeStruct((seq_n, img_n * images, 128), f32),
-                jax.ShapeDtypeStruct(mod_cut.shape, bf16),
-                jax.ShapeDtypeStruct(attn_cut.shape, bf16),
-                jax.ShapeDtypeStruct(exp_cut.shape, bf16),
-            ]
-            + session.outs
+        out_shape=(
+            jax.ShapeDtypeStruct((seq_n, slim, 128), f32),
+            jax.ShapeDtypeStruct((seq_n, img_n, rows - head, 128), f32),
+            jax.ShapeDtypeStruct((seq_n, img_n * images, 128), f32),
+            *[jax.ShapeDtypeStruct(x, bf16) for x in shapes],
+            jax.ShapeDtypeStruct((img_n, count) + shapes[1][1:], bf16),
+            jax.ShapeDtypeStruct((img_n, 1, own, width), bf16),
         ),
-        in_specs=[full] * 4 + session.in_specs,
-        out_specs=tuple([full] * 6 + session.out_specs),
+        in_specs=[full] * 5,
+        out_specs=(full,) * 6 + (any_space,) * 2,
         scratch_shapes=[
             VM(small.shape, f32),
             VM((img_n, slim, 128), f32),
             VM((img_n, slim, 128), f32),
             VM((slim, 128), f32),
         ]
+        + sending
+        + [VM((1, own, width), bf16)]
         + pairs_of_sems("img", "seq", "seq", "seq", "img", "seq", "seq")
-        + session.scratch,
+        + [pltpu.SemaphoreType.DMA((count,))]
+        + [pltpu.SemaphoreType.DMA((img_n, count))] * 2
+        + [pltpu.SemaphoreType.DMA((1,))]
+        + [pltpu.SemaphoreType.DMA((img_n, 1))] * 2,
         compiler_params=params(cid),
         name="opening",
-    )(mod_cut, attn_cut, exp_cut, small, *session.ins)
+    )(mod_w, attn_w, exp_w, out_w, small)
+
+
+def finishing(modw, attnw, expw, bias, outw, shrw, heads):
+    own, width = outw.shape
+    hid_o = shrw.shape[0]
+
+    def kernel(modw_ref, attnw_ref, expw_ref, bias_ref, outw_ref, shrw_ref, *outs):
+        for src, out in zip((modw_ref, attnw_ref, expw_ref, outw_ref, shrw_ref), outs):
+            out[...] = src[...].astype(f32)
+        shift = (128 - lax.axis_index("seq") * own) % 128
+        rolled = pltpu.roll(bias_ref[...], shift, 1)
+        for row in range(4):
+            outs[5 + row][...] = rolled[row : row + 1, :own]
+        outs[9][...] = bias_ref[4:5, :hid_o]
+        outs[10][...] = bias_ref[5:6, :heads]
+
+    full = pl.BlockSpec(memory_space=VM)
+    shapes = [modw.shape, attnw.shape, expw.shape, outw.shape, shrw.shape] + [(1, own)] * 4 + [(1, hid_o), (1, heads)]
+    got = pl.pallas_call(
+        kernel,
+        out_shape=tuple(jax.ShapeDtypeStruct(x, f32) for x in shapes),
+        in_specs=[full] * 6,
+        out_specs=(full,) * len(shapes),
+        compiler_params=pltpu.CompilerParams(vmem_limit_bytes=LIMIT),
+        name="finishing",
+    )(modw, attnw, expw, bias, outw, shrw)
+    return list(got[:5]) + [x.reshape(-1) for x in got[5:]]
 
 
 def closing(cid, mine, expb, lhs, modw, back, images, pairs):
@@ -421,14 +476,14 @@
                 for k in range(3):
                     to = k * width + q * dim_l + p * 128
                     at_c = p * 384 + k * 128
-                    attn_own[:, to : to + 128] = back_all[q, :, at_c : at_c + 128].astype(f32)
+                    attn_own[:, to : to + 128] = back_all[q, :, at_c : at_c + 128]
             if aligned:
                 for i in range(img_n):
                     to = (i * seq_n + q) * hid_o
                     at_c = 3 * dim_l + i * hid_o
-                    exp_own[:, to : to + hid_o] = back_all[q, :, at_c : at_c + hid_o].astype(f32)
+                    exp_own[:, to : to + hid_o] = back_all[q, :, at_c : at_c + hid_o]
             else:
-                exp_own[:, q * hid_l : (q + 1) * hid_l] = back_all[q, :, 3 * dim_l :].astype(f32)
+                exp_own[:, q * hid_l : (q + 1) * hid_l] = back_all[q, :, 3 * dim_l :]
         img_end()
         sums = got[0]
         for i in range(1, img_n):
@@ -464,15 +519,15 @@
         cond_ref[...] = out
         mw_end()
         for q in range(seq_n):
-            modw_own[:, q * mod_l : (q + 1) * mod_l] = mw_recv[q].astype(f32)
+            modw_own[:, q * mod_l : (q + 1) * mod_l] = mw_recv[q]
 
     full = pl.BlockSpec(memory_space=VM)
     got = pl.pallas_call(
         kernel,
         out_shape=(
-            jax.ShapeDtypeStruct((own, mod_l * seq_n), f32),
-            jax.ShapeDtypeStruct((own, 3 * width), f32),
-            jax.ShapeDtypeStruct((own, hid_l * seq_n), f32),
+            jax.ShapeDtypeStruct((own, mod_l * seq_n), bf16),
+            jax.ShapeDtypeStruct((own, 3 * width), bf16),
+            jax.ShapeDtypeStruct((own, hid_l * seq_n), bf16),
             jax.ShapeDtypeStruct((8, 128), f32),
             jax.ShapeDtypeStruct((seq_n, flat, 128), f32),
             jax.ShapeDtypeStruct((img_n, head, 128), f32),
@@ -502,249 +557,6 @@
     return got
 
 
-def opening(cid, mod_cut, attn_cut, exp_cut, small, images, plans):
-    seq_n, own, mod_l = mod_cut.shape
-    img_n, rows, _ = small.shape
-    head = seq_n * images
-    tiles = mod_l // 128
-    slim = -(-tiles * images // 8) * 8
-    session = Session(plans)
-    session.peers = everyone_else("img", "seq")
-    ins, outs = 4 + len(session.ins), 6 + len(plans)
-
-    def kernel(*refs):
-        mod_ref, attn_ref, exp_ref, small_ref = refs[:4]
-        modo_ref, bias_ref, lhs_ref, modw_ref, attnw_ref, expw_ref = refs[ins : ins + 6]
-        small_all, part_buf, part_all, sum_buf = refs[ins + outs : ins + outs + 4]
-        sems = refs[ins + outs + 4 : ins + outs + 18]
-        session.greet()
-        small_go, small_end = direct_ops("img", small_ref, small_all, *sems[:2])
-        mod_go, mod_end = direct_ops("seq", mod_ref, modw_ref, *sems[2:4])
-        attn_go, attn_end = direct_ops("seq", attn_ref, attnw_ref, *sems[4:6])
-        exp_go, exp_end = direct_ops("seq", exp_ref, expw_ref, *sems[12:14])
-        session.bind(refs[4:ins], refs[ins + 6 : ins + outs], refs[ins + outs + 18 :])
-        small_go()
-        mod_go()
-        attn_go()
-        exp_go()
-        session.start()
-        part_buf[...] = jnp.zeros_like(part_buf)
-        small_end()
-        bias_go, bias_end = direct_ops("seq", small_all.at[:, head:], bias_ref, *sems[6:8], everyone=True)
-        bias_go()
-        for i in range(img_n):
-            for q in range(seq_n):
-                lhs_ref[q, i * images : (i + 1) * images] = small_all[i, q * images : (q + 1) * images]
-        mod_end()
-        part = jnp.zeros((img_n * images, mod_l), f32)
-        for q in range(seq_n):
-            part = part + dot(lhs_ref[q][:, :own].astype(bf16), modw_ref[q], ((1,), (0,)))
-        for i in range(img_n):
-            for t in range(tiles):
-                part_buf[i, t * images : (t + 1) * images] = part[
-                    i * images : (i + 1) * images, t * 128 : (t + 1) * 128
-                ]
-        part_go, part_end = direct_ops("img", part_buf, part_all, *sems[8:10])
-        part_go()
-        session.steps(0, 1)
-        part_end()
-        total = part_all[0]
-        for i in range(1, img_n):
-            total = total + part_all[i]
-        sum_buf[...] = total
-        sum_go, sum_end = direct_ops("seq", sum_buf, modo_ref, *sems[10:12], everyone=True)
-        sum_go()
-        bias_end()
-        sum_end()
-        attn_end()
-        exp_end()
-        session.finish()
-
-    full = pl.BlockSpec(memory_space=VM)
-    return pl.pallas_call(
-        kernel,
-        out_shape=tuple(
-            [
-                jax.ShapeDtypeStruct((seq_n, slim, 128), f32),
-                jax.ShapeDtypeStruct((seq_n, img_n, rows - head, 128), f32),
-                jax.ShapeDtypeStruct((seq_n, img_n * images, 128), f32),
-                jax.ShapeDtypeStruct(mod_cut.shape, bf16),
-                jax.ShapeDtypeStruct(attn_cut.shape, bf16),
-                jax.ShapeDtypeStruct(exp_cut.shape, bf16),
-            ]
-            + session.outs
-        ),
-        in_specs=[full] * 4 + session.in_specs,
-        out_specs=tuple([full] * 6 + session.out_specs),
-        scratch_shapes=[
-            VM(small.shape, f32),
-            VM((img_n, slim, 128), f32),
-            VM((img_n, slim, 128), f32),
-            VM((slim, 128), f32),
-        ]
-        + pairs_of_sems("img", "seq", "seq", "seq", "img", "seq", "seq")
-        + session.scratch,
-        compiler_params=params(cid),
-        name="opening",
-    )(mod_cut, attn_cut, exp_cut, small, *session.ins)
-
-
-def closing(cid, mine, expb, lhs, modw, back, images, pairs):
-    seq_n, own, mod_l = modw.shape
-    img_n = expb.shape[0]
-    rows = mine.shape[1]
-    head = seq_n * images
-    tiles = mod_l // 128
-    slim = -(-tiles * images // 8) * 8
-    share = img_n // seq_n
-    cut = back.shape[2]
-    dim_l = pairs * 128
-    width = dim_l * seq_n
-    hid_l = cut - 3 * dim_l
-    hid_o = hid_l // img_n
-    aligned = hid_o % 128 == 0
-    flat = -(-tiles // 8) * 8
-
-    def kernel(
-        mine_ref, expb_ref, lhs_ref, modw_ref, back_ref,
-        modw_own, attn_own, exp_own, bias_ref, modb_ref, cond_ref,
-        seen, block, got, dd, mw_send, mw_recv, mb_send, gs_send, gs_all, gs_seen, back_all, *sems
-    ):
-        barrier = Session([], everyone_else("img", "seq"))
-        barrier.greet()
-        mine_go, mine_end = direct_ops("seq", mine_ref, seen, *sems[:2])
-        back_go, back_end = direct_ops("seq", back_ref, back_all, *sems[2:4])
-        mine_go()
-        back_go()
-        block[...] = jnp.zeros_like(block)
-        gs_send[...] = jnp.zeros_like(gs_send)
-        mb_send[...] = jnp.zeros_like(mb_send)
-        mine_end()
-        total = seen[0]
-        for q in range(1, seq_n):
-            total = total + seen[q]
-        at = slim + 2 * img_n
-        for i in range(img_n):
-            block[i, :slim] = total[:slim]
-            block[i, slim : slim + 1] = total[slim + i : slim + i + 1]
-            block[i, slim + 1 : slim + 2] = total[slim + img_n + i : slim + img_n + i + 1]
-            row = at + 8 + i % share
-            block[i, slim + 2 : slim + 3] = seen[i // share, row : row + 1]
-            block[i, slim + 3 : slim + 4] = seen[i // share, row + share : row + share + 1]
-            block[i, slim + 4 : slim + 5] = expb_ref[i : i + 1]
-            block[i, slim + 5 : slim + 6] = total[at : at + 1]
-        img_go, img_end = direct_ops("img", block, got, *sems[4:6])
-        img_go()
-        back_end()
-        for q in range(seq_n):
-            for p in range(pairs):
-                for k in range(3):
-                    to = k * width + q * dim_l + p * 128
-                    at_c = p * 384 + k * 128
-                    attn_own[:, to : to + 128] = back_all[q, :, at_c : at_c + 128].astype(f32)
-            if aligned:
-                for i in range(img_n):
-                    to = (i * seq_n + q) * hid_o
-                    at_c = 3 * dim_l + i * hid_o
-                    exp_own[:, to : to + hid_o] = back_all[q, :, at_c : at_c + hid_o].astype(f32)
-            else:
-                exp_own[:, q * hid_l : (q + 1) * hid_l] = back_all[q, :, 3 * dim_l :].astype(f32)
-        img_end()
-        sums = got[0]
-        for i in range(1, img_n):
-            sums = sums + got[i]
-        bias_ref[...] = sums[slim:]
-        for t in range(tiles):
-            mb_send[t : t + 1] = jnp.sum(sums[t * images : (t + 1) * images], axis=0, keepdims=True)
-            for i in range(img_n):
-                dd[i * images : (i + 1) * images, t * 128 : (t + 1) * 128] = got[i, t * images : (t + 1) * images]
-        grad = dd[...]
-        high = grad.astype(bf16)
-        low = (grad - high.astype(f32)).astype(bf16)
-        for q in range(seq_n):
-            out = dot(high, modw_ref[q], ((1,), (1,))) + dot(low, modw_ref[q], ((1,), (1,)))
-            for i in range(img_n):
-                gs_send[i, q * images : (q + 1) * images, :own] = out[i * images : (i + 1) * images]
-        gs_go, gs_end = direct_ops("img", gs_send, gs_all, *sems[6:8])
-        gs_go()
-        for q in range(seq_n):
-            mw_send[q] = dot(lhs_ref[q][:, :own].astype(bf16), high, ((0,), (0,))).astype(bf16)
-        mb_go, mb_end = direct_ops("seq", mb_send, modb_ref, *sems[10:12], everyone=True)
-        mb_go()
-        gs_end()
-        all_go, all_end = direct_ops("seq", gs_all, gs_seen, *sems[12:14], everyone=True)
-        all_go()
-        mw_go, mw_end = direct_ops("seq", mw_send, mw_recv, *sems[8:10])
-        mw_go()
-        mb_end()
-        all_end()
-        out = gs_seen[0]
-        for q in range(1, seq_n):
-            out = out + gs_seen[q]
-        cond_ref[...] = out
-        mw_end()
-        for q in range(seq_n):
-            modw_own[:, q * mod_l : (q + 1) * mod_l] = mw_recv[q].astype(f32)
-
-    full = pl.BlockSpec(memory_space=VM)
-    got = pl.pallas_call(
-        kernel,
-        out_shape=(
-            jax.ShapeDtypeStruct((own, mod_l * seq_n), f32),
-            jax.ShapeDtypeStruct((own, 3 * width), f32),
-            jax.ShapeDtypeStruct((own, hid_l * seq_n), f32),
-            jax.ShapeDtypeStruct((8, 128), f32),
-            jax.ShapeDtypeStruct((seq_n, flat, 128), f32),
-            jax.ShapeDtypeStruct((img_n, head, 128), f32),
-        ),
-        in_specs=[full] * 5,
-        out_specs=(full,) * 6,
-        scratch_shapes=[
-            VM((seq_n, rows, 128), f32),
-            VM((img_n, slim + 8, 128), f32),
-            VM((img_n, slim + 8, 128), f32),
-            VM((img_n * images, mod_l), f32),
-            VM((seq_n, own, mod_l), bf16),
-            VM((seq_n, own, mod_l), bf16),
-            VM((flat, 128), f32),
-            VM((img_n, head, 128), f32),
-            VM((img_n, head, 128), f32),
-            VM((seq_n, img_n, head, 128), f32),
-            VM(back.shape, bf16),
-        ]
-        + pairs_of_sems("seq", "seq", "img", "img", "seq", "seq", "seq"),
-        compiler_params=params(cid),
-        name="closing",
-    )(mine, expb, lhs, modw, back)
-    got = list(got)
-    if not aligned:
-        got[2] = got[2].reshape(own, seq_n, img_n, hid_o).transpose(0, 2, 1, 3).reshape(own, hid_l * seq_n)
-    return got
-
-
-def exchange(cid, turns, *plans):
-    session = Session(plans)
-    ins, outs = len(session.ins), len(plans)
-
-    def kernel(*refs):
-        session.greet()
-        session.bind(refs[:ins], refs[ins : ins + outs], refs[ins + outs :])
-        session.start()
-        each(0, turns, lambda i: session.steps(i, turns))
-        session.finish()
-
-    got = pl.pallas_call(
-        kernel,
-        out_shape=tuple(session.outs),
-        in_specs=session.in_specs,
-        out_specs=tuple(session.out_specs),
-        scratch_shapes=session.scratch,
-        compiler_params=params(cid),
-        name=f"exchange_{cid}",
-    )(*session.ins)
-    return got[0] if len(plans) == 1 else got
-
-
 def half_sums(values, low_half):
     first = jnp.sum(jnp.where(low_half, values, 0.0), axis=-1, keepdims=True)
     second = jnp.sum(jnp.where(low_half, 0.0, values), axis=-1, keepdims=True)
@@ -770,7 +582,7 @@
     return query, key, value, low_half, r_query, r_key
 
 
-def attend(cid, attn_input, attn_own, bias, scale, sid_k, sid_q, out_img, exp_own, grad_own):
+def attend(cid, attn_input, attn_own, attn_early, early, bias, scale, sid_k, sid_q, out_img, exp_own, grad_own):
     seq_n, img_n = lax.axis_size("seq"), lax.axis_size("img")
     outer = seq_n // 2
     chunks, size, width = attn_input.shape
@@ -785,18 +597,22 @@
     w_chunks = attn_own.shape[0]
     plans = [gather(x, "seq", True) for x in grad_own] + [gather(out_img, "seq", False, True), gather(exp_own, "img", False)]
     session = Session(plans, everyone_else("seq") + two_level("img", img_n))
-    ins, outs = 6 + len(session.ins), 4 + len(plans)
+    ins, outs = 7 + len(session.ins), 4 + len(plans)
+    weight = (img_n, early + w_chunks) + attn_own.shape[1:]
 
     def kernel(*refs):
-        x_ref, w_ref, b_ref, es_ref, sk_ref, sq_ref = refs[:6]
+        x_ref, w_ref, early_ref, b_ref, es_ref, sk_ref, sq_ref = refs[:7]
         o_ref, p_out, h_out, w_out = refs[ins : ins + 4]
         scratch = refs[ins + outs :]
-        h1, attn_w, packed, k_buf, v_buf, o_buf, o_send, o_recv, hs, hr, wk, ws, wr, out_sem = scratch[:14]
+        h1, attn_w, packed, o_buf, o_send, o_recv, hs, hr, wk, ws, wr, out_sem, early_sem = scratch[:13]
         me = lax.axis_index("seq")
         session.greet()
-        session.bind(refs[6:ins], refs[ins + 4 : ins + outs], scratch[14:])
+        session.bind(refs[7:ins], refs[ins + 4 : ins + outs], scratch[13:])
         h1_in = gather_ops("seq", True, x_ref, h1, None, hs, hr)
-        w_in = gather_ops("img", False, w_ref, attn_w, wk, ws, wr)
+        w_in = gather_ops("img", False, w_ref, attn_w.at[:, early:], wk, ws, wr)
+        if early:
+            load = pltpu.make_async_copy(early_ref, attn_w.at[:, :early], early_sem.at[0])
+            load.start()
         h1_in.start()
         w_in.start()
         session.start()
@@ -825,6 +641,8 @@
         for o in range(1, img_n // 2):
             w_in.handed(o)
         w_in.sent()
+        if early:
+            load.wait()
         quarter = exp_count // 4
         each(0, quarter, exp_in.step)
 
@@ -847,29 +665,22 @@
             g, p = i // pairs, i % pairs
             query, key, value, low_half, r_query, r_key = load_heads(packed, b_ref[p], g, p, rows)
             query_low = query * r_query * es_ref[p]
-            k_buf[...] = (key * r_key).astype(bf16).reshape(seq_n, rows_b, 128)
-            v_buf[...] = value.astype(bf16).reshape(seq_n, rows_b, 128)
-            sid_q = sq_ref[g]
-            parts = []
-            for h in range(2):
-                mine = low_half if h == 0 else jnp.logical_not(low_half)
-                q_t = jnp.transpose(jnp.where(mine, query_low, 0.0)).astype(bf16)
-
-                def step(b, carry, q_t=q_t):
-                    total, acc = carry
-                    scores = dot(k_buf[b], q_t, ((1,), (0,)))
-                    expo = jnp.where(sk_ref[g, b] <= sid_q, jnp.exp(scores), 0.0)
-                    total = total + jnp.sum(expo, axis=0, keepdims=True)
-                    acc = acc + dot(v_buf[b], expo.astype(bf16), ((0,), (0,)))
-                    return total, acc
-
-                total, acc = lax.fori_loop(
-                    0, seq_n, step, (jnp.zeros((1, rows), f32), jnp.zeros((128, rows), f32))
-                )
-                parts.append((acc / total)[64 * h : 64 * h + 64])
-            out = jnp.transpose(jnp.concatenate(parts, axis=0)).astype(bf16).reshape(seq_n, rows_b, 128)
-            o_buf[i] = out
-            o_ref[g, :, lanes((me * pairs + p) * 128, 128)] = out[0]
+            key_t = jnp.transpose(key * r_key).astype(bf16)
+            sid_k = sq_ref[g]
+            masks = [low_half, jnp.logical_not(low_half)]
+            queries = [jnp.where(mine, query_low, 0.0).astype(bf16) for mine in masks]
+            values = [jnp.where(mine, value, 1.0).astype(bf16) for mine in masks]
+            low_b = low_half[:rows_b]
+            for b in range(seq_n):
+                seen = sid_k <= sk_ref[g, b]
+                parts = []
+                for h in range(2):
+                    scores = dot(queries[h][b * rows_b : (b + 1) * rows_b], key_t, ((1,), (0,)))
+                    expo = jnp.where(seen, jnp.exp(scores), 0.0).astype(bf16)
+                    parts.append(dot(expo, values[h], ((1,), (0,))))
+                totals = jnp.where(low_b, pltpu.roll(parts[0], 64, 1), pltpu.roll(parts[1], 64, 1))
+                o_buf[i, b] = (jnp.where(low_b, parts[0], parts[1]) / totals).astype(bf16)
+            o_ref[g, :, lanes((me * pairs + p) * 128, 128)] = o_buf[i, 0]
             for j in range(1, seq_n):
                 ship(i, j).start()
 
@@ -914,18 +725,16 @@
                 jax.ShapeDtypeStruct((images, rows_b, width), bf16),
                 jax.ShapeDtypeStruct(packed, f32),
                 jax.ShapeDtypeStruct((seq_n,) + attn_input.shape, bf16),
-                jax.ShapeDtypeStruct((img_n,) + attn_own.shape, bf16),
+                jax.ShapeDtypeStruct(weight, bf16),
             ]
             + session.outs
         ),
-        in_specs=[full] * 6 + session.in_specs,
+        in_specs=[full] * 2 + [any_space] + [full] * 4 + session.in_specs,
         out_specs=tuple([full] + [any_space] * 3 + session.out_specs),
         scratch_shapes=[
             VM((seq_n,) + attn_input.shape, bf16),
-            VM((img_n,) + attn_own.shape, bf16),
+            VM(weight, bf16),
             VM(packed, f32),
-            VM((seq_n, rows_b, 128), bf16),
-            VM((seq_n, rows_b, 128), bf16),
             VM((turns, seq_n, rows_b, 128), bf16),
             sems,
             sems,
@@ -935,11 +744,12 @@
             img_sems,
             img_sems,
             pltpu.SemaphoreType.DMA((3,)),
+            pltpu.SemaphoreType.DMA((1,)),
         ]
         + session.scratch,
         compiler_params=params(cid),
         name="attend",
-    )(attn_input, attn_own, bias, scale, sid_k, sid_q, *session.ins)
+    )(attn_input, attn_own, attn_early, bias, scale, sid_k, sid_q, *session.ins)
 
 
 def attend_back(cid, packed, h1, attn_w, d_out, bias, scale, sid_k, sid_q, expw_part, shrunk_part, outw_part):
@@ -971,7 +781,8 @@
         scratch = refs[17:]
         p_ref, h_ref, w_ref, dp_ref, dh1, dattn, out_mid, load_sem = scratch[:8]
         k_buf, v_buf, e_buf, g_buf, dk_buf, dv_buf, do_buf, o_send, o_recv = scratch[8:17]
-        more = scratch[17:]
+        expw_held, f_held, outw_held = scratch[17:20]
+        more = scratch[20:]
         me = lax.axis_index("seq")
         session.greet()
 
@@ -993,13 +804,24 @@
         each(0, turns, send)
         loads = [
             pltpu.make_async_copy(src, dst, load_sem.at[n])
-            for n, (src, dst) in enumerate(((p_in, p_ref), (h_in, h_ref), (w_in, w_ref)))
+            for n, (src, dst) in enumerate(
+                (
+                    (p_in, p_ref),
+                    (outw_ref, outw_held),
+                    (f_ref, f_held),
+                    (expw_ref, expw_held),
+                    (h_in, h_ref),
+                    (w_in, w_ref),
+                )
+            )
         ]
         for load in loads:
             load.start()
-        exp_out = scatter_ops("img", False, expw_ref, expw_own, *more[:7])
-        f_out = scatter_ops("seq", True, f_ref, f_own, *more[7:14])
-        mid_out = scatter_ops("seq", False, outw_ref, out_mid.at[:, 0], *more[14:21], inside=True)
+        exp_out = scatter_ops("img", False, expw_ref, expw_own, *more[:7], held=expw_held)
+        f_out = scatter_ops("seq", True, f_ref, f_own, *more[7:14], held=f_held)
+        mid_out = scatter_ops(
+            "seq", False, outw_ref, out_mid.at[:, 0], *more[14:21], inside=True, held=outw_held
+        )
         outw_out = scatter_ops("img", False, out_mid, outw_own, *more[21:28])
         attn_out = scatter_ops("img", False, dattn, attn_own, *more[28:35])
         dh1_out = scatter_ops("seq", True, dh1, dh1_own, *more[35:42])
@@ -1023,47 +845,39 @@
                 ship(i, j).wait_recv()
             d_out = do_buf[i].reshape(rows, 128).astype(f32)
             sid_q = sq_ref[g]
-            parts = []
-            for h in range(2):
-                mine = low_half if h == 0 else jnp.logical_not(low_half)
-                q_f = jnp.where(mine, q_full, 0.0)
-                do_f = jnp.where(mine, d_out, 0.0)
-                q_h = q_f.astype(bf16)
-                do_h = do_f.astype(bf16)
-                q_t = jnp.transpose(q_f).astype(bf16)
-                do_t = jnp.transpose(do_f).astype(bf16)
-
-                def first(b, carry, q_t=q_t, do_t=do_t):
-                    total, mixed = carry
-                    scores = dot(k_buf[b], q_t, ((1,), (0,)))
-                    expo = jnp.where(sk_ref[g, b] <= sid_q, jnp.exp(scores), 0.0)
-                    grad = dot(v_buf[b], do_t, ((1,), (0,)))
-                    e_buf[b] = expo
-                    g_buf[b] = grad
-                    total = total + jnp.sum(expo, axis=0, keepdims=True)
-                    mixed = mixed + jnp.sum(expo * grad, axis=0, keepdims=True)
-                    return total, mixed
-
-                zero = jnp.zeros((1, rows), f32)
-                total, mixed = lax.fori_loop(0, seq_n, first, (zero, zero))
-                inverse = 1.0 / total
-                delta = mixed * inverse
-
-                def second(b, acc, inverse=inverse, delta=delta, q_h=q_h, do_h=do_h, h=h):
-                    probs = e_buf[b] * inverse
-                    scores_grad = (probs * (g_buf[b] - delta)).astype(bf16)
-                    dv = dot(probs.astype(bf16), do_h, ((1,), (0,)))
-                    dk = dot(scores_grad, q_h, ((1,), (0,)))
-                    if h == 0:
-                        dv_buf[b] = dv
-                        dk_buf[b] = dk
-                    else:
-                        dv_buf[b] = dv_buf[b] + dv
-                        dk_buf[b] = dk_buf[b] + dk
-                    return acc + dot(k_buf[b], scores_grad, ((0,), (0,)))
-
-                acc = lax.fori_loop(0, seq_n, second, jnp.zeros((128, rows), f32))
-                parts.append(acc[64 * h : 64 * h + 64])
+            masks = [low_half, jnp.logical_not(low_half)]
+            q_f = [jnp.where(mine, q_full, 0.0) for mine in masks]
+            do_f = [jnp.where(mine, d_out, 0.0) for mine in masks]
+            q_h = [x.astype(bf16) for x in q_f]
+            do_h = [x.astype(bf16) for x in do_f]
+            q_t = [jnp.transpose(x).astype(bf16) for x in q_f]
+            do_t = [jnp.transpose(x).astype(bf16) for x in do_f]
+            total = [jnp.zeros((1, rows), f32)] * 2
+            mixed = [jnp.zeros((1, rows), f32)] * 2
+            for b in range(seq_n):
+                seen = sk_ref[g, b] <= sid_q
+                for h in range(2):
+                    scores = dot(k_buf[b], q_t[h], ((1,), (0,)))
+                    expo = jnp.where(seen, jnp.exp(scores), 0.0)
+                    grad = dot(v_buf[b], do_t[h], ((1,), (0,)))
+                    e_buf[h, b] = expo
+                    g_buf[h, b] = grad
+                    total[h] = total[h] + jnp.sum(expo, axis=0, keepdims=True)
+                    mixed[h] = mixed[h] + jnp.sum(expo * grad, axis=0, keepdims=True)
+            inverse = [1.0 / x for x in total]
+            delta = [x * y for x, y in zip(mixed, inverse)]
+            acc = [jnp.zeros((128, rows), f32)] * 2
+            for b in range(seq_n):
+                dv = dk = jnp.zeros((rows_b, 128), f32)
+                for h in range(2):
+                    probs = e_buf[h, b] * inverse[h]
+                    scores_grad = (probs * (g_buf[h, b] - delta[h])).astype(bf16)
+                    dv = dv + dot(probs.astype(bf16), do_h[h], ((1,), (0,)))
+                    dk = dk + dot(scores_grad, q_h[h], ((1,), (0,)))
+                    acc[h] = acc[h] + dot(k_buf[b], scores_grad, ((0,), (0,)))
+                dv_buf[b] = dv
+                dk_buf[b] = dk
+            parts = [acc[0][:64], acc[1][64:]]
             dq = jnp.transpose(jnp.concatenate(parts, axis=0)).astype(bf16).astype(f32)
             dk = dk_buf[...].reshape(rows, 128).astype(bf16).astype(f32)
             dv = dv_buf[...].reshape(rows, 128).astype(bf16).astype(f32)
@@ -1081,6 +895,8 @@
 
             @pl.when(i == 0)
             def _():
+                for load in loads[1:4]:
+                    load.wait()
                 each(0, img_n, mid_out.step)
                 each(0, chunks, f_out.step)
 
@@ -1089,7 +905,7 @@
         each(0, turns, turn)
         mid_out.finish()
         outw_out.start()
-        for load in loads[1:]:
+        for load in loads[4:]:
             load.wait()
 
         def columns(t):
@@ -1120,10 +936,11 @@
         dh1_out.start_outer()
         each(0, chunks, dh1_out.step)
         each(0, w_chunks // 2, attn_out.step)
-        for j in (1, 0):
-            input_grad(j)
+        input_grad(1)
+        each(w_chunks // 2, (3 * w_chunks) // 4, attn_out.step)
+        input_grad(0)
         dh1_out.start_inner()
-        each(w_chunks // 2, w_chunks, attn_out.step)
+        each((3 * w_chunks) // 4, w_chunks, attn_out.step)
         outw_out.finish()
         f_out.finish()
         dh1_out.finish()
@@ -1148,7 +965,7 @@
             jax.ShapeDtypeStruct(shrunk_part.shape[1:], f32),
             jax.ShapeDtypeStruct((1, own, width), f32),
         ),
-        in_specs=[any_space] * 3 + [full] * 8,
+        in_specs=[any_space] * 3 + [full] * 5 + [any_space] * 3,
         out_specs=(full,) * 6,
         scratch_shapes=[
             VM(packed.shape, f32),
@@ -1158,16 +975,19 @@
             VM(h1.shape, bf16),
             VM(attn_w.shape, bf16),
             VM((img_n, 1, own, width), bf16),
-            pltpu.SemaphoreType.DMA((3,)),
+            pltpu.SemaphoreType.DMA((6,)),
             VM((seq_n, rows_b, 128), bf16),
             VM((seq_n, rows_b, 128), bf16),
-            VM((seq_n, rows_b, rows), f32),
-            VM((seq_n, rows_b, rows), f32),
+            VM((2, seq_n, rows_b, rows), f32),
+            VM((2, seq_n, rows_b, rows), f32),
             VM((seq_n, rows_b, 128), f32),
             VM((seq_n, rows_b, 128), f32),
             VM((turns, seq_n, rows_b, 128), bf16),
             sems,
             sems,
+            VM(expw_part.shape, bf16),
+            VM(shrunk_part.shape, bf16),
+            VM(outw_part.shape, bf16),
         ]
         + [x for scratch in mids for x in scratch],
         compiler_params=params(cid),
@@ -1202,14 +1022,15 @@
     def kernel(x_ref, *refs):
         df_refs = refs[:images]
         shr_ref, exp_ref, eb_ref, dh2_ref, dshr_own, f_ref, dexp_ref, expb_ref = refs[images : images + 8]
-        h2, df, shr, act, slope, dshr, dh2, df_sem, hs, hr, ss, sr, sk, *more = refs[images + 8 :]
+        h2, df, shr, act, slope, dshr, dh2, df_sem, hs, hr, ss, sr, sk, shr_low, *more = refs[images + 8 :]
+        shr_low[...] = shr_ref[...].astype(bf16)
         df_in = [
             gather_ops("seq", True, df_refs[ready + g], df.at[:, ready + g], *more[14 + 3 * g : 17 + 3 * g])
             for g in range(later)
         ]
         session.greet()
         h2_in = gather_ops("seq", True, x_ref, h2, None, hs, hr)
-        shr_in = gather_ops("img", False, shr_ref, shr, sk, ss, sr)
+        shr_in = gather_ops("img", False, shr_low, shr, sk, ss, sr)
         dh2_out = scatter_ops("seq", True, dh2, dh2_ref, *more[:7])
         dshr_out = scatter_ops("img", False, dshr, dshr_own, *more[7:14])
         h2_in.start()
@@ -1300,16 +1121,23 @@
             for j in (2 * o + 1, 2 * o):
                 back_act(j)
                 back_input(j)
+        def dshr_steps(k):
+            each((k * w_chunks) // 4, ((k + 1) * w_chunks) // 4, dshr_out.step)
+
         dh2_out.start_outer()
+        dshr_steps(0)
         each(0, chunks, dh2_out.step)
-        each(0, w_chunks // 2, dshr_out.step)
-        for j in (1, 0):
-            back_act(j)
-            back_input(j)
+        back_act(1)
+        dshr_steps(1)
+        back_input(1)
+        back_act(0)
+        dshr_steps(2)
+        back_input(0)
         dh2_out.start_inner()
-        each(w_chunks // 2, w_chunks, dshr_out.step)
+        shrink(0)
+        dshr_steps(3)
         h2_in.sent()
-        for j in range(seq_n):
+        for j in range(1, seq_n):
             shrink(j)
         each(0, width // tile, expand_grad)
         dh2_out.finish()
@@ -1345,6 +1173,7 @@
             img_sems,
             img_sems,
             pltpu.SemaphoreType.DMA((w_chunks,)),
+            VM(shr_own.shape, bf16),
         ]
         + scatter_scratch(seq_n, mlp_input.shape, bf16)
         + scatter_scratch(img_n, shr_own.shape, bf16)
@@ -1421,19 +1250,22 @@
     mod_l = mods // seq_n
     blk = own * seq_n
 
-    attn_cut = (
-        attn_weight.astype(bf16)
-        .reshape(own, 3, seq_n, pairs, 128)
-        .transpose(2, 0, 3, 1, 4)
-        .reshape(seq_n, own, 3 * dim_l)
-    )
-    exp_cut = (
-        expand_weight.astype(bf16)
-        .reshape(own, img_n, seq_n, hid_o)
-        .transpose(2, 0, 1, 3)
-        .reshape(seq_n, own, hid_l)
-    )
-    mod_cut = mod_weight.astype(bf16).reshape(own, seq_n, mod_l).transpose(1, 0, 2)
+    weights = (mod_weight, attn_weight, expand_weight)
+    if own % 16 or hid_o % 128:
+        attn_cut = (
+            attn_weight.astype(bf16)
+            .reshape(own, 3, seq_n, pairs, 128)
+            .transpose(2, 0, 3, 1, 4)
+            .reshape(seq_n, own, 3 * dim_l)
+        )
+        exp_cut = (
+            expand_weight.astype(bf16)
+            .reshape(own, img_n, seq_n, hid_o)
+            .transpose(2, 0, 1, 3)
+            .reshape(seq_n, own, hid_l)
+        )
+        mod_cut = mod_weight.astype(bf16).reshape(own, seq_n, mod_l).transpose(1, 0, 2)
+        weights = (mod_cut, attn_cut, exp_cut)
     silu_cond = jax.nn.silu(condition).astype(bf16).astype(f32)
     small_bias = jnp.concatenate([query_bias, value_bias, out_bias, shrink_bias, expand_bias, mod_bias])
     small_bias = lax.reduce_precision(small_bias, 8, 7)
@@ -1444,25 +1276,21 @@
     small = jnp.concatenate(
         [pad_to(cond_cut, 128, 2), jnp.broadcast_to(small_bias, (img_n, bias_rows, 128))], axis=1
     )
-    mod_all, bias_all, cond_rows, modw_cut, attn_b, exp_b, out_img = opening(
-        1,
-        mod_cut,
-        attn_cut,
-        exp_cut,
-        small,
-        images,
-        [gather(out_weight.astype(bf16)[None], "img", False)],
+    early = seq_n // 4 if own % 16 == 0 else 0
+    mod_all, bias_all, cond_rows, modw_cut, attn_b, exp_b, attn_early, out_img = opening(
+        1, *weights, out_weight, small, seq_n, images, pairs, early
     )
     out_img = out_img.reshape(img_n, own, width)
-    attn_b = attn_b.reshape(blk, 3 * dim_l)
+    if early:
+        attn_b = attn_b[early:]
     exp_b = exp_b.reshape(blk, hid_l)
 
     def weight_chunks(x):
-        step = max(blk // 4, 8)
+        step = blk // 8 if blk % 128 == 0 else blk // 4
         return x.reshape(x.shape[:-2] + (blk // step, step, x.shape[-1]))
 
     def hidden_chunks(x):
-        step = max(hid_o // 4, 16)
+        step = 16
         return x.reshape(x.shape[:-2] + (hid_o // step, step, x.shape[-1]))
 
     tiles = mod_l // 128
@@ -1485,12 +1313,14 @@
         modulation[:, None, :], 6, axis=-1
     )
 
-    ends = jnp.cumsum(scale_sizes, axis=-1)
+    scales = jnp.arange(scale_sizes.shape[1])
+    ends = jnp.sum(jnp.where(scales[:, None] <= scales[None], scale_sizes[:, :, None], 0), axis=1)
     offset = jnp.arange(rows_p, dtype=jnp.int32)
     place = (seq_i ^ jnp.arange(seq_n, dtype=jnp.int32))[:, None] * rows + offset[None]
     sid = jnp.sum((place[None, :, :, None] >= ends[:, None, None, :]).astype(jnp.int32), axis=-1)
+    sid = jnp.where(offset[None, None] < rows, sid, 1 << 20)
     sid_q = sid.reshape(images, 1, seq_n * rows_p)
-    sid_k = jnp.where(offset[None, None] < rows, sid, 1 << 20)[..., None]
+    sid_k = sid[..., None]
 
     resid_in = pad_to(tokens, rows_p, 1).astype(f32)
     grad_out = pad_to(cotangent, rows_p, 1).astype(f32)
@@ -1507,7 +1337,9 @@
     context_low, packed, h1, attn_w, *gathered = attend(
         5,
         chunked(attn_input),
-        weight_chunks(attn_b),
+        attn_b if early else weight_chunks(attn_b.reshape(blk, 3 * dim_l)),
+        attn_early,
+        early,
         pair_bias,
         pair_scale,
         sid_k,
@@ -1530,7 +1362,7 @@
         chunked(mlp_input),
         df_ready,
         [grad_chunks[g] for g in range(ready, images)],
-        hidden_chunks(shrink_weight.astype(bf16)),
+        hidden_chunks(shrink_weight),
         exp_w,
         e_bias.reshape(1, hid_l),
     )
@@ -1564,7 +1396,7 @@
         outw_part,
     )
     shrunk = shrunk.reshape(images, rows_p, width) + s_bias
-    layer_out = (resid_mid + gain_mlp * shrunk).astype(bf16)
+    layer_out = (resid_mid[:, :rows] + gain_mlp * shrunk[:, :rows]).astype(bf16)
     grad_gain_mlp = jnp.sum(grad_out * shrunk, axis=1)
     sums = jnp.sum(sums.reshape(images, pairs, 8, 128), axis=0)
     qb_part = sums[:, 0].reshape(dim_l)
@@ -1574,7 +1406,7 @@
     grad_attn_input = grad_attn_input.reshape(images, rows_p, width)
     grad_scale_attn = jnp.sum(grad_attn_input * normed_in, axis=1)
     grad_shift_attn = jnp.sum(grad_attn_input, axis=1)
-    token_grad = grad_mid + norm_back(resid_in, grad_attn_input * (1.0 + scale_attn))
+    token_grad = grad_mid[:, :rows] + norm_back(resid_in[:, :rows], grad_attn_input[:, :rows] * (1.0 + scale_attn))
     token_grad = token_grad.astype(bf16)
 
     grad_mod = jnp.concatenate(
@@ -1607,18 +1439,15 @@
         13, mine, lined(expb_part, img_n), cond_rows, modw_cut, back_cut, images, pairs
     )
 
-    def part_of(row):
-        return lax.dynamic_slice_in_dim(bias_own[row], seq_i * own, own, 0)
-
-    shrb_own, outb_own, qb_own, vb_own = part_of(0), part_of(1), part_of(2), part_of(3)
-    expb_own = bias_own[4, :hid_o]
-    logs_total = bias_own[5, :heads]
+    modw_own, attnw_own, expw_own, outw_own, shrw_own, shrb_own, outb_own, qb_own, vb_own, expb_own, logs_total = finishing(
+        modw_own, attnw_own, expw_own, bias_own, outw_own, shrw_own, heads
+    )
     modb_own = lax.dynamic_slice_in_dim(modb_all[:, :tiles].reshape(mods), rank * mod_o, mod_o, 0)
     grad_silu = cond_sum[:, :, :own].reshape(img_n, seq_n, images, own).transpose(2, 0, 1, 3).reshape(images, width)
     cond_grad = jax.vjp(jax.nn.silu, condition)[1](grad_silu)[0]
     return (
-        layer_out[:, :rows],
-        token_grad[:, :rows],
+        layer_out,
+        token_grad,
         cond_grad,
         modw_own,
         modb_own,

time: 319 us -> 299 us (0.937)
  local copies, waits for them, and re-layouts: 27 us -> 15.5 us
  Pallas kernels: 261 us -> 252 us
    pallas_call x1, Pallas kernels: 63.3 us -> 55.7 us  [attend(): pl.pallas_call(kernel, out_shape=tuple([jax.ShapeDtypeStruct((images, row...]
    pallas_call x1 -> x2, Pallas kernels: 22.6 us -> 29.4 us  [the longest x1 26.5 us: opening(): pl.pallas_call(kernel, out_shape=(jax.ShapeDtypeStruct((seq_n, slim, 128)...]
    pallas_call x1, Pallas kernels: 71.5 us -> 67.9 us  [attend_back(): pl.pallas_call(kernel, out_shape=(jax.ShapeDtypeStruct((turns, 8, 128), f...]
    reshape x8 -> x0, local copies, waits for them, and re-layouts: 3.55 us -> none  [the longest x3 1.07 us: body(): attn_cut = attn_weight.astype(bf16).reshape(own, 3, seq_n, pairs, 128).tr...]
    unnamed x49 -> x61, local copies, waits for them, and re-layouts: 10 us -> 8.32 us
where the time goes in v5:
time: 299 us; the launch traced here: 298 us
  Pallas kernels  252 us (84%)
  other arithmetic  21.9 us (7%)
  local copies, waits for them, and re-layouts  15.5 us (5%)
  matrix products  7.21 us (2%)
    pallas_call x1, Pallas kernels, feed_forward(): pl.pallas_call(kernel, out_shape=(jax.ShapeDtypeStruct(mlp_input.shape, f...  73 us
    pallas_call x1, Pallas kernels, attend_back(): pl.pallas_call(kernel, out_shape=(jax.ShapeDtypeStruct((turns, 8, 128), f...  67.9 us
    pallas_call x1, Pallas kernels, attend(): pl.pallas_call(kernel, out_shape=tuple([jax.ShapeDtypeStruct((images, row...  55.7 us
    pallas_call x1, Pallas kernels, opening(): pl.pallas_call(kernel, out_shape=(jax.ShapeDtypeStruct((seq_n, slim, 128)...  26.5 us
    pallas_call x1, Pallas kernels, closing(): pl.pallas_call(kernel, out_shape=(jax.ShapeDtypeStruct((own, mod_l * seq_...  26.3 us
    unnamed x61, local copies, waits for them, and re-layouts  8.32 us

profile of v5, /device:TPU:1, one launch (start us, length us, event | category | flops | bytes accessed | tf_op | source)
XLA Modules:
  0.0 297.9 jit_solution(14535792953499350378)
XLA Ops:
  0.7 0.7 multiply_convert_fusion.1
  1.5 0.8 concatenate.21
  3.0 26.5 %opening.1 = (f32[4,24,128]{2,1,0:T(8,128)}, f32[4,8,8,128]{3,2,1,0:T(8,128)}, f32[4,16,128]{2,1,0:T(8,128)}, bf16[4,32,1536]{2,1,0:T(8,128)(2,1)}, bf16[4,32,76...) custom-call(f32[32,6144]{1,0:T(8,128)} %mod_in.1, ...), custom_call_target="tpu_custom_call" | custom-call | tf_op jit(solution)/shard_map/opening/pallas_call | solution.py:370
  29.5 0.9 reshape.347
  31.6 0.8 broadcast_add_fusion.1
  33.2 1.2 add_convert_fusion.1
  34.6 0.6 dynamic_slice.17
  35.6 0.9 fusion.17
  37.3 1.0 broadcast_select_fusion.refs_5_.refs_6_
  39.0 0.7 slice.64.refs_1_
  39.7 55.7 %attend.1 = (bf16[2,176,1024]{2,1,0:T(8,128)(2,1)}, f32[4,2,176,768]{3,2,1,0:T(8,128)}, bf16[4,11,32,1024]{3,2,1,0:T(8,128)(2,1)}, bf16[8,4,32,768]{3,2,1,0:T(8,...) custom-call(bf16[11,32,1024]{2,1,0:T(8,128)(2,1)} %bitcast.94, ...), custom_call_target="tpu_custom_call" | custom-call | tf_op jit(solution)/shard_map/attend/pallas_call | solution.py:721
  95.4 2.8 convolution_add_fusion
  98.5 0.8 copy-done.12
  99.7 1.2 add_convert_fusion
  101.4 73.0 %feed_forward.1 = (f32[11,32,1024]{2,1,0:T(8,128)}, f32[8,16,1024]{2,1,0:T(8,128)}, bf16[4,11,32,1024]{3,2,1,0:T(8,128)(2,1)}, bf16[1024,1024]{1,0:T(8,128)(2,1)}, f32[1,1024]{1,0:T(1,128)}) custom-call(bf16[11,32,1024]{2,1,0:T(8,128)(2,1)} %bitcast.95, bf16[4,11,16,1024]{3,2,1,0:T(8,128)(2,1)} %get-tuple-element.69.refs_0_, ...), custom_call_target="tpu_custom_call" | custom-call | tf_op jit(solution)/shard_map/feed_forward/pallas_call | solution.py:1151
  174.4 1.9 fusion.13
  176.4 0.7 multiply_reduce_fusion
  177.9 0.7 multiply_reduce_fusion.2
  178.9 1.4 copy-done.23
  180.2 2.6 bitcast_convert_fusion
  182.9 1.8 convolution_convert_fusion
  184.7 67.9 %attend_back.1 = (f32[4,8,128]{2,1,0:T(8,128)}, f32[11,32,1024]{2,1,0:T(8,128)}, bf16[4,32,768]{2,1,0:T(8,128)(2,1)}, bf16[8,16,1024]{2,1,0:T(8,128)(2,1)}, f32[...) custom-call(f32[4,2,176,768]{3,2,1,0:T(8,128)} %get-tuple-element.66.refs_0_, ...), custom_call_target="tpu_custom_call" | custom-call | tf_op jit(solution)/shard_map/attend_back/pallas_call | solution.py:958
  252.6 1.9 pad_maximum_fusion.back_ref
  254.6 3.0 fusion.1
  258.8 0.7 pad_maximum_fusion.1.mine_ref
  259.4 26.3 %closing.1 = (bf16[32,6144]{1,0:T(8,128)(2,1)}, bf16[32,3072]{1,0:T(8,128)(2,1)}, bf16[32,4096]{1,0:T(8,128)(2,1)}, f32[8,128]{1,0:T(8,128)}, f32[4,16,128]{2,1,0:T(8,128)}, /*index=5*/f32[8,8,128]{2,1,0:T(8,128)}) custom-call(f32[4,56,128]{2,1,0:T(8,128)} %pad_maximum_fusion.1.mine_ref, f32[8,128]{1,0:T(8,128)} %bitcast.124, ...), custom_call_target="tpu_custom_call" | custom-call | tf_op jit(solution)/shard_map/closing/pallas_call | solution.py:525
  285.8 2.9 finishing.1
  290.1 1.4 pad_convert_fusion
  292.7 0.8 copy-done.6
  294.0 0.8 fusion.2
  294.8 1.6 copy.66
  296.4 1.6 copy.67
  (128 shorter events, 11.4 us)
Async XLA Ops:
  3.0 29.5 %copy-start.14 = (bf16[2,170,1024]{2,0,1:T(2,128)(2,1)S(1)}, bf16[2,170,1024]{2,0,1:T(2,128)(2,1)}, u32[]{:S(2)}) copy-start(bf16[2,170,1024]{2,0,1:T(2,128)(2,1)} %param.16) | copy-start | bytes 2088964
  32.6 1.8 copy-start
  32.7 1.8 copy-start.24
  32.7 2.6 copy-start.15
  35.4 1.2 copy-start.8
  35.4 1.2 copy-start.21
  36.6 2.5 copy-start.16
  95.4 2.8 copy-start.1
  98.2 1.1 copy-start.12
  174.4 1.9 copy-start.7
  176.3 1.1 copy-start.9
  176.3 1.6 copy-start.13
  178.6 4.3 %copy-start.5 = (f32[2,176,1024]{2,1,0:T(8,128)}, f32[2,176,1024]{2,1,0:T(8,128)S(1)}, u32[]{:S(2)}) copy-start(f32[2,176,1024]{2,1,0:T(8,128)S(1)} %get-tuple-element.157) | copy-start | bytes 4325380
  178.6 1.6 copy-start.23
  180.2 2.6 copy-start.22
  252.6 2.0 copy-start.10
  254.5 3.0 copy-start.2
  254.6 3.0 %copy-start.3 = (f32[11,32,1024]{2,1,0:T(8,128)S(1)}, f32[11,32,1024]{2,1,0:T(8,128)}, u32[]{:S(2)}) copy-start(f32[11,32,1024]{2,1,0:T(8,128)} %get-tuple-element.75) | copy-start | bytes 4325380
  257.5 0.7 copy-start.20
  258.8 30.0 %copy-start.18 = (f32[2,1024]{1,0:T(2,128)S(1)}, f32[2,1024]{1,0:T(2,128)}, u32[]{:S(2)}) copy-start(f32[2,1024]{1,0:T(2,128)} %param.18) | copy-start | bytes 24580
  285.8 2.9 copy-start.19
  285.8 3.7 %copy-start.17 = (f32[4,16,128]{2,1,0:T(8,128)S(1)}, f32[4,16,128]{2,1,0:T(8,128)}, u32[]{:S(2)}) copy-start(f32[4,16,128]{2,1,0:T(8,128)} %get-tuple-element.90) | copy-start | bytes 98308
  290.1 1.6 copy-start.4
  292.2 1.4 copy-start.6
  292.2 1.8 copy-start.11

commit v6 on v5

--- a/solution.py
+++ b/solution.py
@@ -424,7 +424,7 @@
     return list(got[:5]) + [x.reshape(-1) for x in got[5:]]
 
 
-def closing(cid, mine, expb, lhs, modw, back, images, pairs):
+def closing(cid, mine, expb, lhs, modw, attn_back, exp_back, images, pairs):
     seq_n, own, mod_l = modw.shape
     img_n = expb.shape[0]
     rows = mine.shape[1]
@@ -432,25 +432,26 @@
     tiles = mod_l // 128
     slim = -(-tiles * images // 8) * 8
     share = img_n // seq_n
-    cut = back.shape[2]
     dim_l = pairs * 128
     width = dim_l * seq_n
-    hid_l = cut - 3 * dim_l
+    hid_l = exp_back.shape[2]
     hid_o = hid_l // img_n
     aligned = hid_o % 128 == 0
     flat = -(-tiles // 8) * 8
 
     def kernel(
-        mine_ref, expb_ref, lhs_ref, modw_ref, back_ref,
+        mine_ref, expb_ref, lhs_ref, modw_ref, attn_ref, exp_ref,
         modw_own, attn_own, exp_own, bias_ref, modb_ref, cond_ref,
-        seen, block, got, dd, mw_send, mw_recv, mb_send, gs_send, gs_all, gs_seen, back_all, *sems
+        seen, block, got, dd, mw_send, mw_recv, mb_send, gs_send, gs_all, gs_seen, attn_all, exp_all, *sems
     ):
         barrier = Session([], everyone_else("img", "seq"))
         barrier.greet()
         mine_go, mine_end = direct_ops("seq", mine_ref, seen, *sems[:2])
-        back_go, back_end = direct_ops("seq", back_ref, back_all, *sems[2:4])
+        attn_go, attn_end = direct_ops("seq", attn_ref, attn_all, *sems[2:4])
+        exp_go, exp_end = direct_ops("seq", exp_ref, exp_all, *sems[14:16])
         mine_go()
-        back_go()
+        attn_go()
+        exp_go()
         block[...] = jnp.zeros_like(block)
         gs_send[...] = jnp.zeros_like(gs_send)
         mb_send[...] = jnp.zeros_like(mb_send)
@@ -470,20 +471,20 @@
             block[i, slim + 5 : slim + 6] = total[at : at + 1]
         img_go, img_end = direct_ops("img", block, got, *sems[4:6])
         img_go()
-        back_end()
+        attn_end()
+        exp_end()
         for q in range(seq_n):
             for p in range(pairs):
                 for k in range(3):
                     to = k * width + q * dim_l + p * 128
                     at_c = p * 384 + k * 128
-                    attn_own[:, to : to + 128] = back_all[q, :, at_c : at_c + 128]
+                    attn_own[:, to : to + 128] = attn_all[q, :, at_c : at_c + 128]
             if aligned:
                 for i in range(img_n):
                     to = (i * seq_n + q) * hid_o
-                    at_c = 3 * dim_l + i * hid_o
-                    exp_own[:, to : to + hid_o] = back_all[q, :, at_c : at_c + hid_o]
+                    exp_own[:, to : to + hid_o] = exp_all[q, :, i * hid_o : (i + 1) * hid_o]
             else:
-                exp_own[:, q * hid_l : (q + 1) * hid_l] = back_all[q, :, 3 * dim_l :]
+                exp_own[:, q * hid_l : (q + 1) * hid_l] = exp_all[q]
         img_end()
         sums = got[0]
         for i in range(1, img_n):
@@ -532,7 +533,7 @@
             jax.ShapeDtypeStruct((seq_n, flat, 128), f32),
             jax.ShapeDtypeStruct((img_n, head, 128), f32),
         ),
-        in_specs=[full] * 5,
+        in_specs=[full] * 6,
         out_specs=(full,) * 6,
         scratch_shapes=[
             VM((seq_n, rows, 128), f32),
@@ -545,12 +546,13 @@
             VM((img_n, head, 128), f32),
             VM((img_n, head, 128), f32),
             VM((seq_n, img_n, head, 128), f32),
-            VM(back.shape, bf16),
+            VM(attn_back.shape, bf16),
+            VM(exp_back.shape, bf16),
         ]
-        + pairs_of_sems("seq", "seq", "img", "img", "seq", "seq", "seq"),
+        + pairs_of_sems("seq", "seq", "img", "img", "seq", "seq", "seq", "seq"),
         compiler_params=params(cid),
         name="closing",
-    )(mine, expb, lhs, modw, back)
+    )(mine, expb, lhs, modw, attn_back, exp_back)
     got = list(got)
     if not aligned:
         got[2] = got[2].reshape(own, seq_n, img_n, hid_o).transpose(0, 2, 1, 3).reshape(own, hid_l * seq_n)
@@ -580,6 +582,20 @@
     r_query = lax.rsqrt(half_sums(query * query, low_half) + 1e-06)
     r_key = lax.rsqrt(half_sums(key * key, low_half) + 1e-06)
     return query, key, value, low_half, r_query, r_key
+
+
+def some_rows(start, size):
+    return pl.ds(pl.multiple_of(start, 16), size)
+
+
+def centre(v):
+    centered = v - jnp.mean(v, axis=-1, keepdims=True)
+    factor = lax.rsqrt(jnp.mean(centered * centered, axis=-1, keepdims=True) + 1e-06)
+    return centered * factor, factor
+
+
+def centre_back(normed, factor, grad):
+    return factor * (grad - jnp.mean(grad, axis=-1, keepdims=True) - normed * jnp.mean(grad * normed, axis=-1, keepdims=True))
 
 
 def attend(cid, attn_input, attn_own, attn_early, early, bias, scale, sid_k, sid_q, out_img, exp_own, grad_own):
@@ -752,7 +768,9 @@
     )(attn_input, attn_own, attn_early, bias, scale, sid_k, sid_q, *session.ins)
 
 
-def attend_back(cid, packed, h1, attn_w, d_out, bias, scale, sid_k, sid_q, expw_part, shrunk_part, outw_part):
+def attend_back(
+    cid, packed, h1, attn_w, d_out, bias, scale, sid_k, sid_q, expw_part, shrunk_part, outw_part, mid, d_mid, tokens, cotangent, lines
+):
     seq_n, images, rows_b, wide = packed.shape
     img_n = lax.axis_size("img")
     outer = seq_n // 2
@@ -765,6 +783,8 @@
     own = outw_part.shape[2]
     tile = 256
     blocks_per_tile = tile // (w_chunks * w_size)
+    pieces = -(-width // wide)
+    h_chunks, f_chunks = chunks // images, shrunk_part.shape[1] // images
     session = Session([], everyone_else("seq") + two_level("img", img_n))
     mids = [
         scatter_scratch(img_n, expw_part.shape[1:], bf16),
@@ -777,8 +797,10 @@
 
     def kernel(*refs):
         p_in, h_in, w_in, do_ref, b_ref, es_ref, sk_ref, sq_ref, expw_ref, f_ref, outw_ref = refs[:11]
-        st_ref, dh1_own, attn_own, expw_own, f_own, outw_own = refs[11:17]
-        scratch = refs[17:]
+        mid_in, dmid_in, tok_ref, dy_ref, line_ref = refs[11:16]
+        st_ref, sum_ref, layer_ref, token_ref, attn_own, expw_own, outw_own = refs[16:23]
+        f_own, dh1_own, late_sem = refs[23:26]
+        scratch = refs[26:]
         p_ref, h_ref, w_ref, dp_ref, dh1, dattn, out_mid, load_sem = scratch[:8]
         k_buf, v_buf, e_buf, g_buf, dk_buf, dv_buf, do_buf, o_send, o_recv = scratch[8:17]
         expw_held, f_held, outw_held = scratch[17:20]
@@ -898,11 +920,37 @@
                 for load in loads[1:4]:
                     load.wait()
                 each(0, img_n, mid_out.step)
-                each(0, chunks, f_out.step)
+                each(0, shrunk_part.shape[1], f_out.step)
 
             each((i * exp_chunks) // turns, ((i + 1) * exp_chunks) // turns, exp_out.step)
 
         each(0, turns, turn)
+        late = []
+        for n, src in enumerate((mid_in, dmid_in)):
+            for k in range(pieces):
+                low, high = k * wide, min((k + 1) * wide, width)
+                dst = p_ref.at[n * pieces + k, :, :, : high - low]
+                late.append(pltpu.make_async_copy(src.at[:, :, low:high], dst, late_sem.at[len(late)]))
+        for copy in late:
+            copy.start()
+
+        def held_rows(n, g):
+            parts = [p_ref[n * pieces + k, g, :, : min(wide, width - k * wide)] for k in range(pieces)]
+            return jnp.concatenate(parts, axis=1)
+
+        def layer(g):
+            total = f_own[pl.ds(g * f_chunks, f_chunks)].reshape(rows_b, width) + line_ref[g, 2:3]
+            layer_ref[g] = (held_rows(0, g) + line_ref[g, 1:2] * total).astype(bf16)
+            sum_ref[g, 2:3] = jnp.sum(dy_ref[g].astype(f32) * total, axis=0, keepdims=True)
+
+        def token(g):
+            grad = dh1_own[pl.ds(g * h_chunks, h_chunks)].reshape(rows_b, width)
+            normed, factor = centre(tok_ref[g].astype(f32))
+            back = centre_back(normed, factor, grad * line_ref[g, 0:1])
+            token_ref[g] = (held_rows(1, g) + back).astype(bf16)
+            sum_ref[g, 0:1] = jnp.sum(grad * normed, axis=0, keepdims=True)
+            sum_ref[g, 1:2] = jnp.sum(grad, axis=0, keepdims=True)
+
         mid_out.finish()
         outw_out.start()
         for load in loads[4:]:
@@ -943,7 +991,12 @@
         each((3 * w_chunks) // 4, w_chunks, attn_out.step)
         outw_out.finish()
         f_out.finish()
+        sum_ref[...] = jnp.zeros_like(sum_ref)
+        for copy in late:
+            copy.wait()
+        each(0, images, layer)
         dh1_out.finish()
+        each(0, images, token)
         attn_out.finish()
 
         def last(i):
@@ -959,15 +1012,19 @@
         kernel,
         out_shape=(
             jax.ShapeDtypeStruct((turns, 8, 128), f32),
-            jax.ShapeDtypeStruct(h1.shape[1:], f32),
+            jax.ShapeDtypeStruct((images, 8, width), f32),
+            jax.ShapeDtypeStruct(tokens.shape, bf16),
+            jax.ShapeDtypeStruct(tokens.shape, bf16),
             jax.ShapeDtypeStruct(attn_w.shape[1:], bf16),
             jax.ShapeDtypeStruct(expw_part.shape[1:], bf16),
-            jax.ShapeDtypeStruct(shrunk_part.shape[1:], f32),
             jax.ShapeDtypeStruct((1, own, width), f32),
         ),
-        in_specs=[any_space] * 3 + [full] * 5 + [any_space] * 3,
-        out_specs=(full,) * 6,
+        in_specs=[any_space] * 3 + [full] * 5 + [any_space] * 5 + [full] * 3,
+        out_specs=(full,) * 7,
         scratch_shapes=[
+            VM(shrunk_part.shape[1:], f32),
+            VM(h1.shape[1:], f32),
+            pltpu.SemaphoreType.DMA((2 * pieces,)),
             VM(packed.shape, f32),
             VM(h1.shape, bf16),
             VM(attn_w.shape, bf16),
@@ -992,7 +1049,9 @@
         + [x for scratch in mids for x in scratch],
         compiler_params=params(cid),
         name="attend_back",
-    )(packed, h1, attn_w, d_out, bias, scale, sid_k, sid_q, expw_part, shrunk_part, outw_part)
+    )(
+        packed, h1, attn_w, d_out, bias, scale, sid_k, sid_q, expw_part, shrunk_part, outw_part, mid, d_mid, tokens, cotangent, lines
+    )
 
 
 def gelu_both(x):
@@ -1004,25 +1063,32 @@
     return x * half, slope
 
 
-def feed_forward(cid, mlp_input, grad_parts, grad_own, shr_own, exp_w, e_bias):
+def feed_forward(cid, tokens, context, out_w, cotangent, lines, grad_parts, grad_own, shr_own, exp_w, e_bias):
     seq_n, img_n = lax.axis_size("seq"), lax.axis_size("img")
     outer = seq_n // 2
-    chunks, size, width = mlp_input.shape
-    rows = chunks * size
+    rows, width = tokens.shape
     hid_l = exp_w.shape[1]
     ready, later = len(grad_parts), len(grad_own)
     images = ready + later
     g_chunks, g_size, _ = grad_own[0].shape
+    chunks, size = images * g_chunks, g_size
+    rows_p = rows // images
     w_chunks, w_size, _ = shr_own.shape
     hid_o = w_chunks * w_size
     tile = 256
     blocks_per_tile = tile // hid_o
     session = Session([], two_level("seq", seq_n) + two_level("img", img_n))
 
-    def kernel(x_ref, *refs):
+    def kernel(tok_ref, ctx_ref, ow_ref, dy_ref, line_ref, *refs):
         df_refs = refs[:images]
-        shr_ref, exp_ref, eb_ref, dh2_ref, dshr_own, f_ref, dexp_ref, expb_ref = refs[images : images + 8]
-        h2, df, shr, act, slope, dshr, dh2, df_sem, hs, hr, ss, sr, sk, shr_low, *more = refs[images + 8 :]
+        shr_ref, exp_ref, eb_ref = refs[images : images + 3]
+        mid_out, dmid_ref, do_ref, dout_ref, sum_ref, dshr_own, f_out, dexp_out, expb_ref = refs[images + 3 : images + 12]
+        x_ref, dh2_ref, attn, da, mid_ref, f_ref, dexp_ref, out_sem = refs[images + 12 : images + 20]
+        h2, df, shr, act, slope, dshr, dh2, df_sem, hs, hr, ss, sr, sk, shr_low, *more = refs[images + 20 :]
+        stores = [
+            pltpu.make_async_copy(src, dst, out_sem.at[n])
+            for n, (src, dst) in enumerate(((mid_ref, mid_out), (f_ref, f_out), (dexp_ref, dexp_out)))
+        ]
         shr_low[...] = shr_ref[...].astype(bf16)
         df_in = [
             gather_ops("seq", True, df_refs[ready + g], df.at[:, ready + g], *more[14 + 3 * g : 17 + 3 * g])
@@ -1033,8 +1099,27 @@
         shr_in = gather_ops("img", False, shr_low, shr, sk, ss, sr)
         dh2_out = scatter_ops("seq", True, dh2, dh2_ref, *more[:7])
         dshr_out = scatter_ops("img", False, dshr, dshr_own, *more[7:14])
+        shr_in.start()
+
+        def columns(t):
+            return lanes(t * tile, tile)
+
+        def project(t):
+            part = dot(ctx_ref[...], ow_ref[:, columns(t)], ((1,), (0,)))
+            attn[:, columns(t)] = part + line_ref[0, 3:4, columns(t)]
+
+        each(0, width // tile, project)
+        def middle(g):
+            here = some_rows(g * rows_p, rows_p)
+            mid = tok_ref[here].astype(f32) + line_ref[g, 0:1] * attn[here]
+            mid_ref[here] = mid
+            normed, _ = centre(mid)
+            low = (normed * line_ref[g, 1:2] + line_ref[g, 2:3]).astype(bf16)
+            x_ref[pl.ds(g * g_chunks, g_chunks)] = low.reshape(g_chunks, g_size, width)
+
+        each(0, images, middle)
+        stores[0].start()
         h2_in.start()
-        shr_in.start()
         for ops in df_in:
             ops.start()
         loads = [pltpu.make_async_copy(ref, df.at[:, g], df_sem.at[g]) for g, ref in enumerate(df_refs[:ready])]
@@ -1042,9 +1127,6 @@
             load.start()
         h2[0] = x_ref[...]
         expb_ref[...] = jnp.zeros_like(expb_ref)
-
-        def columns(t):
-            return lanes(t * tile, tile)
 
         def expand(j):
             def run(t):
@@ -1139,9 +1221,40 @@
         h2_in.sent()
         for j in range(1, seq_n):
             shrink(j)
+        stores[1].start()
         each(0, width // tile, expand_grad)
+        stores[2].start()
         dh2_out.finish()
+        sum_ref[...] = jnp.zeros_like(sum_ref)
+        def middle_back(g):
+            here = some_rows(g * rows_p, rows_p)
+            grad = dh2_ref[pl.ds(g * g_chunks, g_chunks)].reshape(rows_p, width)
+            normed, factor = centre(mid_ref[here])
+            back = centre_back(normed, factor, grad * line_ref[g, 1:2])
+            back = dy_ref[here].astype(f32) + back
+            dmid_ref[here] = back
+            low = (back * line_ref[g, 0:1]).astype(bf16)
+            da[here] = low
+            sum_ref[g, 0:1] = jnp.sum(grad * normed, axis=0, keepdims=True)
+            sum_ref[g, 1:2] = jnp.sum(grad, axis=0, keepdims=True)
+            sum_ref[g, 2:3] = jnp.sum(back * attn[here], axis=0, keepdims=True)
+            sum_ref[g, 3:4] = jnp.sum(low.astype(f32), axis=0, keepdims=True)
+
+        each(0, images, middle_back)
+
+        def context_grad(t):
+            weight = ow_ref[pl.ds(pl.multiple_of(t * tile, tile), tile), :]
+            do_ref[:, columns(t)] = dot(da[...], weight, ((1,), (1,))).astype(bf16)
+
+        def out_grad(t):
+            part = dot(ctx_ref[:, columns(t)], da[...], ((0,), (0,)))
+            dout_ref[pl.ds(pl.multiple_of(t * tile, tile), tile), :] = part.astype(bf16)
+
+        each(0, width // tile, context_grad)
+        each(0, width // tile, out_grad)
         dshr_out.finish()
+        for store in stores:
+            store.wait()
 
     full = pl.BlockSpec(memory_space=VM)
     any_space = pl.BlockSpec(memory_space=pl.ANY)
@@ -1151,22 +1264,34 @@
     return pl.pallas_call(
         kernel,
         out_shape=(
-            jax.ShapeDtypeStruct(mlp_input.shape, f32),
+            jax.ShapeDtypeStruct((rows, width), f32),
+            jax.ShapeDtypeStruct((rows, width), f32),
+            jax.ShapeDtypeStruct((rows, width), bf16),
+            jax.ShapeDtypeStruct((width, width), bf16),
+            jax.ShapeDtypeStruct((images, 8, width), f32),
             jax.ShapeDtypeStruct(shr_own.shape, f32),
-            jax.ShapeDtypeStruct((seq_n,) + mlp_input.shape, bf16),
+            jax.ShapeDtypeStruct((seq_n, chunks, size, width), bf16),
             jax.ShapeDtypeStruct(exp_w.shape, bf16),
             jax.ShapeDtypeStruct((1, hid_l), f32),
         ),
-        in_specs=[full] + [any_space] * ready + [full] * (later + 3),
-        out_specs=(full,) * 5,
+        in_specs=[full] * 5 + [any_space] * ready + [full] * (later + 3),
+        out_specs=(any_space,) + (full,) * 5 + (any_space,) * 2 + (full,),
         scratch_shapes=[
-            VM((seq_n,) + mlp_input.shape, bf16),
+            VM((chunks, size, width), bf16),
+            VM((chunks, size, width), f32),
+            VM((rows, width), f32),
+            VM((rows, width), bf16),
+            VM((rows, width), f32),
+            VM((seq_n, chunks, size, width), bf16),
+            VM(exp_w.shape, bf16),
+            pltpu.SemaphoreType.DMA((3,)),
+            VM((seq_n, chunks, size, width), bf16),
             VM((seq_n, images, g_chunks, g_size, width), bf16),
             VM((img_n,) + shr_own.shape, bf16),
             VM((seq_n, rows, hid_l), bf16),
             VM((seq_n, rows, hid_l), bf16),
             VM((img_n,) + shr_own.shape, bf16),
-            VM((seq_n,) + mlp_input.shape, bf16),
+            VM((seq_n, chunks, size, width), bf16),
             pltpu.SemaphoreType.DMA((max(ready, 1),)),
             seq_sems,
             seq_sems,
@@ -1175,21 +1300,17 @@
             pltpu.SemaphoreType.DMA((w_chunks,)),
             VM(shr_own.shape, bf16),
         ]
-        + scatter_scratch(seq_n, mlp_input.shape, bf16)
+        + scatter_scratch(seq_n, (chunks, size, width), bf16)
         + scatter_scratch(img_n, shr_own.shape, bf16)
         + [pltpu.SemaphoreType.DMA((g_chunks,)), grad_sems, grad_sems] * later,
         compiler_params=params(cid),
         name="feed_forward",
-    )(mlp_input, *grad_parts, *grad_own, shr_own, exp_w, e_bias)
+    )(tokens, context, out_w, cotangent, lines, *grad_parts, *grad_own, shr_own, exp_w, e_bias)
 
 
 def normalize(values):
     centered = values - jnp.mean(values, axis=-1, keepdims=True)
     return centered * lax.rsqrt(jnp.mean(centered * centered, axis=-1, keepdims=True) + 1e-06)
-
-
-def norm_back(values, grad_rows):
-    return jax.vjp(normalize, values)[1](grad_rows)[0]
 
 
 def pad_to(x, size, axis):
@@ -1322,12 +1443,14 @@
     sid_q = sid.reshape(images, 1, seq_n * rows_p)
     sid_k = sid[..., None]
 
-    resid_in = pad_to(tokens, rows_p, 1).astype(f32)
-    grad_out = pad_to(cotangent, rows_p, 1).astype(f32)
+    tokens_low = pad_to(tokens, rows_p, 1)
+    grad_low = pad_to(cotangent, rows_p, 1)
+    resid_in = tokens_low.astype(f32)
+    grad_out = grad_low.astype(f32)
     local = images * rows_p
 
     def chunked(x):
-        return x.reshape(x.shape[: x.ndim - 3] + (local // 32, 32, width))
+        return x.reshape(x.shape[: x.ndim - 3] + (local // 16, 16, width))
 
     normed_in = normalize(resid_in)
     attn_input = (normed_in * (1.0 + scale_attn) + shift_attn).astype(bf16)
@@ -1352,36 +1475,35 @@
     context_low = context_low.reshape(local, width)
     out_w = out_w.reshape(width, width)
     exp_w = exp_w.reshape(width, hid_l)
-    attn_out = (mm(context_low, out_w) + o_bias).reshape(images, rows_p, width)
-    resid_mid = resid_in + gain_attn * attn_out
-    normed_mid = normalize(resid_mid)
-    mlp_input = (normed_mid * (1.0 + scale_mlp) + shift_mlp).astype(bf16)
     shrb_part = jnp.sum(grad_shrunk.astype(f32), axis=(0, 1))
-    grad_mlp_input, shrw_own, shrunk_part, expw_part, expb_part = feed_forward(
+    lines = [gain_attn, 1.0 + scale_mlp, shift_mlp, jnp.broadcast_to(o_bias, (images, 1, width))]
+    lines = jnp.concatenate(lines + [jnp.zeros((images, 4, width), f32)], axis=1)
+    resid_mid, grad_mid, grad_context, outw_part, mid_sums, shrw_own, shrunk_part, expw_part, expb_part = feed_forward(
         7,
-        chunked(mlp_input),
+        tokens_low.reshape(local, width),
+        context_low,
+        out_w,
+        grad_low.reshape(local, width),
+        lines,
         df_ready,
         [grad_chunks[g] for g in range(ready, images)],
         hidden_chunks(shrink_weight),
         exp_w,
         e_bias.reshape(1, hid_l),
     )
-    grad_mlp_input = grad_mlp_input.reshape(images, rows_p, width)
+    resid_mid = resid_mid.reshape(images, rows_p, width)
+    grad_mid = grad_mid.reshape(images, rows_p, width)
+    grad_context = grad_context.reshape(images, rows_p, width)
+    outw_part = outw_part.reshape(img_n, seq_n, own, width)
+    grad_scale_mlp, grad_shift_mlp, grad_gain_attn = mid_sums[:, 0], mid_sums[:, 1], mid_sums[:, 2]
+    outb_part = jnp.sum(mid_sums[:, 3], axis=0)
     shrw_own = shrw_own.reshape(hid_o, width)
     expb_part = expb_part.reshape(hid_l)
     expw_part = expw_part.reshape(img_n, blk, hid_l)
 
-    grad_scale_mlp = jnp.sum(grad_mlp_input * normed_mid, axis=1)
-    grad_shift_mlp = jnp.sum(grad_mlp_input, axis=1)
-    grad_mid = grad_out + norm_back(resid_mid, grad_mlp_input * (1.0 + scale_mlp))
-    grad_gain_attn = jnp.sum(grad_mid * attn_out, axis=1)
-    grad_attn_out = (grad_mid * gain_attn).astype(bf16)
-    outb_part = jnp.sum(grad_attn_out.astype(f32), axis=(0, 1))
-    da = grad_attn_out.reshape(local, width)
-    grad_context = mm_nt(da, out_w).astype(bf16)
-    grad_context = grad_context.reshape(images, rows_p, width)
-    outw_part = mm_tn(context_low, da).astype(bf16).reshape(img_n, seq_n, own, width)
-    sums, grad_attn_input, attnw_blk, expw_blk, shrunk, outw_own = attend_back(
+    lines = [1.0 + scale_attn, gain_mlp, jnp.broadcast_to(s_bias, (images, 1, width))]
+    lines = jnp.concatenate(lines + [jnp.zeros((images, 5, width), f32)], axis=1)
+    sums, row_sums, layer_out, token_grad, attnw_blk, expw_blk, outw_own = attend_back(
         11,
         packed,
         h1,
@@ -1394,20 +1516,18 @@
         weight_chunks(expw_part),
         shrunk_part,
         outw_part,
+        resid_mid,
+        grad_mid,
+        tokens_low,
+        grad_low,
+        lines,
     )
-    shrunk = shrunk.reshape(images, rows_p, width) + s_bias
-    layer_out = (resid_mid[:, :rows] + gain_mlp * shrunk[:, :rows]).astype(bf16)
-    grad_gain_mlp = jnp.sum(grad_out * shrunk, axis=1)
+    grad_scale_attn, grad_shift_attn, grad_gain_mlp = row_sums[:, 0], row_sums[:, 1], row_sums[:, 2]
     sums = jnp.sum(sums.reshape(images, pairs, 8, 128), axis=0)
     qb_part = sums[:, 0].reshape(dim_l)
     vb_part = sums[:, 1].reshape(dim_l)
     logs_part = jnp.sum(sums[:, 2].reshape(dim_l // headdim, headdim), axis=1)
     outw_own = outw_own.reshape(own, width)
-    grad_attn_input = grad_attn_input.reshape(images, rows_p, width)
-    grad_scale_attn = jnp.sum(grad_attn_input * normed_in, axis=1)
-    grad_shift_attn = jnp.sum(grad_attn_input, axis=1)
-    token_grad = grad_mid[:, :rows] + norm_back(resid_in[:, :rows], grad_attn_input[:, :rows] * (1.0 + scale_attn))
-    token_grad = token_grad.astype(bf16)
 
     grad_mod = jnp.concatenate(
         [grad_gain_attn, grad_gain_mlp, grad_scale_attn, grad_scale_mlp, grad_shift_attn, grad_shift_mlp],
@@ -1432,11 +1552,16 @@
     )
     bias_mine = pad_to(bias_mine, -(-bias_mine.shape[0] // 8) * 8, 0)
     mine = jnp.concatenate([grad_mod, jnp.broadcast_to(bias_mine[None], (seq_n,) + bias_mine.shape)], axis=1)
-    back_cut = jnp.concatenate(
-        [attnw_blk.reshape(seq_n, own, 3 * dim_l), expw_blk.reshape(seq_n, own, hid_l)], axis=2
-    )
     modw_own, attnw_own, expw_own, bias_own, modb_all, cond_sum = closing(
-        13, mine, lined(expb_part, img_n), cond_rows, modw_cut, back_cut, images, pairs
+        13,
+        mine,
+        lined(expb_part, img_n),
+        cond_rows,
+        modw_cut,
+        attnw_blk.reshape(seq_n, own, 3 * dim_l),
+        expw_blk.reshape(seq_n, own, hid_l),
+        images,
+        pairs,
     )
 
     modw_own, attnw_own, expw_own, outw_own, shrw_own, shrb_own, outb_own, qb_own, vb_own, expb_own, logs_total = finishing(
@@ -1446,8 +1571,8 @@
     grad_silu = cond_sum[:, :, :own].reshape(img_n, seq_n, images, own).transpose(2, 0, 1, 3).reshape(images, width)
     cond_grad = jax.vjp(jax.nn.silu, condition)[1](grad_silu)[0]
     return (
-        layer_out,
-        token_grad,
+        layer_out[:, :rows],
+        token_grad[:, :rows],
         cond_grad,
         modw_own,
         modb_own,

time: 299 us -> 290 us (0.970)
  other arithmetic: 21.9 us -> 7.98 us
  Pallas kernels: 252 us -> 264 us
  matrix products: 7.21 us -> 0 us
    dot_general x3 -> x0, matrix products: 7.21 us -> none  [the longest x1 2.79 us: mm(): return jnp.dot(a, b, preferred_element_type=f32)]
    pallas_call x1, Pallas kernels: 73 us -> 80.1 us  [feed_forward(): pl.pallas_call(kernel, out_shape=(jax.ShapeDtypeStruct((rows, width), f32...]
    reduce_sum x6 -> x1, other arithmetic: 6.84 us -> 0.02 us  [body(): outb_part = jnp.sum(mid_sums[:, 3], axis=0)]
    unnamed x61 -> x35, local copies, waits for them, and re-layouts: 8.32 us -> 4.91 us
    convert_element_type x3 -> x0, other arithmetic: 3.37 us -> none  [the longest x1 1.37 us: body(): resid_in = pad_to(tokens, rows_p, 1).astype(f32)]
where the time goes in v6:
time: 290 us; the launch traced here: 289 us
  Pallas kernels  264 us (91%)
  local copies, waits for them, and re-layouts  16.6 us (6%)
  other arithmetic  7.98 us (3%)
    pallas_call x1, Pallas kernels, feed_forward(): pl.pallas_call(kernel, out_shape=(jax.ShapeDtypeStruct((rows, width), f32...  80.1 us
    pallas_call x1, Pallas kernels, attend_back(): pl.pallas_call(kernel, out_shape=(jax.ShapeDtypeStruct((turns, 8, 128), f...  70.7 us
    pallas_call x1, Pallas kernels, attend(): pl.pallas_call(kernel, out_shape=tuple([jax.ShapeDtypeStruct((images, row...  56.7 us
    pallas_call x1, Pallas kernels, closing(): pl.pallas_call(kernel, out_shape=(jax.ShapeDtypeStruct((own, mod_l * seq_...  26.7 us
    pallas_call x1, Pallas kernels, opening(): pl.pallas_call(kernel, out_shape=(jax.ShapeDtypeStruct((seq_n, slim, 128)...  26.5 us

profile of v6, /device:TPU:1, one launch (start us, length us, event | category | flops | bytes accessed | tf_op | source)
XLA Modules:
  0.0 289.1 jit_solution(16560725201887868436)
XLA Ops:
  0.6 0.8 concatenate.24
  1.5 0.7 multiply_convert_fusion.1
  2.3 0.6 pad_maximum_fusion.1.small_ref
  3.0 26.5 %opening.1 = (f32[4,24,128]{2,1,0:T(8,128)}, f32[4,8,8,128]{3,2,1,0:T(8,128)}, f32[4,16,128]{2,1,0:T(8,128)}, bf16[4,32,1536]{2,1,0:T(8,128)(2,1)}, bf16[4,32,76...) custom-call(f32[32,6144]{1,0:T(8,128)} %mod_in.1, ...), custom_call_target="tpu_custom_call" | custom-call | tf_op jit(solution)/shard_map/opening/pallas_call | solution.py:370
  29.5 0.8 copy.105
  30.4 0.9 reshape.297
  32.0 0.3 fusion.2
  32.4 1.2 fusion.5
  33.6 0.7 slice.76.refs_1_
  34.7 0.6 pad_maximum_fusion.2.refs_3_.refs_4_
  35.4 0.6 dynamic_slice.17
  36.4 0.3 copy.82
  36.7 1.0 broadcast_select_fusion.refs_5_.refs_6_
  37.9 0.6 broadcast_select_fusion.1.refs_6_.refs_7_
  38.9 0.9 fusion.8
  39.8 56.7 %attend.1 = (bf16[2,176,1024]{2,1,0:T(8,128)(2,1)}, f32[4,2,176,768]{3,2,1,0:T(8,128)}, bf16[4,22,16,1024]{3,2,1,0:T(8,128)(2,1)}, bf16[8,4,32,768]{3,2,1,0:T(8,...) custom-call(bf16[22,16,1024]{2,1,0:T(8,128)(2,1)} %bitcast.92, ...), custom_call_target="tpu_custom_call" | custom-call | tf_op jit(solution)/shard_map/attend/pallas_call | solution.py:737
  96.5 0.9 pad.26.refs_13_
  97.4 1.0 pad.30.refs_14_
  98.5 0.7 concatenate.27.line_ref
  99.2 0.6 dynamic-slice_bitcast_fusion.refs_4_
  99.8 80.1 %feed_forward.1 = (f32[352,1024]{1,0:T(8,128)}, f32[352,1024]{1,0:T(8,128)}, bf16[352,1024]{1,0:T(8,128)(2,1)}, bf16[1024,1024]{1,0:T(8,128)(2,1)}, f32[2,8,1024...) custom-call(bf16[352,1024]{1,0:T(8,128)(2,1)} %bitcast.90, ...), custom_call_target="tpu_custom_call" | custom-call | tf_op jit(solution)/shard_map/feed_forward/pallas_call | solution.py:1264
  180.1 0.7 maximum_maximum_fusion.refs_15_
  180.8 70.7 %attend_back.1 = (f32[4,8,128]{2,1,0:T(8,128)}, f32[2,8,1024]{2,1,0:T(8,128)}, bf16[2,176,1024]{2,1,0:T(8,128)(2,1)}, bf16[2,176,1024]{2,1,0:T(8,128)(2,1)}, bf1...) custom-call(f32[4,2,176,768]{3,2,1,0:T(8,128)} %get-tuple-element.69.refs_0_, ...), custom_call_target="tpu_custom_call" | custom-call | tf_op jit(solution)/shard_map/attend_back/pallas_call | solution.py:1011
  251.5 2.7 copy.91
  254.3 1.6 copy.92
  256.1 0.2 dynamic_update_slice.4
  256.8 0.7 pad_maximum_fusion.mine_ref
  257.4 26.7 %closing.1 = (bf16[32,6144]{1,0:T(8,128)(2,1)}, bf16[32,3072]{1,0:T(8,128)(2,1)}, bf16[32,4096]{1,0:T(8,128)(2,1)}, f32[8,128]{1,0:T(8,128)}, f32[4,16,128]{2,1,0:T(8,128)}, /*index=5*/f32[8,8,128]{2,1,0:T(8,128)}) custom-call(f32[4,56,128]{2,1,0:T(8,128)} %pad_maximum_fusion.mine_ref, f32[8,128]{1,0:T(8,128)} %bitcast.128, ...), custom_call_target="tpu_custom_call" | custom-call | tf_op jit(solution)/shard_map/closing/pallas_call | solution.py:526
  284.1 0.8 copy.90
  285.0 0.6 fusion.7
  285.6 2.9 finishing.1
  288.5 0.6 dynamic_slice.19
  (94 shorter events, 3.2 us)
Async XLA Ops:
  3.0 28.6 %copy-start.1 = (bf16[2,170,1024]{2,0,1:T(2,128)(2,1)S(1)}, bf16[2,170,1024]{2,0,1:T(2,128)(2,1)}, u32[]{:S(2)}) copy-start(bf16[2,170,1024]{2,0,1:T(2,128)(2,1)} %param.16) | copy-start | bytes 2088964
  31.8 1.8 copy-start.3
  32.0 3.3 %copy-start.10 = (f32[16]{0:T(128)S(1)}, f32[16]{0:T(128)}, u32[]{:S(2)}) copy-start(f32[16]{0:T(128)} %param.31) | copy-start | bytes 196
  32.0 4.1 %copy-start.9 = (s32[2,10]{1,0:T(2,128)S(1)}, s32[2,10]{1,0:T(2,128)}, u32[]{:S(2)}) copy-start(s32[2,10]{1,0:T(2,128)} %param.19) | copy-start | bytes 244
  33.6 5.0 %copy-start.2 = (bf16[2,170,1024]{2,0,1:T(2,128)(2,1)S(1)}, bf16[2,170,1024]{2,0,1:T(2,128)(2,1)}, u32[]{:S(2)}) copy-start(bf16[2,170,1024]{2,0,1:T(2,128)(2,1)} %param.17) | copy-start | bytes 2088964
  251.5 2.8 copy-start
  251.5 4.4 %copy-start.4 = (f32[2,8,1024]{2,1,0:T(8,128)S(1)}, f32[2,8,1024]{2,1,0:T(8,128)}, u32[]{:S(2)}) copy-start(f32[2,8,1024]{2,1,0:T(8,128)} %get-tuple-element.84) | copy-start | bytes 196612
  251.5 4.4 %copy-start.8 = (f32[4,8,128]{2,1,0:T(8,128)S(1)}, f32[4,8,128]{2,1,0:T(8,128)}, u32[]{:S(2)}) copy-start(f32[4,8,128]{2,1,0:T(8,128)} %get-tuple-element.86) | copy-start | bytes 49156
  251.5 5.0 %copy-start.5 = (f32[2,8,1024]{2,1,0:T(8,128)S(1)}, f32[2,8,1024]{2,1,0:T(8,128)}, u32[]{:S(2)}) copy-start(f32[2,8,1024]{2,1,0:T(8,128)} %get-tuple-element.85) | copy-start | bytes 196612
  255.9 29.1 %copy-start.7 = (f32[2,1024]{1,0:T(2,128)S(1)}, f32[2,1024]{1,0:T(2,128)}, u32[]{:S(2)}) copy-start(f32[2,1024]{1,0:T(2,128)} %param.18) | copy-start | bytes 24580
  284.1 4.4 %copy-start.6 = (f32[4,16,128]{2,1,0:T(8,128)S(1)}, f32[4,16,128]{2,1,0:T(8,128)}, u32[]{:S(2)}) copy-start(f32[4,16,128]{2,1,0:T(8,128)} %get-tuple-element.100) | copy-start | bytes 98308

commit v7 on v6

--- a/solution.py
+++ b/solution.py
@@ -175,12 +175,39 @@
         start_outer()
         start_inner()
 
+    def step_one(o, c):
+        near(o, c).wait_recv()
+        total = mine(2 * o, c) + near_buf[o, c].astype(f32)
+        send_buf[o, c] = total.astype(send_buf.dtype)
+        far(o, c).start()
+
     def step(c):
         for o in range(1, outer):
-            near(o, c).wait_recv()
-            total = mine(2 * o, c) + near_buf[o, c].astype(f32)
-            send_buf[o, c] = total.astype(send_buf.dtype)
-            far(o, c).start()
+            step_one(o, c)
+
+    def start_one(o):
+        each(0, chunks, lambda c: near(o, c).start())
+
+    def by_blocks(per_tile, make):
+        order = []
+        for k in reversed(range(n // per_tile)):
+            outers = [o for o in range(1, outer) if (2 * o + 1) // per_tile == k]
+
+            def one(k=k, outers=outers):
+                make((me // per_tile) ^ k)
+                for o in outers:
+                    start_one(o)
+                if k == 0:
+                    start_inner()
+
+            if k:
+                one()
+            order += outers
+        halves = []
+        for o in order:
+            for low, high in ((0, (chunks + 1) // 2), ((chunks + 1) // 2, chunks)):
+                halves.append(lambda o=o, low=low, high=high: each(low, high, lambda c: step_one(o, c)))
+        return one, halves
 
     def finish():
         def last(c):
@@ -198,8 +225,26 @@
         each(0, chunks, last)
 
     return SimpleNamespace(
-        start=start, start_outer=start_outer, start_inner=start_inner, step=step, finish=finish
+        start=start,
+        start_outer=start_outer,
+        start_inner=start_inner,
+        step=step,
+        finish=finish,
+        by_blocks=by_blocks,
     )
+
+
+def in_turns(halves, turns):
+    taken = [0, 0]
+
+    def take():
+        taken[1] += 1
+        upto = -(-len(halves) * taken[1] // turns)
+        for half in halves[taken[0] : upto]:
+            half()
+        taken[0] = upto
+
+    return take
 
 
 def scatter_scratch(n, inner, dtype):
@@ -610,11 +655,11 @@
     pairs = wide // 384
     turns = images * pairs
     tile = 256 if wide % 256 == 0 else 128
-    w_chunks = attn_own.shape[0]
+    w_chunks = attn_own.shape[0] - early
     plans = [gather(x, "seq", True) for x in grad_own] + [gather(out_img, "seq", False, True), gather(exp_own, "img", False)]
     session = Session(plans, everyone_else("seq") + two_level("img", img_n))
     ins, outs = 7 + len(session.ins), 4 + len(plans)
-    weight = (img_n, early + w_chunks) + attn_own.shape[1:]
+    weight = (img_n,) + attn_own.shape
 
     def kernel(*refs):
         x_ref, w_ref, early_ref, b_ref, es_ref, sk_ref, sq_ref = refs[:7]
@@ -625,7 +670,7 @@
         session.greet()
         session.bind(refs[7:ins], refs[ins + 4 : ins + outs], scratch[13:])
         h1_in = gather_ops("seq", True, x_ref, h1, None, hs, hr)
-        w_in = gather_ops("img", False, w_ref, attn_w.at[:, early:], wk, ws, wr)
+        w_in = gather_ops("img", False, w_ref.at[early:], attn_w.at[:, early:], wk, ws, wr)
         if early:
             load = pltpu.make_async_copy(early_ref, attn_w.at[:, :early], early_sem.at[0])
             load.start()
@@ -974,21 +1019,24 @@
 
             each(0, width // tile, run)
 
-        each(0, width // tile, weight_grad)
-        attn_out.start()
+        own_tile, halves = attn_out.by_blocks(blocks_per_tile, weight_grad)
+        take = in_turns(halves, 6)
         outw_out.step(0)
+        for k in range(seq_n - 1, 1, -1):
+            input_grad(k)
+            if k in (3, 2):
+                take()
+        dh1_out.start_outer()
+        own_tile()
+        each(0, chunks, dh1_out.step)
+        take()
         exp_out.finish()
-        for o in range(1, outer):
-            for j in (2 * o + 1, 2 * o):
-                input_grad(j)
-        dh1_out.start_outer()
-        each(0, chunks, dh1_out.step)
-        each(0, w_chunks // 2, attn_out.step)
         input_grad(1)
-        each(w_chunks // 2, (3 * w_chunks) // 4, attn_out.step)
+        take()
         input_grad(0)
         dh1_out.start_inner()
-        each((3 * w_chunks) // 4, w_chunks, attn_out.step)
+        take()
+        take()
         outw_out.finish()
         f_out.finish()
         sum_ref[...] = jnp.zeros_like(sum_ref)
@@ -1075,7 +1123,7 @@
     rows_p = rows // images
     w_chunks, w_size, _ = shr_own.shape
     hid_o = w_chunks * w_size
-    tile = 256
+    tile, broad = 256, min(512, hid_l)
     blocks_per_tile = tile // hid_o
     session = Session([], two_level("seq", seq_n) + two_level("img", img_n))
 
@@ -1130,22 +1178,24 @@
 
         def expand(j):
             def run(t):
-                u = dot(h2[j].reshape(rows, width), exp_ref[:, columns(t)], ((1,), (0,))) + eb_ref[:, columns(t)]
+                here = lanes(t * broad, broad)
+                u = dot(h2[j].reshape(rows, width), exp_ref[:, here], ((1,), (0,))) + eb_ref[:, here]
                 value, grad = gelu_both(u)
-                act[j, :, columns(t)] = value.astype(bf16)
-                slope[j, :, columns(t)] = grad.astype(bf16)
-
-            each(0, hid_l // tile, run)
+                act[j, :, here] = value.astype(bf16)
+                slope[j, :, here] = grad.astype(bf16)
+
+            each(0, hid_l // broad, run)
 
         def back_act(j):
             def run(t):
-                weight = shr[pl.ds(t * blocks_per_tile, blocks_per_tile)].reshape(tile, width)
+                here = lanes(t * broad, broad)
+                weight = shr[pl.ds(t * (broad // hid_o), broad // hid_o)].reshape(broad, width)
                 grad = dot(df[j].reshape(rows, width), weight, ((1,), (1,)))
-                grad = (slope[j, :, columns(t)].astype(f32) * grad).astype(bf16)
-                slope[j, :, columns(t)] = grad
-                expb_ref[:, columns(t)] += jnp.sum(grad.astype(f32), axis=0, keepdims=True)
-
-            each(0, hid_l // tile, run)
+                grad = (slope[j, :, here].astype(f32) * grad).astype(bf16)
+                slope[j, :, here] = grad
+                expb_ref[:, here] += jnp.sum(grad.astype(f32), axis=0, keepdims=True)
+
+            each(0, hid_l // broad, run)
 
         def back_input(j):
             def run(t):
@@ -1174,53 +1224,49 @@
             part = dot(left, slope[...].reshape(seq_n * rows, hid_l), ((0,), (0,)))
             dexp_ref[pl.ds(pl.multiple_of(t * tile, tile), tile), :] = part.astype(bf16)
 
-        expand(0)
         h2_in.near()
-        expand(1)
+        each(0, 2, expand)
         half = chunks // 2
         each(0, half, h2_in.step)
         each(0, w_chunks // 2, shr_in.step)
         each(half, chunks, h2_in.step)
-        for o in range(1, outer):
-            expand(2 * o)
         each(w_chunks // 2, w_chunks, shr_in.step)
-        for ops in df_in:
-            each(0, g_chunks, ops.step)
         for o in range(1, outer):
             h2_in.handed(o)
-            expand(2 * o + 1)
         for ops in df_in:
+            each(0, g_chunks // 2, ops.step)
+        each(2, seq_n, expand)
+        for ops in df_in:
+            each(g_chunks // 2, g_chunks, ops.step)
             ops.finish()
         for load in loads:
             load.wait()
-        each(0, hid_l // tile, shrink_grad)
+        own_tile, halves = dshr_out.by_blocks(blocks_per_tile, shrink_grad)
+        take = in_turns(halves, 6)
         shr_in.near()
         for o in range(1, img_n // 2):
             shr_in.handed(o)
         shr_in.sent()
-        dshr_out.start()
-        for o in range(1, outer):
-            for j in (2 * o + 1, 2 * o):
-                back_act(j)
-                back_input(j)
-        def dshr_steps(k):
-            each((k * w_chunks) // 4, ((k + 1) * w_chunks) // 4, dshr_out.step)
-
+        for k in range(seq_n - 1, 1, -1):
+            back_act(k)
+            back_input(k)
+            if k in (3, 2):
+                take()
         dh2_out.start_outer()
-        dshr_steps(0)
+        own_tile()
         each(0, chunks, dh2_out.step)
+        take()
         back_act(1)
-        dshr_steps(1)
+        take()
         back_input(1)
         back_act(0)
-        dshr_steps(2)
+        take()
         back_input(0)
         dh2_out.start_inner()
         shrink(0)
-        dshr_steps(3)
+        take()
         h2_in.sent()
-        for j in range(1, seq_n):
-            shrink(j)
+        each(1, seq_n, shrink)
         stores[1].start()
         each(0, width // tile, expand_grad)
         stores[2].start()
@@ -1402,8 +1448,6 @@
         1, *weights, out_weight, small, seq_n, images, pairs, early
     )
     out_img = out_img.reshape(img_n, own, width)
-    if early:
-        attn_b = attn_b[early:]
     exp_b = exp_b.reshape(blk, hid_l)
 
     def weight_chunks(x):

time: 290 us -> 282 us (0.972)
  Pallas kernels: 264 us -> 257 us
    pallas_call x1, Pallas kernels: 70.7 us -> 66 us  [attend_back(): pl.pallas_call(kernel, out_shape=(jax.ShapeDtypeStruct((turns, 8, 128), f...]
where the time goes in v7:
time: 282 us
  Pallas kernels  257 us (91%)
  local copies, waits for them, and re-layouts  15.9 us (6%)
  other arithmetic  7.98 us (3%)
    pallas_call x1, Pallas kernels, feed_forward(): pl.pallas_call(kernel, out_shape=(jax.ShapeDtypeStruct((rows, width), f32...  78.7 us
    pallas_call x1, Pallas kernels, attend_back(): pl.pallas_call(kernel, out_shape=(jax.ShapeDtypeStruct((turns, 8, 128), f...  66 us
    pallas_call x1, Pallas kernels, attend(): pl.pallas_call(kernel, out_shape=tuple([jax.ShapeDtypeStruct((images, row...  56.7 us
    pallas_call x1, Pallas kernels, opening(): pl.pallas_call(kernel, out_shape=(jax.ShapeDtypeStruct((seq_n, slim, 128)...  26.5 us
    pallas_call x1, Pallas kernels, closing(): pl.pallas_call(kernel, out_shape=(jax.ShapeDtypeStruct((own, mod_l * seq_...  26.1 us

profile of v7, /device:TPU:1, one launch (start us, length us, event | category | flops | bytes accessed | tf_op | source)
XLA Modules:
  0.0 281.9 jit_solution(15587470671743582582)
XLA Ops:
  0.6 0.8 concatenate.24
  1.5 0.7 multiply_convert_fusion.1
  2.3 0.6 pad_maximum_fusion.1.small_ref
  3.0 26.5 %opening.1 = (f32[4,24,128]{2,1,0:T(8,128)}, f32[4,8,8,128]{3,2,1,0:T(8,128)}, f32[4,16,128]{2,1,0:T(8,128)}, bf16[4,32,1536]{2,1,0:T(8,128)(2,1)}, bf16[4,32,76...) custom-call(f32[32,6144]{1,0:T(8,128)} %mod_in.1, ...), custom_call_target="tpu_custom_call" | custom-call | tf_op jit(solution)/shard_map/opening/pallas_call | solution.py:415
  29.5 0.8 copy.105
  30.4 0.9 reshape.297
  32.0 0.3 fusion.2
  32.3 1.2 fusion.5
  34.0 0.6 pad_maximum_fusion.2.refs_3_.refs_4_
  34.7 0.6 dynamic_slice.17
  35.7 0.3 copy.82
  36.1 1.0 broadcast_select_fusion.refs_5_.refs_6_
  37.2 0.6 broadcast_select_fusion.1.refs_6_.refs_7_
  38.0 0.2 convert_reduce_fusion.1
  38.2 0.9 fusion.8
  39.1 56.7 %attend.1 = (bf16[2,176,1024]{2,1,0:T(8,128)(2,1)}, f32[4,2,176,768]{3,2,1,0:T(8,128)}, bf16[4,22,16,1024]{3,2,1,0:T(8,128)(2,1)}, bf16[8,4,32,768]{3,2,1,0:T(8,...) custom-call(bf16[22,16,1024]{2,1,0:T(8,128)(2,1)} %bitcast.92, ...), custom_call_target="tpu_custom_call" | custom-call | tf_op jit(solution)/shard_map/attend/pallas_call | solution.py:782
  95.8 0.9 pad.26.refs_13_
  96.8 1.0 pad.30.refs_14_
  97.9 0.7 concatenate.27.line_ref
  98.6 0.6 dynamic-slice_bitcast_fusion.refs_4_
  99.2 78.7 %feed_forward.1 = (f32[352,1024]{1,0:T(8,128)}, f32[352,1024]{1,0:T(8,128)}, bf16[352,1024]{1,0:T(8,128)(2,1)}, bf16[1024,1024]{1,0:T(8,128)(2,1)}, f32[2,8,1024...) custom-call(bf16[352,1024]{1,0:T(8,128)(2,1)} %bitcast.90, ...), custom_call_target="tpu_custom_call" | custom-call | tf_op jit(solution)/shard_map/feed_forward/pallas_call | solution.py:1310
  178.0 0.7 maximum_maximum_fusion.refs_15_
  178.7 66.0 %attend_back.1 = (f32[4,8,128]{2,1,0:T(8,128)}, f32[2,8,1024]{2,1,0:T(8,128)}, bf16[2,176,1024]{2,1,0:T(8,128)(2,1)}, bf16[2,176,1024]{2,1,0:T(8,128)(2,1)}, bf1...) custom-call(f32[4,2,176,768]{3,2,1,0:T(8,128)} %get-tuple-element.69.refs_0_, ...), custom_call_target="tpu_custom_call" | custom-call | tf_op jit(solution)/shard_map/attend_back/pallas_call | solution.py:1059
  244.8 2.7 copy.91
  247.5 1.6 copy.92
  249.4 0.2 dynamic_update_slice.4
  250.0 0.7 pad_maximum_fusion.mine_ref
  250.6 26.1 %closing.1 = (bf16[32,6144]{1,0:T(8,128)(2,1)}, bf16[32,3072]{1,0:T(8,128)(2,1)}, bf16[32,4096]{1,0:T(8,128)(2,1)}, f32[8,128]{1,0:T(8,128)}, f32[4,16,128]{2,1,0:T(8,128)}, /*index=5*/f32[8,8,128]{2,1,0:T(8,128)}) custom-call(f32[4,56,128]{2,1,0:T(8,128)} %pad_maximum_fusion.mine_ref, f32[8,128]{1,0:T(8,128)} %bitcast.128, ...), custom_call_target="tpu_custom_call" | custom-call | tf_op jit(solution)/shard_map/closing/pallas_call | solution.py:571
  276.8 0.8 copy.90
  277.7 0.6 fusion.7
  278.3 2.9 %finishing.1 = (f32[32,6144]{1,0:T(8,128)}, f32[32,3072]{1,0:T(8,128)}, f32[32,4096]{1,0:T(8,128)}, f32[32,1024]{1,0:T(8,128)}, f32[128,1024]{1,0:T(8,128)}, /*i...) custom-call(bf16[32,6144]{1,0:T(8,128)(2,1)} %get-tuple-element.93.m, ...), custom_call_target="tpu_custom_call" | custom-call | tf_op jit(solution)/shard_map/finishing/pallas_call | solution.py:461
  281.2 0.6 dynamic_slice.19
  (91 shorter events, 3.0 us)
Async XLA Ops:
  3.0 28.6 %copy-start.1 = (bf16[2,170,1024]{2,0,1:T(2,128)(2,1)S(1)}, bf16[2,170,1024]{2,0,1:T(2,128)(2,1)}, u32[]{:S(2)}) copy-start(bf16[2,170,1024]{2,0,1:T(2,128)(2,1)} %param.16) | copy-start | bytes 2088964
  31.8 2.8 copy-start.9
  31.8 3.6 %copy-start.8 = (s32[2,10]{1,0:T(2,128)S(1)}, s32[2,10]{1,0:T(2,128)}, u32[]{:S(2)}) copy-start(s32[2,10]{1,0:T(2,128)} %param.19) | copy-start | bytes 244
  33.6 4.3 %copy-start.2 = (bf16[2,170,1024]{2,0,1:T(2,128)(2,1)S(1)}, bf16[2,170,1024]{2,0,1:T(2,128)(2,1)}, u32[]{:S(2)}) copy-start(bf16[2,170,1024]{2,0,1:T(2,128)(2,1)} %param.17) | copy-start | bytes 2088964
  244.7 2.8 copy-start
  244.7 4.4 %copy-start.3 = (f32[2,8,1024]{2,1,0:T(8,128)S(1)}, f32[2,8,1024]{2,1,0:T(8,128)}, u32[]{:S(2)}) copy-start(f32[2,8,1024]{2,1,0:T(8,128)} %get-tuple-element.84) | copy-start | bytes 196612
  244.7 4.4 %copy-start.7 = (f32[4,8,128]{2,1,0:T(8,128)S(1)}, f32[4,8,128]{2,1,0:T(8,128)}, u32[]{:S(2)}) copy-start(f32[4,8,128]{2,1,0:T(8,128)} %get-tuple-element.86) | copy-start | bytes 49156
  244.8 5.0 %copy-start.4 = (f32[2,8,1024]{2,1,0:T(8,128)S(1)}, f32[2,8,1024]{2,1,0:T(8,128)}, u32[]{:S(2)}) copy-start(f32[2,8,1024]{2,1,0:T(8,128)} %get-tuple-element.85) | copy-start | bytes 196612
  249.1 28.6 %copy-start.6 = (f32[2,1024]{1,0:T(2,128)S(1)}, f32[2,1024]{1,0:T(2,128)}, u32[]{:S(2)}) copy-start(f32[2,1024]{1,0:T(2,128)} %param.18) | copy-start | bytes 24580
  276.8 4.4 %copy-start.5 = (f32[4,16,128]{2,1,0:T(8,128)S(1)}, f32[4,16,128]{2,1,0:T(8,128)}, u32[]{:S(2)}) copy-start(f32[4,16,128]{2,1,0:T(8,128)} %get-tuple-element.100) | copy-start | bytes 98308
